TPU v7x, 128 devices: a whole 4x4x4 slice. The times are simulated.
128 devices in a mesh: gx: 16 (over x_lo, z, core), gy: 8 (over x_hi, y).
Axes of the slice: x: 4 (x_hi: 2, x_lo: 2; x = x_hi * 2 + x_lo), y: 4, z: 4, core: 2. Of those that a mesh axis runs over, the one named last changes fastest.
Arguments:
- offset: float32 [3, 3072, 128], P(None, ('gx', 'gy')), may hold values from 0.5 to 1.5
- particle_mass: float32 [3072, 128], P(('gx', 'gy')), may hold values from 0.5 to 2
- velocity: float32 [3, 3072, 128], P(None, ('gx', 'gy')), may hold values from -6 to 6
- affine: float32 [9, 3072, 128], P(None, ('gx', 'gy')), may hold values from -3 to 3
- deform: float32 [9, 3072, 128], P(None, ('gx', 'gy')), may hold values from -0.3 to 1.3, as said below
- particle_cell: int32 [3072, 128], P(('gx', 'gy')), may hold values from 0 to 127
- body_id: int32 [3072, 128], P(('gx', 'gy')), may hold values from 0 to 63
- slot_tile_number: int32 [3072], P(('gx', 'gy')), may hold values from 0 to 127, as said below
- block_count: int32 [16, 8], P('gx', 'gy'), may hold values from 12 to 24, as said below
- normal_code: int32 [128, 64, 256], P('gx', 'gy'), may hold values from 0 to 25
Outputs:
- new_velocity: float32 [3, 3072, 128], P(None, ('gx', 'gy'))
- new_affine: float32 [9, 3072, 128], P(None, ('gx', 'gy'))
- new_deform: float32 [9, 3072, 128], P(None, ('gx', 'gy'))
- new_stress: float32 [6, 3072, 128], P(None, ('gx', 'gy'))
Inputs may be any that keep to these rules, and one draw needn't show every extreme that they name: `deform`: A 3 x 3 identity plus entries between -0.3 and 0.3. `slot_tile_number`: on every device the first four slots lie in tiles on the low x, high x, low y and high y faces of its part of the grid, in that order. `block_count`: slots below the count are live; some device has exactly 24.
All inputs are finite; a program needn't handle non-finite values.
Results may differ from a plain program's by a relative error of at most 0.000073.
Values sent between devices are 32-bit elements; how exact they have to be, the bound alone decides.
No kernel may reach another device: no remote copies, remote signals or barrier semaphores. Data moves between devices by JAX's collectives and lax.ppermute only.
A program may use at most 128 MiB of HBM per device.

v0:
```python
import jax
import jax.numpy as jnp
from jax import lax
from jax.sharding import PartitionSpec as P

DT = 0.1
MU = 2.0
LAM = 3.0
GRAVITY = -2.0
FLOOR = 0.25


def from_behind(block, axis, distance):
    devices = range(lax.axis_size(axis))
    route = [(i - distance, i) for i in devices if i - distance in devices]
    return lax.ppermute(block, axis, route)


def padded(block, sides, width):
    for axis, dim in sides:
        count = lax.axis_size(axis)
        forward = [(i, i + 1) for i in range(count - 1)]
        backward = [(target, source) for source, target in forward]
        low = lax.ppermute(
            lax.slice_in_dim(block, block.shape[dim] - width, None, axis=dim), axis, forward
        )
        high = lax.ppermute(lax.slice_in_dim(block, 0, width, axis=dim), axis, backward)
        block = jnp.concatenate([low, block, high], axis=dim)
    return block


def spline_weights(fraction):
    return [
        0.5 * (1.5 - fraction) * (1.5 - fraction),
        0.75 - (fraction - 1.0) * (fraction - 1.0),
        0.5 * (fraction - 0.5) * (fraction - 0.5),
    ]


def determinant(matrix):
    return (
        matrix[0] * (matrix[4] * matrix[8] - matrix[5] * matrix[7])
        - matrix[1] * (matrix[3] * matrix[8] - matrix[5] * matrix[6])
        + matrix[2] * (matrix[3] * matrix[7] - matrix[4] * matrix[6])
    )


def kirchhoff(matrix):
    volume_ratio = determinant(matrix)
    pressure = 0.5 * LAM * (volume_ratio * volume_ratio - 1.0)
    entries = []
    for row_index in range(3):
        for column_position in range(3):
            element = (
                matrix[3 * row_index] * matrix[3 * column_position]
                + matrix[3 * row_index + 1] * matrix[3 * column_position + 1]
                + matrix[3 * row_index + 2] * matrix[3 * column_position + 2]
            )
            if row_index == column_position:
                element = MU * (element - 1.0) + pressure
            else:
                element = MU * element
            entries.append(element)
    return jnp.stack(entries)


def advance_deform(affine_new, deform):
    entries = []
    for row_index in range(3):
        for column_position in range(3):
            element = deform[3 * row_index + column_position]
            for inner_index in range(3):
                element = (
                    element
                    + DT
                    * affine_new[3 * row_index + inner_index]
                    * deform[3 * inner_index + column_position]
                )
            entries.append(element)
    return jnp.stack(entries)


def unit_normals(direction):
    shifted = direction + (direction >= 13).astype(jnp.int32)
    components = [shifted // 9 - 1, shifted // 3 % 3 - 1, shifted % 3 - 1]
    components = [part_value.astype(jnp.float32) for part_value in components]
    length = jnp.sqrt(
        components[0] * components[0]
        + components[1] * components[1]
        + components[2] * components[2]
    )
    return jnp.stack([part_value / length for part_value in components])


def node_update(node_grid, normal):
    first_body_mass = node_grid[0]
    momentum_zero = node_grid[1:4]
    mass_one = node_grid[4]
    momentum_one = node_grid[5:8]
    gravity_step = jnp.array([0.0, 0.0, DT * GRAVITY], dtype=node_grid.dtype).reshape(
        (3,) + (1,) * (node_grid.ndim - 1)
    )
    speed_zero = momentum_zero / jnp.maximum(first_body_mass, FLOOR) + gravity_step
    speed_one = momentum_one / jnp.maximum(mass_one, FLOOR) + gravity_step
    center_speed = (momentum_zero + momentum_one) / jnp.maximum(
        first_body_mass + mass_one, FLOOR
    ) + gravity_step
    contact_share = jnp.minimum(1.0, jnp.minimum(first_body_mass, mass_one) / FLOOR)
    approach_zero = jnp.maximum(jnp.sum((speed_zero - center_speed) * normal, 0), 0.0)
    approach_one = jnp.maximum(jnp.sum((center_speed - speed_one) * normal, 0), 0.0)
    speed_zero = speed_zero - (contact_share * approach_zero)[None] * normal
    speed_one = speed_one + (contact_share * approach_one)[None] * normal
    return jnp.concatenate([speed_zero, speed_one], 0)


def patch_axis(fraction, cell_coord, node_coord):
    weights = spline_weights(fraction)
    weight_sum = jnp.zeros(fraction.shape + node_coord.shape, jnp.float32)
    moment_sum = jnp.zeros(fraction.shape + node_coord.shape, jnp.float32)
    for stencil in range(3):
        onehot = (cell_coord[..., None] + stencil == node_coord).astype(jnp.float32)
        weight_sum = weight_sum + weights[stencil][..., None] * onehot
        moment_sum = moment_sum + (weights[stencil] * (stencil - fraction))[..., None] * onehot
    return (weight_sum, moment_sum)


def build_weights(fraction, cell_index, column_x, column_y, column_z):
    weight_x, moment_x = patch_axis(fraction[0], cell_index // 32, column_x)
    weight_y, moment_y = patch_axis(fraction[1], cell_index // 8 % 4, column_y)
    weight_z, moment_z = patch_axis(fraction[2], cell_index % 8, column_z)
    shared_yz = weight_y * weight_z
    return jnp.stack(
        [
            weight_x * shared_yz,
            moment_x * shared_yz,
            weight_x * moment_y * weight_z,
            weight_x * weight_y * moment_z,
        ],
        1,
    )


def per_device(
    offset,
    particle_mass,
    velocity,
    affine,
    deform,
    particle_cell,
    body_id,
    slot_tile_number,
    block_count,
    normal_code,
):
    blocks, particles = particle_mass.shape
    side_x, vertical_extent, depth_z = normal_code.shape
    vertical_tiles = vertical_extent // 4
    tiles_z = depth_z // 8
    group_size = 8
    groups = blocks // group_size
    live_count = block_count[0, 0]
    live_mask = (jnp.arange(blocks, dtype=jnp.int32) < live_count).astype(jnp.float32)[:, None]
    field_zero = (body_id % 2 == 0).astype(jnp.float32)
    field_one = 1.0 - field_zero
    weighted = particle_mass * live_mask
    stress_old = kirchhoff(deform)
    affine_force = weighted[None] * (affine - 4.0 * DT * stress_old)
    zero_rows = jnp.zeros_like(weighted)
    channel_sets = [
        [weighted * field_zero]
        + [weighted * velocity[row_index] * field_zero for row_index in range(3)]
        + [weighted * field_one]
        + [weighted * velocity[row_index] * field_one for row_index in range(3)]
    ]
    for column_position in range(3):
        channel_sets.append(
            [zero_rows]
            + [affine_force[3 * row_index + column_position] * field_zero for row_index in range(3)]
            + [zero_rows]
            + [affine_force[3 * row_index + column_position] * field_one for row_index in range(3)]
        )
    sources = jnp.stack([jnp.stack(channels) for channels in channel_sets])
    column = jnp.arange(384, dtype=jnp.int32)
    column_x = column // 60
    column_y = column // 10 % 6
    column_z = column % 10

    def scatter_work(members):
        fraction, cell_index, source = members
        kernel = build_weights(fraction, cell_index, column_x, column_y, column_z)
        return jnp.einsum("lcgp,glpq->cgq", source, kernel, precision=lax.Precision.HIGHEST)

    def scatter_step(group_index, patches):
        start = group_index * group_size
        fraction = lax.dynamic_slice_in_dim(offset, start, group_size, 1)
        cell_index = lax.dynamic_slice_in_dim(particle_cell, start, group_size, 0)
        source = lax.dynamic_slice_in_dim(sources, start, group_size, 2)
        result = scatter_work((fraction, cell_index, source))
        return lax.dynamic_update_slice_in_dim(patches, result, start, 1)

    patches = lax.fori_loop(0, groups, scatter_step, jnp.zeros((8, blocks, 384), jnp.float32))
    tile_x = slot_tile_number // (vertical_tiles * tiles_z)
    tile_y = slot_tile_number // tiles_z % vertical_tiles
    tile_z = slot_tile_number % tiles_z
    grid_cells = (side_x + 2) * (vertical_extent + 2) * (depth_z + 2)
    node_x = tile_x[:, None] * 4 + column_x[None, :]
    node_y = tile_y[:, None] * 4 + column_y[None, :]
    node_z = tile_z[:, None] * 8 + column_z[None, :]
    flat_index = (node_x * (vertical_extent + 2) + node_y) * (depth_z + 2) + node_z
    flat_index = jnp.where(column[None, :] < 360, flat_index, grid_cells)
    node_grid = jnp.zeros((8, grid_cells + 1), jnp.float32)
    node_grid = node_grid.at[:, flat_index].add(patches)
    node_grid = node_grid[:, :grid_cells].reshape(8, side_x + 2, vertical_extent + 2, depth_z + 2)
    depth_index = jnp.arange(depth_z + 2, dtype=jnp.int32)
    inside_z = ((depth_index >= 1) & (depth_index <= depth_z)).astype(jnp.float32)
    from_right = from_behind(node_grid[:, 0:1], "gx", -1)
    from_left = from_behind(node_grid[:, side_x + 1 : side_x + 2], "gx", 1)
    inner_rows = node_grid[:, 1 : side_x + 1]
    inner_rows = inner_rows.at[:, side_x - 1 : side_x].add(from_right).at[:, 0:1].add(from_left)
    from_above = from_behind(inner_rows[:, :, 0:1], "gy", -1)
    from_below = from_behind(inner_rows[:, :, vertical_extent + 1 : vertical_extent + 2], "gy", 1)
    inner_rows = (
        inner_rows.at[:, :, vertical_extent : vertical_extent + 1]
        .add(from_above)
        .at[:, :, 1:2]
        .add(from_below)
    )
    owned_nodes = inner_rows[:, :, 1 : vertical_extent + 1]
    normal = jnp.pad(unit_normals(normal_code), ((0, 0), (0, 0), (0, 0), (1, 1)))
    speeds = node_update(owned_nodes, normal) * inside_z
    speeds = padded(speeds, (("gx", 1), ("gy", 2)), 1)
    flat_speeds = jnp.concatenate([speeds.reshape(6, -1), jnp.zeros((6, 1), jnp.float32)], 1)
    block_speeds = flat_speeds[:, flat_index]

    def gather_work(members):
        fraction, cell_index, speed_rows = members
        kernel = build_weights(fraction, cell_index, column_x, column_y, column_z)
        return jnp.einsum("glpq,cgq->lcgp", kernel, speed_rows, precision=lax.Precision.HIGHEST)

    def gather_step(group_index, gathered):
        start = group_index * group_size
        fraction = lax.dynamic_slice_in_dim(offset, start, group_size, 1)
        cell_index = lax.dynamic_slice_in_dim(particle_cell, start, group_size, 0)
        speed_rows = lax.dynamic_slice_in_dim(block_speeds, start, group_size, 1)
        result = gather_work((fraction, cell_index, speed_rows))
        return lax.dynamic_update_slice_in_dim(gathered, result, start, 2)

    gathered = lax.fori_loop(
        0, groups, gather_step, jnp.zeros((4, 6, blocks, particles), jnp.float32)
    )
    chosen = gathered[:, 0:3] * field_zero + gathered[:, 3:6] * field_one
    new_velocity = chosen[0] * live_mask
    new_affine = (
        4.0
        * jnp.stack(
            [
                chosen[1 + column_position][row_index]
                for row_index in range(3)
                for column_position in range(3)
            ]
        )
        * live_mask
    )
    new_deform = advance_deform(new_affine, deform) * live_mask
    stress_new = kirchhoff(new_deform)
    new_stress = (
        jnp.stack(
            [
                stress_new[0],
                stress_new[4],
                stress_new[8],
                stress_new[1],
                stress_new[2],
                stress_new[5],
            ]
        )
        * live_mask
    )
    return (new_velocity, new_affine, new_deform, new_stress)


def solution(mesh):
    placed = (
        P(None, ("gx", "gy"), None),
        P(("gx", "gy"), None),
        P(None, ("gx", "gy"), None),
        P(None, ("gx", "gy"), None),
        P(None, ("gx", "gy"), None),
        P(("gx", "gy"), None),
        P(("gx", "gy"), None),
        P(("gx", "gy")),
        P("gx", "gy"),
        P("gx", "gy", None),
    )
    return jax.shard_map(
        per_device,
        mesh=mesh,
        in_specs=placed,
        out_specs=(
            P(None, ("gx", "gy"), None),
            P(None, ("gx", "gy"), None),
            P(None, ("gx", "gy"), None),
            P(None, ("gx", "gy"), None),
        ),
        check_vma=False,
    )
```

profile of v0, /device:TPU:101, one launch (start us, length us, event | category | flops | bytes accessed | tf_op | source)
XLA Modules:
  0.0 297.9 jit_solution(4940650232002878872)
XLA Ops:
  0.7 0.9 constant_dynamic-update-slice_fusion.16
  1.6 0.8 constant_dynamic-update-slice_fusion.15
  2.4 0.8 constant_dynamic-update-slice_fusion.14
  4.0 0.8 constant_dynamic-update-slice_fusion.11
  4.8 1.3 fusion.140
  6.8 0.8 constant_dynamic-update-slice_fusion.7
  9.8 0.9 subtract_multiply_fusion
  13.0 42.8 %while.40 = (s32[]{:T(128)}, f32[8,24,384]{2,0,1:T(8,128)S(1)}, s32[24,128]{1,0:T(8,128)S(1)}, f32[3,24,128]{2,1,0:T(8,128)S(1)}, f32[4,8,24,128]{3,2,1,0:T(8,12...) while((s32[]{:T(128)}, f32[8,24,384]{2,0,1:T(8,128)S(1)}, ...), condition=%wide.region_1.2_spmd.clone.clone, body=%wide.region_0.1_spmd.clone.clone.sunk | while | flops 196723456 | bytes 13550299 | solution.py:201
  13.2 2.7 fusion.162
  15.9 2.7 fusion.163
  18.5 2.7 fusion.164
  21.2 2.7 fusion.161
  23.9 3.4 %fusion.165 = f32[8,24,384]{2,0,1:T(8,128)S(1)} fusion(f32[8,24,384]{2,0,1:T(8,128)S(1)} %get-tuple-element.1021, s32[]{:T(128)S(6)} %select_n.500, f32[8,1,128,384]{3,2,1,0:T(8,128)S(1)} %fusion.161, f32[8,1,128,384]{3,2,1,0:T(8,128)S(1)} %fusion.162, f32[8,1,128,384]{3,2,1,0:T(8,128)S(1)} %fusion.163, f32[8,1,128,384]{3,2,1,0:T(8,128)S(1)} %fusion.164, ...), kind=kOutput, calls=%fused_computation.54.clone.1 | convolution fusion | flops 155713536 | bytes 6520836 | tf_op jit(solution)/shard_map/while/body/eval_jaxpr/lcgp,glpq->cgq/dot_general | solution.py:191
  27.5 2.7 fusion.162
  30.1 2.7 fusion.163
  32.8 2.7 fusion.164
  35.5 2.7 fusion.161
  38.2 3.4 %fusion.165 = f32[8,24,384]{2,0,1:T(8,128)S(1)} fusion(f32[8,24,384]{2,0,1:T(8,128)S(1)} %get-tuple-element.1021, s32[]{:T(128)S(6)} %select_n.500, f32[8,1,128,384]{3,2,1,0:T(8,128)S(1)} %fusion.161, f32[8,1,128,384]{3,2,1,0:T(8,128)S(1)} %fusion.162, f32[8,1,128,384]{3,2,1,0:T(8,128)S(1)} %fusion.163, f32[8,1,128,384]{3,2,1,0:T(8,128)S(1)} %fusion.164, ...), kind=kOutput, calls=%fused_computation.54.clone.1 | convolution fusion | flops 155713536 | bytes 6520836 | tf_op jit(solution)/shard_map/while/body/eval_jaxpr/lcgp,glpq->cgq/dot_general | solution.py:191
  41.7 2.7 fusion.162
  44.4 2.7 fusion.163
  47.1 2.7 fusion.164
  49.8 2.7 fusion.161
  52.5 3.4 %fusion.165 = f32[8,24,384]{2,0,1:T(8,128)S(1)} fusion(f32[8,24,384]{2,0,1:T(8,128)S(1)} %get-tuple-element.1021, s32[]{:T(128)S(6)} %select_n.500, f32[8,1,128,384]{3,2,1,0:T(8,128)S(1)} %fusion.161, f32[8,1,128,384]{3,2,1,0:T(8,128)S(1)} %fusion.162, f32[8,1,128,384]{3,2,1,0:T(8,128)S(1)} %fusion.163, f32[8,1,128,384]{3,2,1,0:T(8,128)S(1)} %fusion.164, ...), kind=kOutput, calls=%fused_computation.54.clone.1 | convolution fusion | flops 155713536 | bytes 6520836 | tf_op jit(solution)/shard_map/while/body/eval_jaxpr/lcgp,glpq->cgq/dot_general | solution.py:191
  55.9 2.8 copy.25
  58.8 55.9 %scatter_custom_fusion = f32[8,25801]{0,1:T(8,128)} fusion(s32[9216]{0:T(1024)S(1)} %reshape.1325, f32[9216,8]{1,0:T(8,128)} %copy.25, f32[]{:T(128)} %constant.860.clone.1), kind=kCustom, calls=%fused_computation.225 | custom fusion | flops 73728 | bytes 826144 | tf_op jit(solution)/shard_map/scatter-add | solution.py:212
  114.8 9.6 %slice.697 = f32[8,25800]{0,1:T(8,128)} slice(f32[8,25801]{0,1:T(8,128)} %scatter_custom_fusion), slice={[0:8], [0:25800]} | slice | bytes 1651200 | tf_op jit(solution)/shard_map/slice | solution.py:213
  124.3 8.1 %copy.26 = f32[8,25800]{1,0:T(8,128)S(1)} copy(f32[8,25800]{0,1:T(8,128)} %slice.697) | data formatting | bytes 1651200 | tf_op jit(solution)/shard_map/slice | solution.py:213
  132.4 1.0 reshape.1313
  133.5 2.6 collective-permute-start
  136.1 5.1 %collective-permute-start.1 = (f32[8,1,10,258]{3,2,1,0:T(8,128)S(1)}, f32[8,1,10,258]{3,2,1,0:T(8,128)S(1)}, u32[]{:S(2)}, u32[]{:S(2)}) collective-permute-start(f32[8,1,10,258]{3,2,1,0:T(8,128)S(1)} %get-tuple-element.788), channel_id=1, source_target_pairs={{0,8},{8,16},{16,24},{24,32},{32,40},{40,48},{48,56},{56,64},{64,7... | collective-permute-start | bytes 247688 | tf_op jit(solution)/shard_map/ppermute | solution.py:16
  141.8 0.8 divide_bitcast_fusion.2
  142.7 0.8 divide_bitcast_fusion.1
  144.0 4.6 %collective-permute-start.2 = (f32[8,8,1,258]{3,2,1,0:T(1,128)S(1)}, f32[8,8,1,258]{3,2,1,0:T(1,128)S(1)}, u32[]{:S(2)}, u32[]{:S(2)}) collective-permute-start(f32[8,8,1,258]{3,2,1,0:T(1,128)S(1)} %get-tuple-element.798), channel_id=1, source_target_pairs={{1,0},{2,1},{3,2},{4,3},{5,4},{6,5},{7,6},{9,8},{10,9},{11,10},{12... | collective-permute-start | bytes 198152 | tf_op jit(solution)/shard_map/ppermute | solution.py:16
  148.6 1.9 collective-permute-start.3
  151.1 3.5 %scatter-add.30 = f32[8,8,10,258]{3,2,1,0:T(8,128)S(1)} dynamic-update-slice(f32[8,8,10,258]{3,2,1,0:T(8,128)S(1)} %fusion.106, f32[8,8,1,258]{3,2,1,0:T(1,128)S(1)} %slice_add_fusion.3, s32[]{:T(128)} %constant.859.clone.1, s32[]{:T(128)} %constant.859.clone.1, s32[]{:T(128)} %constant.874.clone.1, s32[]{:T(128)} %constant.859.clone.1) | dynamic-update-slice | bytes 132100 | tf_op jit(solution)/shard_map/scatter-add | solution.py:224
  154.6 4.2 %collective-permute-done.3 = f32[8,8,1,258]{3,2,1,0:T(1,128)S(1)} collective-permute-done((f32[8,8,1,258]{3,2,1,0:T(1,128)S(1)}, f32[8,8,1,258]{3,2,1,0:T(1,128)S(1)}, u32[]{:S(2)}, u32[]{:S(2)}) %collective-permute-start.3) | collective-permute-done | bytes 66080 | tf_op jit(solution)/shard_map/ppermute | solution.py:16
  159.0 3.5 %scatter-add.31 = f32[8,8,10,258]{3,2,1,0:T(8,128)S(1)} dynamic-update-slice(f32[8,8,10,258]{3,2,1,0:T(8,128)S(1)} %scatter-add.30, f32[8,8,1,258]{3,2,1,0:T(1,128)S(1)} %slice_add_fusion.2, s32[]{:T(128)} %constant.859.clone.1, s32[]{:T(128)} %constant.859.clone.1, s32[]{:T(128)} %constant.862.clone.1, s32[]{:T(128)} %constant.859.clone.1) | dynamic-update-slice | bytes 132100 | tf_op jit(solution)/shard_map/scatter-add | solution.py:226
  162.6 1.2 multiply_reduce_fusion.1
  164.1 7.2 %collective-permute-start.4 = (f32[6,1,8,258]{3,2,1,0:T(8,128)S(1)}, f32[6,1,8,258]{3,2,1,0:T(8,128)S(1)}, u32[]{:S(2)}, u32[]{:S(2)}) collective-permute-start(f32[6,1,8,258]{3,2,1,0:T(8,128)S(1)} %get-tuple-element.801), channel_id=1, source_target_pairs={{0,8},{8,16},{16,24},{24,32},{32,40},{40,48},{48,56},{56,64},{64,7... | collective-permute-start | bytes 148616 | tf_op jit(solution)/shard_map/ppermute | solution.py:24
  171.3 1.9 collective-permute-start.5
  173.3 5.8 %collective-permute-done.5 = f32[6,1,8,258]{3,2,1,0:T(8,128)S(1)} collective-permute-done((f32[6,1,8,258]{3,2,1,0:T(8,128)S(1)}, f32[6,1,8,258]{3,2,1,0:T(8,128)S(1)}, u32[]{:S(2)}, u32[]{:S(2)}) %collective-permute-start.5) | collective-permute-done | bytes 49568 | tf_op jit(solution)/shard_map/ppermute | solution.py:27
  179.2 1.9 collective-permute-start.6
  181.2 7.0 %collective-permute-start.7 = (f32[6,10,1,258]{3,2,1,0:T(1,128)S(1)}, f32[6,10,1,258]{3,2,1,0:T(1,128)S(1)}, u32[]{:S(2)}, u32[]{:S(2)}) collective-permute-start(f32[6,10,1,258]{3,2,1,0:T(1,128)S(1)} %get-tuple-element.800), channel_id=1, source_target_pairs={{1,0},{2,1},{3,2},{4,3},{5,4},{6,5},{7,6},{9,8},{10,9},{11,10},{12... | collective-permute-start | bytes 185768 | tf_op jit(solution)/shard_map/ppermute | solution.py:27
  188.2 1.5 collective-permute-done.7
  190.6 7.8 %copy.27 = f32[6,25800]{0,1:T(8,128)} copy(f32[6,25800]{1,0:T(8,128)S(1)} %reshape.1314) | data formatting | bytes 1238400 | tf_op jit(solution)/shard_map/reshape | solution.py:232
  198.4 9.7 %concatenate.23 = f32[6,25801]{0,1:T(8,128)} pad(f32[6,25800]{0,1:T(8,128)} %copy.27, f32[]{:T(128)} %constant.860.clone.1), padding=0_0x0_1 | pad | bytes 1238428 | tf_op jit(solution)/shard_map/concatenate | solution.py:232
  208.1 35.9 %gather_fusion = f32[9216,6]{1,0:T(8,128)} fusion(f32[6,25801]{0,1:T(8,128)} %concatenate.23, s32[9216]{0:T(1024)S(1)} %copy-done.10), kind=kCustom, calls=%fused_computation | custom fusion | bytes 479232 | tf_op jit(solution)/shard_map/gather | solution.py:233
  244.1 3.1 %copy.28 = f32[24,384,6]{1,2,0:T(8,128)S(1)} copy(f32[24,384,6]{2,1,0:T(8,128)} %bitcast.342) | data formatting | bytes 442368 | tf_op jit(solution)/shard_map/gather | solution.py:233
  247.2 48.7 %while.41 = (s32[]{:T(128)}, f32[4,6,24,128]{3,2,1,0:T(8,128)S(1)}, f32[6,24,384]{2,0,1:T(8,128)S(1)}, s32[24,128]{1,0:T(8,128)S(1)}, f32[3,24,128]{2,1,0:T(8,12...) while((s32[]{:T(128)}, f32[4,6,24,128]{3,2,1,0:T(8,128)S(1)}, ...), condition=%wide.region_6.7_spmd.clone.clone, body=%wide.region_5.6_spmd.clone.clone.sunk | while | flops 158974720 | bytes 13484763 | solution.py:248
  247.4 2.7 fusion.169
  250.1 2.7 fusion.170
  252.7 2.7 fusion.171
  255.4 2.7 fusion.168
  258.1 5.3 %fusion.172 = f32[4,6,8,128]{3,1,0,2:T(8,128)S(1)} fusion(f32[8,1,128,384]{3,2,1,0:T(8,128)S(1)} %fusion.168, f32[8,1,128,384]{3,2,1,0:T(8,128)S(1)} %fusion.169, f32[8,1,128,384]{3,2,1,0:T(8,128)S(1)} %fusion.170, f32[8,1,128,384]{3,2,1,0:T(8,128)S(1)} %fusion.171, f32[6,24,384]{2,0,1:T(8,128)S(1)} %get-tuple-element.1066, s32[]{:T(128)S(6)} %select_n.503), kind=kOutput, calls=%fused_computation.161.clone.1 | convolution fusion | flops 117964800 | bytes 6488068 | tf_op jit(solution)/shard_map/while/body/eval_jaxpr/glpq,cgq->lcgp/dot_general | solution.py:238
  263.6 2.7 fusion.169
  266.3 2.7 fusion.170
  269.0 2.7 fusion.171
  271.7 2.7 fusion.168
  274.3 5.3 %fusion.172 = f32[4,6,8,128]{3,1,0,2:T(8,128)S(1)} fusion(f32[8,1,128,384]{3,2,1,0:T(8,128)S(1)} %fusion.168, f32[8,1,128,384]{3,2,1,0:T(8,128)S(1)} %fusion.169, f32[8,1,128,384]{3,2,1,0:T(8,128)S(1)} %fusion.170, f32[8,1,128,384]{3,2,1,0:T(8,128)S(1)} %fusion.171, f32[6,24,384]{2,0,1:T(8,128)S(1)} %get-tuple-element.1066, s32[]{:T(128)S(6)} %select_n.503), kind=kOutput, calls=%fused_computation.161.clone.1 | convolution fusion | flops 117964800 | bytes 6488068 | tf_op jit(solution)/shard_map/while/body/eval_jaxpr/glpq,cgq->lcgp/dot_general | solution.py:238
  279.9 2.7 fusion.169
  282.6 2.7 fusion.170
  285.2 2.7 fusion.171
  287.9 2.7 fusion.168
  290.6 5.3 %fusion.172 = f32[4,6,8,128]{3,1,0,2:T(8,128)S(1)} fusion(f32[8,1,128,384]{3,2,1,0:T(8,128)S(1)} %fusion.168, f32[8,1,128,384]{3,2,1,0:T(8,128)S(1)} %fusion.169, f32[8,1,128,384]{3,2,1,0:T(8,128)S(1)} %fusion.170, f32[8,1,128,384]{3,2,1,0:T(8,128)S(1)} %fusion.171, f32[6,24,384]{2,0,1:T(8,128)S(1)} %get-tuple-element.1066, s32[]{:T(128)S(6)} %select_n.503), kind=kOutput, calls=%fused_computation.161.clone.1 | convolution fusion | flops 117964800 | bytes 6488068 | tf_op jit(solution)/shard_map/while/body/eval_jaxpr/glpq,cgq->lcgp/dot_general | solution.py:238
  (167 shorter events, 11.4 us)
Async XLA Ops:
  0.6 12.4 %copy-start.3 = (f32[3,24,128]{2,1,0:T(8,128)S(1)}, f32[3,24,128]{2,1,0:T(8,128)}, u32[]{:S(2)}) copy-start(f32[3,24,128]{2,1,0:T(8,128)} %param.23) | copy-start | bytes 110596
  0.6 12.4 %copy-start.8 = (s32[24,128]{1,0:T(8,128)S(1)}, s32[24,128]{1,0:T(8,128)}, u32[]{:S(2)}) copy-start(s32[24,128]{1,0:T(8,128)} %param.28) | copy-start | bytes 36868
  6.7 3.0 %copy-start.12 = (f32[24]{0:T(128)}, f32[24]{0:T(128)S(1)}, u32[]{:S(2)}) copy-start(f32[24]{0:T(128)S(1)} %compare_convert_fusion) | copy-start | bytes 292
  55.8 2.9 copy-start.15
  132.4 9.4 %copy-start.9 = (s32[8,8,256]{2,1,0:T(8,128)S(1)}, s32[8,8,256]{2,1,0:T(8,128)}, u32[]{:S(2)}) copy-start(s32[8,8,256]{2,1,0:T(8,128)} %param.32) | copy-start | bytes 196612
  133.5 10.0 %collective-permute-start = (f32[8,1,10,258]{3,2,1,0:T(8,128)S(1)}, f32[8,1,10,258]{3,2,1,0:T(8,128)S(1)}, u32[]{:S(2)}, u32[]{:S(2)}) collective-permute-start(f32[8,1,10,258]{3,2,1,0:T(8,128)S(1)} %get-tuple-element.789), channel_id=1, source_target_pairs={{8,0},{16,8},{24,16},{32,24},{40,32},{48,40},{56,48},{64,56},{72,6... | collective-permute-start | bytes 247688 | tf_op jit(solution)/shard_map/ppermute | solution.py:16
  136.1 7.7 %collective-permute-start.1 = (f32[8,1,10,258]{3,2,1,0:T(8,128)S(1)}, f32[8,1,10,258]{3,2,1,0:T(8,128)S(1)}, u32[]{:S(2)}, u32[]{:S(2)}) collective-permute-start(f32[8,1,10,258]{3,2,1,0:T(8,128)S(1)} %get-tuple-element.788), channel_id=1, source_target_pairs={{0,8},{8,16},{16,24},{24,32},{32,40},{40,48},{48,56},{56,64},{64,7... | collective-permute-start | bytes 247688 | tf_op jit(solution)/shard_map/ppermute | solution.py:16
  144.0 7.0 %collective-permute-start.2 = (f32[8,8,1,258]{3,2,1,0:T(1,128)S(1)}, f32[8,8,1,258]{3,2,1,0:T(1,128)S(1)}, u32[]{:S(2)}, u32[]{:S(2)}) collective-permute-start(f32[8,8,1,258]{3,2,1,0:T(1,128)S(1)} %get-tuple-element.798), channel_id=1, source_target_pairs={{1,0},{2,1},{3,2},{4,3},{5,4},{6,5},{7,6},{9,8},{10,9},{11,10},{12... | collective-permute-start | bytes 198152 | tf_op jit(solution)/shard_map/ppermute | solution.py:16
  148.6 10.3 %collective-permute-start.3 = (f32[8,8,1,258]{3,2,1,0:T(1,128)S(1)}, f32[8,8,1,258]{3,2,1,0:T(1,128)S(1)}, u32[]{:S(2)}, u32[]{:S(2)}) collective-permute-start(f32[8,8,1,258]{3,2,1,0:T(1,128)S(1)} %get-tuple-element.797), channel_id=1, source_target_pairs={{0,1},{1,2},{2,3},{3,4},{4,5},{5,6},{6,7},{8,9},{9,10},{10,11},{11... | collective-permute-start | bytes 198152 | tf_op jit(solution)/shard_map/ppermute | solution.py:16
  151.0 12.7 %copy-start.5 = (f32[1,8,8,256]{3,2,1,0:T(8,128)S(1)}, f32[1,8,8,256]{3,2,1,0:T(8,128)}, u32[]{:S(2)}) copy-start(f32[1,8,8,256]{3,2,1,0:T(8,128)} %get-tuple-element.730) | copy-start | bytes 196612
  151.1 12.7 %copy-start.6 = (f32[1,8,8,256]{3,2,1,0:T(8,128)S(1)}, f32[1,8,8,256]{3,2,1,0:T(8,128)}, u32[]{:S(2)}) copy-start(f32[1,8,8,256]{3,2,1,0:T(8,128)} %get-tuple-element.803) | copy-start | bytes 196612
  151.1 12.7 %copy-start.7 = (f32[1,8,8,256]{3,2,1,0:T(8,128)S(1)}, f32[1,8,8,256]{3,2,1,0:T(8,128)}, u32[]{:S(2)}) copy-start(f32[1,8,8,256]{3,2,1,0:T(8,128)} %get-tuple-element.804) | copy-start | bytes 196612
  151.1 12.7 %copy-start.14 = (f32[3]{0:T(128)S(1)}, f32[3]{0:T(128)}, u32[]{:S(2)}) copy-start(f32[3]{0:T(128)} %constant.890.clone) | copy-start | bytes 40
  164.1 9.2 %collective-permute-start.4 = (f32[6,1,8,258]{3,2,1,0:T(8,128)S(1)}, f32[6,1,8,258]{3,2,1,0:T(8,128)S(1)}, u32[]{:S(2)}, u32[]{:S(2)}) collective-permute-start(f32[6,1,8,258]{3,2,1,0:T(8,128)S(1)} %get-tuple-element.801), channel_id=1, source_target_pairs={{0,8},{8,16},{16,24},{24,32},{32,40},{40,48},{48,56},{56,64},{64,7... | collective-permute-start | bytes 148616 | tf_op jit(solution)/shard_map/ppermute | solution.py:24
  171.3 7.8 %collective-permute-start.5 = (f32[6,1,8,258]{3,2,1,0:T(8,128)S(1)}, f32[6,1,8,258]{3,2,1,0:T(8,128)S(1)}, u32[]{:S(2)}, u32[]{:S(2)}) collective-permute-start(f32[6,1,8,258]{3,2,1,0:T(8,128)S(1)} %get-tuple-element.802), channel_id=1, source_target_pairs={{8,0},{16,8},{24,16},{32,24},{40,32},{48,40},{56,48},{64,56},{72,6... | collective-permute-start | bytes 148616 | tf_op jit(solution)/shard_map/ppermute | solution.py:27
  179.2 8.9 %collective-permute-start.6 = (f32[6,10,1,258]{3,2,1,0:T(1,128)S(1)}, f32[6,10,1,258]{3,2,1,0:T(1,128)S(1)}, u32[]{:S(2)}, u32[]{:S(2)}) collective-permute-start(f32[6,10,1,258]{3,2,1,0:T(1,128)S(1)} %get-tuple-element.799), channel_id=1, source_target_pairs={{0,1},{1,2},{2,3},{3,4},{4,5},{5,6},{6,7},{8,9},{9,10},{10,11},{11... | collective-permute-start | bytes 185768 | tf_op jit(solution)/shard_map/ppermute | solution.py:24
  181.2 8.5 %collective-permute-start.7 = (f32[6,10,1,258]{3,2,1,0:T(1,128)S(1)}, f32[6,10,1,258]{3,2,1,0:T(1,128)S(1)}, u32[]{:S(2)}, u32[]{:S(2)}) collective-permute-start(f32[6,10,1,258]{3,2,1,0:T(1,128)S(1)} %get-tuple-element.800), channel_id=1, source_target_pairs={{1,0},{2,1},{3,2},{4,3},{5,4},{6,5},{7,6},{9,8},{10,9},{11,10},{12... | collective-permute-start | bytes 185768 | tf_op jit(solution)/shard_map/ppermute | solution.py:27
  198.4 9.7 %copy-start.10 = (s32[9216]{0:T(1024)S(1)}, s32[9216]{0:T(1024)}, u32[]{:S(2)}) copy-start(s32[9216]{0:T(1024)} %broadcast_clamp_fusion) | copy-start | bytes 110596
  244.1 3.1 %copy-start.4 = (f32[3,24,128]{2,1,0:T(8,128)S(1)}, f32[3,24,128]{2,1,0:T(8,128)}, u32[]{:S(2)}) copy-start(f32[3,24,128]{2,1,0:T(8,128)} %param.23) | copy-start | bytes 110596
  247.2 48.8 %copy-start.11 = (f32[24,128]{1,0:T(8,128)S(1)}, f32[24,128]{1,0:T(8,128)}, u32[]{:S(2)}) copy-start(f32[24,128]{1,0:T(8,128)} %get-tuple-element.728) | copy-start | bytes 36868
  247.2 48.8 %copy-start.13 = (f32[24]{0:T(128)S(1)}, f32[24]{0:T(128)}, u32[]{:S(2)}) copy-start(f32[24]{0:T(128)} %copy-done.12) | copy-start | bytes 292
  247.2 49.7 %copy-start = (f32[9,24,128]{2,1,0:T(8,128)S(1)}, f32[9,24,128]{2,1,0:T(8,128)}, u32[]{:S(2)}) copy-start(f32[9,24,128]{2,1,0:T(8,128)} %param.27) | copy-start | bytes 331780
  296.9 1.1 copy-start.2
  297.1 0.8 copy-start.1
where the time goes:
time: 303 us; the launch traced here: 298 us
  other arithmetic  138 us (46%)
  local copies, waits for them, and re-layouts  86.5 us (29%)
  starting transfers between devices  32.2 us (11%)
  matrix products  26 us (9%)
  waiting for transfers between devices  12.2 us (4%)
    scatter-add x1, other arithmetic, per_device(): node_grid = node_grid.at[:, flat_index].add(patches)  55.9 us
    gather x2, local copies, waits for them, and re-layouts, per_device(): block_speeds = flat_speeds[:, flat_index]  39 us
    slice x2, local copies, waits for them, and re-layouts, per_device(): node_grid[:, :grid_cells]  17.7 us
    mul x6, other arithmetic, build_weights(): weight_x * shared_yz  16 us
    mul x6, other arithmetic, build_weights(): moment_x * shared_yz  16 us
    mul x6, other arithmetic, build_weights(): weight_x * moment_y * weight_z  16 us
    mul x6, other arithmetic, build_weights(): weight_x * weight_y * moment_z  16 us
    dot_general x3, matrix products, gather_work(): jnp.einsum('glpq,cgq->lcgp', kernel, speed_rows, precision=lax.Precision....  15.9 us
  transfers between devices with their start and end apart: 8, of which 5 were waited for; matrix products, arithmetic and copies ran while one was open for 2% of the time, Pallas kernels for 0%

commit v1 on v0

v1 whole, which is shorter than its diff:
```python
import functools

import jax
import jax.numpy as jnp
from jax import lax
from jax.experimental import pallas as pl
from jax.experimental.pallas import tpu as pltpu
from jax.sharding import PartitionSpec as P

DT = 0.1
MU = 2.0
LAM = 3.0
GRAVITY = -2.0
FLOOR = 0.25

F32 = jnp.float32
BF16 = jnp.bfloat16
VMEM_LIMIT = 24 * 1024 * 1024

SIDE = 10
DEPTH = 256
SLOTS = 24
LANES = 128
FACE_ROWS = 176

POS_Y, POS_Z, FIELD0, FIELD1, POS_X, WX = 0, 1, 2, 3, 4, 5
MASS = WX + 6
VEL = MASS + 1
AFF = VEL + 3
SCATTER_ROWS = AFF + 9
GATHER_ROWS = WX + 6


def spline(distance):
    size = jnp.abs(distance)
    outer = jnp.maximum(1.5 - size, 0.0)
    inner = jnp.maximum(0.5 - size, 0.0)
    return 0.5 * outer * outer - 1.5 * inner * inner


def determinant(m):
    return (
        m[0] * (m[4] * m[8] - m[5] * m[7])
        - m[1] * (m[3] * m[8] - m[5] * m[6])
        + m[2] * (m[3] * m[7] - m[4] * m[6])
    )


def kirchhoff(m):
    ratio = determinant(m)
    pressure = 0.5 * LAM * (ratio * ratio - 1.0)
    entries = []
    for i in range(3):
        for j in range(3):
            e = m[3 * i] * m[3 * j] + m[3 * i + 1] * m[3 * j + 1] + m[3 * i + 2] * m[3 * j + 2]
            entries.append(MU * (e - 1.0) + pressure if i == j else MU * e)
    return entries


def split(x):
    high = x.astype(BF16)
    return high, (x - high.astype(F32)).astype(BF16)


def matmul_t(a, b):
    return lax.dot_general(a, b, (((1,), (1,)), ((), ())), preferred_element_type=F32)


def matmul(a, b):
    return lax.dot_general(a, b, (((1,), (0,)), ((), ())), preferred_element_type=F32)


def iota(shape, axis):
    return lax.broadcasted_iota(jnp.int32, shape, axis)


def common_rows(table, offset, cell, body):
    cell_x = lax.shift_right_logical(cell, 5).astype(F32)
    cell_y = (lax.shift_right_logical(cell, 3) & 3).astype(F32)
    cell_z = (cell & 7).astype(F32)
    field_one = (body & 1).astype(F32)
    pos_x = cell_x + offset[0]
    table[POS_X] = pos_x
    table[POS_Y] = cell_y + offset[1]
    table[POS_Z] = cell_z + offset[2]
    table[FIELD0] = 1.0 - field_one
    table[FIELD1] = field_one
    for x in range(6):
        table[WX + x] = spline(float(x) - pos_x)


def y_coords(tile_y):
    s = iota((8, LANES), 0)
    wrapped = jnp.where(s < 4, s + 4, s - 4)
    return jnp.where(tile_y == 0, s, wrapped).astype(F32)


def low_side(axis):
    return lax.axis_index(axis) % 2


def scatter_kernel(
    tile_ref, count_ref, offset, mass, velocity, affine, deform, cell, body, code,
    grid, planes, face_a, face_d,
    table, left_hi, left_lo, acc, turned,
):
    live = (iota((SLOTS, LANES), 0) < count_ref[0, 0]).astype(F32)
    common_rows(table, offset, cell[...], body[...])
    weighted = mass[...] * live
    table[MASS] = weighted
    for k in range(3):
        table[VEL + k] = weighted * velocity[k]
    stress = kirchhoff([deform[k] for k in range(9)])
    for k in range(9):
        table[AFF + k] = weighted * (affine[k] - 4.0 * DT * stress[k])

    acc[...] = jnp.zeros_like(acc)
    zeros = jnp.zeros((48, LANES), BF16)
    for u in range(2):
        left_hi[u, 0:48, LANES : 2 * LANES] = zeros
        left_lo[u, 0:48, LANES : 2 * LANES] = zeros

    def one(s, u):
        tile = tile_ref[s]
        tile_x = lax.shift_right_logical(tile, 6)
        tile_y = lax.shift_right_logical(tile, 5) & 1
        tile_z = tile & 31

        def row(k):
            return table[k, pl.ds(s, 1), :]

        dy = y_coords(tile_y) - row(POS_Y)
        wy = spline(dy)
        pos_x = row(POS_X)
        wxy = [wy * row(WX + x) for x in range(6)]

        def put(channel, column, values):
            for pair in range(3):
                hi, lo = split(jnp.concatenate(values[2 * pair : 2 * pair + 2], 0))
                at = channel * 48 + pair * 16
                left_hi[u, at : at + 16, column * LANES : (column + 1) * LANES] = hi
                left_lo[u, at : at + 16, column * LANES : (column + 1) * LANES] = lo

        m = row(MASS)
        put(0, 0, [w * m for w in wxy])
        for k in range(3):
            base = row(VEL + k) + row(AFF + 3 * k + 1) * dy
            ax = row(AFF + 3 * k)
            az = row(AFF + 3 * k + 2)
            put(1 + k, 0, [wxy[x] * (base + ax * (float(x) - pos_x)) for x in range(6)])
            put(1 + k, 1, [wxy[x] * az for x in range(6)])

        dz = iota((16, LANES), 0).astype(F32) - row(POS_Z)
        wz = spline(dz)
        mz = wz * dz
        parts = []
        for f in range(2):
            mask = row(FIELD0 + f)
            parts.append([split(wz * mask), split(mz * mask)])
        right_hi = jnp.concatenate(
            [jnp.concatenate([parts[f][0][0], parts[f][1][0]], 1) for f in range(2)], 0
        )
        right_lo = jnp.concatenate(
            [jnp.concatenate([parts[f][0][1], parts[f][1][1]], 1) for f in range(2)], 0
        )
        both = matmul_t(jnp.concatenate([right_hi, right_lo], 0), left_hi[u])
        rest = matmul_t(right_hi, left_lo[u])
        total = both[0:32] + both[32:64] + rest
        quadrant = tile_x * 2 + tile_y
        start = pl.multiple_of(tile_z * 8, 8)
        for f in range(2):
            acc[quadrant, f, pl.ds(start, 16), 0:192] += total[16 * f : 16 * f + 16]

    def step(pair, carry):
        one(pair * 2, 0)
        one(pair * 2 + 1, 1)
        return carry

    lax.fori_loop(0, SLOTS // 2, step, 0)

    for q in range(4):
        for f in range(2):
            for h in range(2):
                piece = acc[q, f, pl.ds(1 + LANES * h, LANES), 0:256]
                turned[q, f, :, h * LANES : (h + 1) * LANES] = piece.T[0:192]

    s8 = iota((8, DEPTH), 0)
    for f in range(2):
        for c in range(4):
            for x in range(SIDE):
                low = None
                high = None
                for tx in range(2):
                    local = x - 4 * tx
                    if not 0 <= local < 6:
                        continue
                    at = (c * 6 + local) * 8
                    v0 = turned[2 * tx, f, at : at + 8, :]
                    v1 = turned[2 * tx + 1, f, at : at + 8, :]
                    low_v = v0 + jnp.where(s8 >= 4, v1, 0.0)
                    high_v = jnp.where(s8 < 2, v1, 0.0)
                    low = low_v if low is None else low + low_v
                    high = high_v if high is None else high + high_v
                channel = 4 * f + c
                grid[channel, x, 0:8, :] = low
                grid[channel, x, 8:16, :] = high
                if x in (0, 1, 8, 9):
                    plane = x if x < 2 else x - 6
                    planes[channel, plane, 0:8, :] = low
                    planes[channel, plane, 8:16, :] = high

    side = low_side("gy")
    start_a = pl.multiple_of((1 - side) * 8, 8)
    start_d = pl.multiple_of(side * 8, 8)
    for face, start, owned in ((face_a, start_a, (1 - side) * 7), (face_d, start_d, side * 7)):
        for channel in range(8):
            for x in range(SIDE):
                at = channel * 20 + x * 2
                face[at : at + 2, :] = grid[channel, x, pl.ds(start, 2), :]
        for x in range(8):
            face[160 + x : 161 + x, :] = code[x, pl.ds(owned, 1), :].astype(F32)
        face[168:176, :] = jnp.zeros((8, DEPTH), F32)


def corner_kernel(planes, recv_a, recv_d, code, face_a, face_d, work, codes):
    side_y = low_side("gy")
    side_x = low_side("gx")
    work[...] = planes[...]
    for recv, start in ((recv_a, (1 - side_y) * 8), (recv_d, side_y * 8)):
        start = pl.multiple_of(start, 8)
        for channel in range(8):
            for plane in range(4):
                x = plane if plane < 2 else plane + 6
                at = channel * 20 + x * 2
                work[channel, plane, pl.ds(start, 2), :] += recv[at : at + 2, :]
    y_code_a = jnp.where(side_y == 0, 9, 0)
    y_code_d = jnp.where(side_y == 0, 0, 9)
    for face, first, owned in (
        (face_a, (1 - side_x) * 2, (1 - side_x) * 7),
        (face_d, side_x * 2, side_x * 7),
    ):
        for channel in range(8):
            for p in range(2):
                at = channel * 2 + p
                face[at * 8 : at * 8 + 8, :] = work[channel, first + p, 0:8, :]
                face[128 + at * 2 : 130 + at * 2, :] = work[channel, first + p, 8:10, :]
        codes[1:9, :] = code[owned].astype(F32)
        codes[pl.ds(y_code_a, 1), :] = recv_a[pl.ds(160 + owned, 1), :]
        codes[pl.ds(y_code_d, 1), :] = recv_d[pl.ds(160 + owned, 1), :]
        face[160:170, :] = codes[0:10, :]
        face[170:176, :] = jnp.zeros((6, DEPTH), F32)


def node_speeds(sums, code, inside):
    m0, m1 = sums[0], sums[4]
    r0 = 1.0 / jnp.maximum(m0, FLOOR)
    r1 = 1.0 / jnp.maximum(m1, FLOOR)
    rc = 1.0 / jnp.maximum(m0 + m1, FLOOR)
    share = jnp.minimum(1.0, jnp.minimum(m0, m1) * (1.0 / FLOOR))
    shifted = code + jnp.where(code >= 13.0, 1.0, 0.0)
    third = jnp.where(shifted >= 9.0, 1.0, 0.0) + jnp.where(shifted >= 18.0, 1.0, 0.0)
    rest = shifted - 9.0 * third
    second = jnp.where(rest >= 3.0, 1.0, 0.0) + jnp.where(rest >= 6.0, 1.0, 0.0)
    direction = [third - 1.0, second - 1.0, rest - 3.0 * second - 1.0]
    square = (
        direction[0] * direction[0] + direction[1] * direction[1] + direction[2] * direction[2]
    )
    inverse = jnp.where(square > 2.5, 1.0 / 3.0, jnp.where(square > 1.5, 0.5, 1.0))
    u0 = [sums[1 + k] * r0 for k in range(3)]
    u1 = [sums[5 + k] * r1 for k in range(3)]
    uc = [(sums[1 + k] + sums[5 + k]) * rc for k in range(3)]
    approach0 = sum((u0[k] - uc[k]) * direction[k] for k in range(3))
    approach1 = sum((uc[k] - u1[k]) * direction[k] for k in range(3))
    scale = share * inverse
    push0 = scale * jnp.maximum(approach0, 0.0)
    push1 = scale * jnp.maximum(approach1, 0.0)
    gravity = [0.0, 0.0, DT * GRAVITY]
    v0 = [(u0[k] - push0 * direction[k] + gravity[k]) * inside for k in range(3)]
    v1 = [(u1[k] + push1 * direction[k] + gravity[k]) * inside for k in range(3)]
    return v0, v1


def gather_kernel(
    last_x, last_y, tile_ref, count_ref, grid, y_a, y_d, x_a, x_d, code,
    offset, cell, body, deform,
    new_velocity, new_affine, new_deform, new_stress,
    table, work, codes, nodes_hi, nodes_lo, partial,
):
    side_y = low_side("gy")
    side_x = low_side("gx")
    common_rows(table, offset, cell[...], body[...])

    work[...] = grid[...]
    for x in range(8):
        codes[x + 1, 1:9, :] = code[x].astype(F32)
    for recv, start, halo in (
        (y_a, (1 - side_y) * 8, (1 - side_y) * 9),
        (y_d, side_y * 8, side_y * 9),
    ):
        start = pl.multiple_of(start, 8)
        for channel in range(8):
            for x in range(SIDE):
                at = channel * 20 + x * 2
                work[channel, x, pl.ds(start, 2), :] += recv[at : at + 2, :]
        for x in range(8):
            codes[x + 1, pl.ds(halo, 1), :] = recv[160 + x : 161 + x, :]
    for recv, first, halo in (
        (x_a, (1 - side_x) * 8, (1 - side_x) * 9),
        (x_d, side_x * 8, side_x * 9),
    ):
        for channel in range(8):
            for p in range(2):
                at = channel * 2 + p
                work[channel, first + p, 0:8, :] += recv[at * 8 : at * 8 + 8, :]
                work[channel, first + p, 8:10, :] += recv[128 + at * 2 : 130 + at * 2, :]
        codes[halo, 0:10, :] = recv[160:170, :]

    index_x = lax.axis_index("gx")
    index_y = lax.axis_index("gy")
    s8 = iota((8, LANES), 0)
    lane = iota((8, LANES), 1)
    inside_low = jnp.where((s8 == 0) & (index_y == 0), 0.0, 1.0)
    inside_high = jnp.where((s8 == 1) & (index_y == last_y), 0.0, 1.0)

    def tiles(v):
        a, b = v
        first = jnp.where(lane < 1, 0.0, pltpu.roll(a, 1, 1))
        second = jnp.where(lane < 9, pltpu.roll(a, 9, 1), pltpu.roll(b, 9, 1))
        third = jnp.where(lane < 17, pltpu.roll(b, 17, 1), 0.0)
        return first, second, third

    def node_step(pair, carry):
        found = []
        for k in range(2):
            x = pair * 2 + k
            edge = ((x == 0) & (index_x == 0)) | ((x == SIDE - 1) & (index_x == last_x))
            inside_x = jnp.where(edge, 0.0, 1.0)
            rows = []
            for r in range(2):
                inside = (inside_low if r == 0 else inside_high) * inside_x
                halves = []
                for h in range(2):
                    lanes = slice(h * LANES, (h + 1) * LANES)
                    sums = [work[c, x, 8 * r : 8 * r + 8, lanes] for c in range(8)]
                    halves.append(node_speeds(sums, codes[x, 8 * r : 8 * r + 8, lanes], inside))
                rows.append(halves)
            found.append(rows)
        at = pl.multiple_of(pair * 16, 16)
        for f in range(2):
            for c in range(3):
                ready = []
                for k in range(2):
                    low = tiles([found[k][0][h][f][c] for h in range(2)])
                    high = tiles([found[k][1][h][f][c] for h in range(2)])
                    ready.append((low, high))
                for j in range(3):
                    for ty in range(2):
                        pieces = []
                        for k in range(2):
                            low, high = ready[k][0][j], ready[k][1][j]
                            pieces.append(low if ty == 0 else jnp.where(s8 < 2, high, low))
                        hi, lo = split(jnp.concatenate(pieces, 0))
                        lanes = slice(f * LANES, (f + 1) * LANES)
                        nodes_hi[ty, j, c, pl.ds(at, 16), lanes] = hi
                        nodes_lo[ty, j, c, pl.ds(at, 16), lanes] = lo
        return carry

    lax.fori_loop(0, SIDE // 2, node_step, 0)

    def one(s):
        tile = tile_ref[s]
        tile_x = lax.shift_right_logical(tile, 6)
        tile_y = lax.shift_right_logical(tile, 5) & 1
        tile_z = tile & 31
        j = (tile_z >= 15).astype(jnp.int32) + (tile_z >= 30).astype(jnp.int32)
        local = tile_z - 15 * j
        odd = local & 1

        def row(k):
            return table[k, pl.ds(s, 1), :]

        pos_z = row(POS_Z) + (odd * 8).astype(F32)
        tile_row = lax.shift_right_logical(local, 1)
        windows = []
        for r in range(2):
            dz = (iota((16, LANES), 0) + 16 * r).astype(F32) - pos_z
            wz = spline(dz)
            mz = wz * dz
            for f in range(2):
                mask = row(FIELD0 + f)
                windows.append(split(wz * mask) + split(mz * mask))
        none = jnp.zeros((16, LANES), BF16)

        def spread(f, part):
            w0, w1 = windows[f][part], windows[2 + f][part]
            rows = []
            for k in range(8):
                tail = jnp.where(tile_row == k - 1, w1, none) if k else none
                rows.append(jnp.where(tile_row == k, w0, tail))
            return jnp.concatenate(rows, 0)

        def weights(part):
            columns = [
                jnp.concatenate([spread(f, p) for f in range(2)], 0) for p in (part, part + 2)
            ]
            return jnp.concatenate(columns, 1)

        first = pl.multiple_of(tile_x * 32, 32)
        hi = [nodes_hi[tile_y, j, c, pl.ds(first, 48), :] for c in range(3)]
        lo = [nodes_lo[tile_y, j, c, pl.ds(first, 48), :] for c in range(3)]
        weights_hi = weights(0)
        nodes = jnp.concatenate(hi, 0)
        summed = (
            matmul(nodes, weights_hi)
            + matmul(jnp.concatenate(lo, 0), weights_hi)
            + matmul(nodes, weights(1))
        )

        dy = y_coords(tile_y) - row(POS_Y)
        wy = spline(dy)
        pos_x = row(POS_X)
        wxy = [wy * row(WX + x) for x in range(6)]
        dx = [float(x) - pos_x for x in range(6)]
        place = pl.ds(pl.multiple_of(s * 8, 8), 8)
        for c in range(3):
            speed = jnp.zeros((8, LANES), F32)
            along_x = jnp.zeros((8, LANES), F32)
            along_z = jnp.zeros((8, LANES), F32)
            for x in range(6):
                at = (c * 6 + x) * 8
                part = wxy[x] * summed[at : at + 8, 0:LANES]
                speed = speed + part
                along_x = along_x + part * dx[x]
                along_z = along_z + wxy[x] * summed[at : at + 8, LANES : 2 * LANES]
            partial[4 * c, place, :] = speed
            partial[4 * c + 1, place, :] = along_x
            partial[4 * c + 2, place, :] = speed * dy
            partial[4 * c + 3, place, :] = along_z

    def step(pair, carry):
        one(pair * 2)
        one(pair * 2 + 1)
        return carry

    lax.fori_loop(0, SLOTS // 2, step, 0)

    live = (iota((SLOTS, LANES), 0) < count_ref[0, 0]).astype(F32)

    def collect(k):
        total = partial[k, pl.ds(0, SLOTS, stride=8), :]
        for y in range(1, 8):
            total = total + partial[k, pl.ds(y, SLOTS, stride=8), :]
        return total * live

    moved = []
    for c in range(3):
        new_velocity[c] = collect(4 * c)
        for k in range(3):
            value = 4.0 * collect(4 * c + 1 + k)
            new_affine[3 * c + k] = value
            moved.append(value)
    old = [deform[k] for k in range(9)]
    fresh = []
    for i in range(3):
        for j in range(3):
            value = old[3 * i + j]
            for k in range(3):
                value = value + DT * moved[3 * i + k] * old[3 * k + j]
            fresh.append(value * live)
    for k in range(9):
        new_deform[k] = fresh[k]
    stress = kirchhoff(fresh)
    for k, entry in enumerate((0, 4, 8, 1, 2, 5)):
        new_stress[k] = stress[entry] * live


def vmem(shape, dtype=F32):
    return pltpu.VMEM(shape, dtype)


def swap(block, axis, shift):
    size = lax.axis_size(axis)
    route = [(i, ((i + shift) ^ 1) - shift) for i in range(size)]
    return lax.ppermute(block, axis, [(i, k) for i, k in route if 0 <= k < size])


def per_device(
    offset, particle_mass, velocity, affine, deform,
    particle_cell, body_id, slot_tile_number, block_count, normal_code,
):
    params = pltpu.CompilerParams(vmem_limit_bytes=VMEM_LIMIT)
    smem = pl.BlockSpec(memory_space=pltpu.SMEM)
    whole = pl.BlockSpec(memory_space=pltpu.VMEM)
    face = jax.ShapeDtypeStruct((FACE_ROWS, DEPTH), F32)

    grid, planes, y_a, y_d = pl.pallas_call(
        scatter_kernel,
        out_shape=(
            jax.ShapeDtypeStruct((8, SIDE, 16, DEPTH), F32),
            jax.ShapeDtypeStruct((8, 4, 16, DEPTH), F32),
            face,
            face,
        ),
        in_specs=[smem, smem] + [whole] * 8,
        out_specs=(whole,) * 4,
        scratch_shapes=[
            vmem((SCATTER_ROWS, SLOTS, LANES)),
            vmem((2, 192, 256), BF16),
            vmem((2, 192, 256), BF16),
            vmem((4, 2, 272, 256)),
            vmem((4, 2, 192, DEPTH)),
        ],
        compiler_params=params,
        name="scatter",
    )(
        slot_tile_number, block_count, offset, particle_mass, velocity, affine, deform,
        particle_cell, body_id, normal_code,
    )
    got_y_a = swap(y_a, "gy", 0)
    got_y_d = swap(y_d, "gy", 1)
    x_a, x_d = pl.pallas_call(
        corner_kernel,
        out_shape=(face, face),
        in_specs=[whole] * 4,
        out_specs=(whole,) * 2,
        scratch_shapes=[vmem((8, 4, 16, DEPTH)), vmem((16, DEPTH))],
        compiler_params=params,
        name="corners",
    )(planes, got_y_a, got_y_d, normal_code)
    got_x_a = swap(x_a, "gx", 0)
    got_x_d = swap(x_d, "gx", 1)

    slots, particles = particle_mass.shape
    return pl.pallas_call(
        functools.partial(gather_kernel, lax.axis_size("gx") - 1, lax.axis_size("gy") - 1),
        out_shape=tuple(
            jax.ShapeDtypeStruct((k, slots, particles), F32) for k in (3, 9, 9, 6)
        ),
        in_specs=[smem, smem] + [whole] * 10,
        out_specs=(whole,) * 4,
        scratch_shapes=[
            vmem((GATHER_ROWS, SLOTS, LANES)),
            vmem((8, SIDE, 16, DEPTH)),
            vmem((SIDE, 16, DEPTH)),
            vmem((2, 3, 3, 8 * SIDE, 256), BF16),
            vmem((2, 3, 3, 8 * SIDE, 256), BF16),
            vmem((12, 8 * SLOTS, LANES)),
        ],
        compiler_params=params,
        name="gather",
    )(
        slot_tile_number, block_count, grid, got_y_a, got_y_d, got_x_a, got_x_d, normal_code,
        offset, particle_cell, body_id, deform,
    )


def solution(mesh):
    both = ("gx", "gy")
    field = P(None, both, None)
    flat = P(both, None)
    return jax.shard_map(
        per_device,
        mesh=mesh,
        in_specs=(
            field, flat, field, field, field, flat, flat, P(both), P("gx", "gy"),
            P("gx", "gy", None),
        ),
        out_specs=(field,) * 4,
        check_vma=False,
    )
```

time: 303 us -> 44.6 us (0.15); the launches traced: 298 us -> 44 us
  other arithmetic: 138 us -> 0 us
  local copies, waits for them, and re-layouts: 86.5 us -> 7.79 us
  matrix products: 26 us -> 0 us
  starting transfers between devices: 32.2 us -> 8.91 us
  Pallas kernels: 0 us -> 12.1 us
    mul x39 -> x0, other arithmetic: 66.7 us -> none  [the longest x6 16 us: build_weights(): weight_x * shared_yz]
    scatter-add x3 -> x0, other arithmetic: 56 us -> none  [the longest x1 55.9 us: per_device(): node_grid = node_grid.at[:, flat_index].add(patches)]
    gather x2 -> x0, local copies, waits for them, and re-layouts: 39 us -> none  [per_device(): block_speeds = flat_speeds[:, flat_index]]
    dot_general x6 -> x0, matrix products: 26 us -> none  [the longest x3 15.9 us: gather_work(): jnp.einsum('glpq,cgq->lcgp', kernel, speed_rows, precision=lax.Precision....]
    ppermute x8 -> x4, starting transfers between devices: 32.2 us -> 8.91 us  [swap(): lax.ppermute(block, axis, [(i, k) for i, k in route if 0 <= k < size])]
    slice x6 -> x0, local copies, waits for them, and re-layouts: 18 us -> none  [the longest x2 17.7 us: per_device(): node_grid[:, :grid_cells]]
    pallas_call x0 -> x3, Pallas kernels: none -> 12.1 us  [the longest x1 7.04 us: per_device(): pl.pallas_call(functools.partial(gather_kernel, lax.axis_size('gx') - 1,...]
    concatenate x1 -> x0, local copies, waits for them, and re-layouts: 9.68 us -> none  [per_device(): jnp.concatenate([speeds.reshape(6, -1), jnp.zeros((6, 1), jnp.float32)], 1)]
  transfers between devices with their start and end apart: 8 -> 4, of which waited for: 5 -> 3; matrix products, arithmetic and copies ran while one was open for 2% -> 0% of each run, Pallas kernels for 0% -> 0%
where the time goes in v1:
time: 44.6 us; the launch traced here: 44 us
  waiting for transfers between devices  13.9 us (31%)
  Pallas kernels  12.1 us (27%)
  starting transfers between devices  8.91 us (20%)
  local copies, waits for them, and re-layouts  7.79 us (17%)
  between operations  1.38 us (3%)
    ppermute x4, waiting for transfers between devices, swap(): lax.ppermute(block, axis, [(i, k) for i, k in route if 0 <= k < size])  13.9 us
    ppermute x4, starting transfers between devices, swap(): lax.ppermute(block, axis, [(i, k) for i, k in route if 0 <= k < size])  8.91 us
    unnamed x30, local copies, waits for them, and re-layouts  7.79 us
    pallas_call x1, Pallas kernels, per_device(): pl.pallas_call(functools.partial(gather_kernel, lax.axis_size('gx') - 1,...  7.04 us
    pallas_call x1, Pallas kernels, per_device(): pl.pallas_call(scatter_kernel, out_shape=(jax.ShapeDtypeStruct((8, SIDE,...  4.82 us
  transfers between devices with their start and end apart: 4, of which 3 were waited for; matrix products, arithmetic and copies ran while one was open for 0% of the time, Pallas kernels for 0%

profile of v1, /device:TPU:101, one launch (start us, length us, event | category | flops | bytes accessed | tf_op | source)
XLA Modules:
  0.0 44.0 jit_solution(12687038693864588025)
XLA Ops:
  0.6 0.0 copy-start.14
  1.3 0.0 copy-start
  1.3 0.8 %copy-done = s32[8,8,256]{2,1,0:T(8,128)S(1)} copy-done((s32[8,8,256]{2,1,0:T(8,128)S(1)}, s32[8,8,256]{2,1,0:T(8,128)}, u32[]{:S(2)}) %copy-start) | copy-done | bytes 65560
  2.1 0.0 copy-start.3
  2.1 0.9 %copy-done.3 = f32[9,24,128]{2,1,0:T(8,128)S(1)} copy-done((f32[9,24,128]{2,1,0:T(8,128)S(1)}, f32[9,24,128]{2,1,0:T(8,128)}, u32[]{:S(2)}) %copy-start.3) | copy-done | bytes 110616
  3.0 0.0 copy-start.4
  3.0 0.8 %copy-done.4 = f32[3,24,128]{2,1,0:T(8,128)S(1)} copy-done((f32[3,24,128]{2,1,0:T(8,128)S(1)}, f32[3,24,128]{2,1,0:T(8,128)}, u32[]{:S(2)}) %copy-start.4) | copy-done | bytes 36888
  3.8 0.0 copy-start.6
  3.8 0.9 %copy-done.6 = f32[9,24,128]{2,1,0:T(8,128)S(1)} copy-done((f32[9,24,128]{2,1,0:T(8,128)S(1)}, f32[9,24,128]{2,1,0:T(8,128)}, u32[]{:S(2)}) %copy-start.6) | copy-done | bytes 110616
  4.7 0.0 copy-start.7
  4.7 0.7 %copy-done.7 = s32[24,128]{1,0:T(8,128)S(1)} copy-done((s32[24,128]{1,0:T(8,128)S(1)}, s32[24,128]{1,0:T(8,128)}, u32[]{:S(2)}) %copy-start.7) | copy-done | bytes 12312
  5.4 0.0 copy-start.9
  5.4 0.7 %copy-done.9 = s32[24,128]{1,0:T(8,128)S(1)} copy-done((s32[24,128]{1,0:T(8,128)S(1)}, s32[24,128]{1,0:T(8,128)}, u32[]{:S(2)}) %copy-start.9) | copy-done | bytes 12312
  6.1 0.0 copy-start.11
  6.1 0.8 %copy-done.11 = f32[3,24,128]{2,1,0:T(8,128)S(1)} copy-done((f32[3,24,128]{2,1,0:T(8,128)S(1)}, f32[3,24,128]{2,1,0:T(8,128)}, u32[]{:S(2)}) %copy-start.11) | copy-done | bytes 36888
  6.9 0.0 copy-start.12
  6.9 0.7 %copy-done.12 = f32[24,128]{1,0:T(8,128)S(1)} copy-done((f32[24,128]{1,0:T(8,128)S(1)}, f32[24,128]{1,0:T(8,128)}, u32[]{:S(2)}) %copy-start.12) | copy-done | bytes 12312
  7.6 0.0 copy-start.13
  7.6 0.7 %copy-done.13 = s32[24]{0:T(128)S(1)} copy-done((s32[24]{0:T(128)S(1)}, s32[24]{0:T(128)}, u32[]{:S(2)}) %copy-start.13) | copy-done | bytes 120
  8.3 0.0 copy-start.2
  8.3 0.0 copy-start.5
  8.3 0.0 copy-start.8
  8.3 0.0 copy-start.10
  8.3 4.8 %scatter.1 = (f32[8,10,16,256]{3,2,1,0:T(8,128)S(1)}, f32[8,4,16,256]{3,2,1,0:T(8,128)S(1)}, f32[176,256]{1,0:T(8,128)S(1)}, f32[176,256]{1,0:T(8,128)S(1)}) custom-call(s32[24]{0:T(128)S(1)} %copy-done.13, s32[1,1]{1,0:T(1,128)S(6)} %copy.14.count_ref, f32[3,24,128]{2,1,0:T(8,128)S(1)} %copy-done.4, f32[24,128]{1,0:T(8,128)S(1)} %copy-done.12, ...), custom_call_target="tpu_custom_call" | custom-call | tf_op jit(solution)/shard_map/scatter/pallas_call | solution.py:496
  13.1 1.4 %collective-permute-start = (f32[176,256]{1,0:T(8,128)S(1)}, f32[176,256]{1,0:T(8,128)S(1)}, u32[]{:S(2)}, u32[]{:S(2)}) collective-permute-start(f32[176,256]{1,0:T(8,128)S(1)} %get-tuple-element.11), channel_id=1, source_target_pairs={{0,1},{1,0},{2,3},{3,2},{4,5},{5,4},{6,7},{7,6},{8,9},{9,8},{10,11... | collective-permute-start | bytes 540680 | tf_op jit(solution)/shard_map/ppermute | solution.py:484
  14.5 3.7 %collective-permute-start.1 = (f32[176,256]{1,0:T(8,128)S(1)}, f32[176,256]{1,0:T(8,128)S(1)}, u32[]{:S(2)}, u32[]{:S(2)}) collective-permute-start(f32[176,256]{1,0:T(8,128)S(1)} %get-tuple-element.12), channel_id=1, source_target_pairs={{1,2},{2,1},{3,4},{4,3},{5,6},{6,5},{9,10},{10,9},{11,12},{12,11},... | collective-permute-start | bytes 540680 | tf_op jit(solution)/shard_map/ppermute | solution.py:484
  18.2 0.4 collective-permute-done.recv_a.y_a
  18.6 6.5 %collective-permute-done.1.recv_d.y_d = f32[176,256]{1,0:T(8,128)S(1)} collective-permute-done((f32[176,256]{1,0:T(8,128)S(1)}, f32[176,256]{1,0:T(8,128)S(1)}, u32[]{:S(2)}, u32[]{:S(2)}) %collective-permute-start.1) | collective-permute-done | bytes 180256 | tf_op jit(solution)/shard_map/ppermute | solution.py:484
  25.1 0.0 copy-start.1
  25.1 0.8 %copy-done.1 = s32[8,8,256]{2,1,0:T(8,128)S(1)} copy-done((s32[8,8,256]{2,1,0:T(8,128)S(1)}, s32[8,8,256]{2,1,0:T(8,128)}, u32[]{:S(2)}) %copy-start.1) | copy-done | bytes 65560
  26.0 0.2 corners.1
  26.2 1.9 %collective-permute-start.2 = (f32[176,256]{1,0:T(8,128)S(1)}, f32[176,256]{1,0:T(8,128)S(1)}, u32[]{:S(2)}, u32[]{:S(2)}) collective-permute-start(f32[176,256]{1,0:T(8,128)S(1)} %get-tuple-element.14), channel_id=1, source_target_pairs={{0,8},{8,0},{16,24},{24,16},{32,40},{40,32},{48,56},{56,48},{64,72... | collective-permute-start | bytes 540680 | tf_op jit(solution)/shard_map/ppermute | solution.py:484
  28.1 1.9 %collective-permute-start.3 = (f32[176,256]{1,0:T(8,128)S(1)}, f32[176,256]{1,0:T(8,128)S(1)}, u32[]{:S(2)}, u32[]{:S(2)}) collective-permute-start(f32[176,256]{1,0:T(8,128)S(1)} %get-tuple-element.15), channel_id=1, source_target_pairs={{8,16},{16,8},{24,32},{32,24},{40,48},{48,40},{56,64},{64,56},{72,... | collective-permute-start | bytes 540680 | tf_op jit(solution)/shard_map/ppermute | solution.py:484
  30.0 0.0 collective-permute-done.2.x_a
  30.0 7.0 %collective-permute-done.3.x_d = f32[176,256]{1,0:T(8,128)S(1)} collective-permute-done((f32[176,256]{1,0:T(8,128)S(1)}, f32[176,256]{1,0:T(8,128)S(1)}, u32[]{:S(2)}, u32[]{:S(2)}) %collective-permute-start.3) | collective-permute-done | bytes 180256 | tf_op jit(solution)/shard_map/ppermute | solution.py:484
  37.0 0.0 copy-done.14
  37.0 0.0 copy-done.2
  37.0 0.0 copy-done.5
  37.0 0.0 copy-done.8
  37.0 0.0 copy-done.10
  37.0 7.0 %gather.1 = (f32[3,24,128]{2,1,0:T(8,128)}, f32[9,24,128]{2,1,0:T(8,128)}, f32[9,24,128]{2,1,0:T(8,128)}, f32[6,24,128]{2,1,0:T(8,128)}) custom-call(s32[24]{0:T(128)S(1)} %copy-done.14, s32[1,1]{1,0:T(1,128)S(6)} %copy.14.count_ref, f32[8,10,16,256]{3,2,1,0:T(8,128)S(1)} %get-tuple-element.10.grid, f32[176,256]{1,0:T(8,128)S(1)} %collective-permute-done.recv_a.y_a, ...), custom_call_target="tpu_custom_call" | custom-call | tf_op jit(solution)/shard_map/gather/pallas_call | solution.py:534
Async XLA Ops:
  0.6 36.3 %copy-start.14 = (s32[24]{0:T(128)S(1)}, s32[24]{0:T(128)}, u32[]{:S(2)}) copy-start(s32[24]{0:T(128)} %tile_ref.3) | copy-start | bytes 292
  1.3 0.8 %copy-start = (s32[8,8,256]{2,1,0:T(8,128)S(1)}, s32[8,8,256]{2,1,0:T(8,128)}, u32[]{:S(2)}) copy-start(s32[8,8,256]{2,1,0:T(8,128)} %code.5) | copy-start | bytes 196612
  2.1 0.9 %copy-start.3 = (f32[9,24,128]{2,1,0:T(8,128)S(1)}, f32[9,24,128]{2,1,0:T(8,128)}, u32[]{:S(2)}) copy-start(f32[9,24,128]{2,1,0:T(8,128)} %deform.3) | copy-start | bytes 331780
  3.0 0.8 %copy-start.4 = (f32[3,24,128]{2,1,0:T(8,128)S(1)}, f32[3,24,128]{2,1,0:T(8,128)}, u32[]{:S(2)}) copy-start(f32[3,24,128]{2,1,0:T(8,128)} %offset.3) | copy-start | bytes 110596
  3.8 0.9 %copy-start.6 = (f32[9,24,128]{2,1,0:T(8,128)S(1)}, f32[9,24,128]{2,1,0:T(8,128)}, u32[]{:S(2)}) copy-start(f32[9,24,128]{2,1,0:T(8,128)} %affine.1) | copy-start | bytes 331780
  4.7 0.7 %copy-start.7 = (s32[24,128]{1,0:T(8,128)S(1)}, s32[24,128]{1,0:T(8,128)}, u32[]{:S(2)}) copy-start(s32[24,128]{1,0:T(8,128)} %cell.3) | copy-start | bytes 36868
  5.4 0.7 %copy-start.9 = (s32[24,128]{1,0:T(8,128)S(1)}, s32[24,128]{1,0:T(8,128)}, u32[]{:S(2)}) copy-start(s32[24,128]{1,0:T(8,128)} %body.3) | copy-start | bytes 36868
  6.1 0.8 %copy-start.11 = (f32[3,24,128]{2,1,0:T(8,128)S(1)}, f32[3,24,128]{2,1,0:T(8,128)}, u32[]{:S(2)}) copy-start(f32[3,24,128]{2,1,0:T(8,128)} %velocity.1) | copy-start | bytes 110596
  6.9 0.7 %copy-start.12 = (f32[24,128]{1,0:T(8,128)S(1)}, f32[24,128]{1,0:T(8,128)}, u32[]{:S(2)}) copy-start(f32[24,128]{1,0:T(8,128)} %mass.1) | copy-start | bytes 36868
  7.6 0.7 %copy-start.13 = (s32[24]{0:T(128)S(1)}, s32[24]{0:T(128)}, u32[]{:S(2)}) copy-start(s32[24]{0:T(128)} %tile_ref.3) | copy-start | bytes 292
  8.3 28.7 %copy-start.2 = (s32[8,8,256]{2,1,0:T(8,128)S(1)}, s32[8,8,256]{2,1,0:T(8,128)}, u32[]{:S(2)}) copy-start(s32[8,8,256]{2,1,0:T(8,128)} %code.5) | copy-start | bytes 196612
  8.3 28.7 %copy-start.5 = (f32[3,24,128]{2,1,0:T(8,128)S(1)}, f32[3,24,128]{2,1,0:T(8,128)}, u32[]{:S(2)}) copy-start(f32[3,24,128]{2,1,0:T(8,128)} %offset.3) | copy-start | bytes 110596
  8.3 28.7 %copy-start.8 = (s32[24,128]{1,0:T(8,128)S(1)}, s32[24,128]{1,0:T(8,128)}, u32[]{:S(2)}) copy-start(s32[24,128]{1,0:T(8,128)} %cell.3) | copy-start | bytes 36868
  8.3 28.7 %copy-start.10 = (s32[24,128]{1,0:T(8,128)S(1)}, s32[24,128]{1,0:T(8,128)}, u32[]{:S(2)}) copy-start(s32[24,128]{1,0:T(8,128)} %body.3) | copy-start | bytes 36868
  13.1 5.5 %collective-permute-start = (f32[176,256]{1,0:T(8,128)S(1)}, f32[176,256]{1,0:T(8,128)S(1)}, u32[]{:S(2)}, u32[]{:S(2)}) collective-permute-start(f32[176,256]{1,0:T(8,128)S(1)} %get-tuple-element.11), channel_id=1, source_target_pairs={{0,1},{1,0},{2,3},{3,2},{4,5},{5,4},{6,7},{7,6},{8,9},{9,8},{10,11... | collective-permute-start | bytes 540680 | tf_op jit(solution)/shard_map/ppermute | solution.py:484
  14.5 10.7 %collective-permute-start.1 = (f32[176,256]{1,0:T(8,128)S(1)}, f32[176,256]{1,0:T(8,128)S(1)}, u32[]{:S(2)}, u32[]{:S(2)}) collective-permute-start(f32[176,256]{1,0:T(8,128)S(1)} %get-tuple-element.12), channel_id=1, source_target_pairs={{1,2},{2,1},{3,4},{4,3},{5,6},{6,5},{9,10},{10,9},{11,12},{12,11},... | collective-permute-start | bytes 540680 | tf_op jit(solution)/shard_map/ppermute | solution.py:484
  25.1 0.8 %copy-start.1 = (s32[8,8,256]{2,1,0:T(8,128)S(1)}, s32[8,8,256]{2,1,0:T(8,128)}, u32[]{:S(2)}) copy-start(s32[8,8,256]{2,1,0:T(8,128)} %code.5) | copy-start | bytes 196612
  26.2 3.8 %collective-permute-start.2 = (f32[176,256]{1,0:T(8,128)S(1)}, f32[176,256]{1,0:T(8,128)S(1)}, u32[]{:S(2)}, u32[]{:S(2)}) collective-permute-start(f32[176,256]{1,0:T(8,128)S(1)} %get-tuple-element.14), channel_id=1, source_target_pairs={{0,8},{8,0},{16,24},{24,16},{32,40},{40,32},{48,56},{56,48},{64,72... | collective-permute-start | bytes 540680 | tf_op jit(solution)/shard_map/ppermute | solution.py:484
  28.1 8.9 %collective-permute-start.3 = (f32[176,256]{1,0:T(8,128)S(1)}, f32[176,256]{1,0:T(8,128)S(1)}, u32[]{:S(2)}, u32[]{:S(2)}) collective-permute-start(f32[176,256]{1,0:T(8,128)S(1)} %get-tuple-element.15), channel_id=1, source_target_pairs={{8,16},{16,8},{24,32},{32,24},{40,48},{48,40},{56,64},{64,56},{72,... | collective-permute-start | bytes 540680 | tf_op jit(solution)/shard_map/ppermute | solution.py:484

commit v2 on v1

v2 whole, which is shorter than its diff:
```python
import functools

import jax
import jax.numpy as jnp
from jax import lax
from jax.experimental import pallas as pl
from jax.experimental.pallas import tpu as pltpu
from jax.sharding import PartitionSpec as P

DT = 0.1
MU = 2.0
LAM = 3.0
GRAVITY = -2.0
FLOOR = 0.25

F32 = jnp.float32
BF16 = jnp.bfloat16
VMEM_LIMIT = 24 * 1024 * 1024

SIDE = 10
DEPTH = 256
SLOTS = 24
LANES = 128
FACE_ROWS = 176

POS_Y, POS_Z, FIELD0, FIELD1, POS_X, LIVE, WX = 0, 1, 2, 3, 4, 5, 6
GATHER_ROWS = WX + 6
MASS = GATHER_ROWS
VEL = MASS + 1
AFF = VEL + 3
SCATTER_ROWS = AFF + 9


def spline(distance):
    size = jnp.abs(distance)
    outer = jnp.maximum(1.5 - size, 0.0)
    inner = jnp.maximum(0.5 - size, 0.0)
    return 0.5 * outer * outer - 1.5 * inner * inner


def determinant(m):
    return (
        m[0] * (m[4] * m[8] - m[5] * m[7])
        - m[1] * (m[3] * m[8] - m[5] * m[6])
        + m[2] * (m[3] * m[7] - m[4] * m[6])
    )


def kirchhoff(m):
    ratio = determinant(m)
    pressure = 0.5 * LAM * (ratio * ratio - 1.0)
    entries = []
    for i in range(3):
        for j in range(3):
            e = m[3 * i] * m[3 * j] + m[3 * i + 1] * m[3 * j + 1] + m[3 * i + 2] * m[3 * j + 2]
            entries.append(MU * (e - 1.0) + pressure if i == j else MU * e)
    return entries


def split(x):
    high = x.astype(BF16)
    return high, (x - high.astype(F32)).astype(BF16)


def matmul_t(a, b):
    return lax.dot_general(a, b, (((1,), (1,)), ((), ())), preferred_element_type=F32)


def matmul(a, b):
    return lax.dot_general(a, b, (((1,), (0,)), ((), ())), preferred_element_type=F32)


def iota(shape, axis):
    return lax.broadcasted_iota(jnp.int32, shape, axis)


def common_rows(table, offset, cell, body):
    cell_x = lax.shift_right_logical(cell, 5).astype(F32)
    cell_y = (lax.shift_right_logical(cell, 3) & 3).astype(F32)
    cell_z = (cell & 7).astype(F32)
    field_one = (body & 1).astype(F32)
    pos_x = cell_x + offset[0]
    table[POS_X] = pos_x
    table[POS_Y] = cell_y + offset[1]
    table[POS_Z] = cell_z + offset[2]
    table[FIELD0] = 1.0 - field_one
    table[FIELD1] = field_one
    for x in range(6):
        table[WX + x] = spline(float(x) - pos_x)


def y_coords(tile_y):
    s = iota((8, LANES), 0)
    wrapped = jnp.where(s < 4, s + 4, s - 4)
    return jnp.where(tile_y == 0, s, wrapped).astype(F32)


def low_side(axis):
    return lax.axis_index(axis) % 2


def scatter_kernel(
    count_ref, tile_in, offset_in, mass_in, velocity_in, affine_in, deform_in, cell_in, body_in,
    code_in,
    grid, face_a, face_d, table, codes,
    tile_ref, offset, mass, velocity, affine, deform, cell, body, code,
    rows, left_hi, left_lo, acc, turned, sems,
):
    pairs = (
        (tile_in, tile_ref), (deform_in, deform), (affine_in, affine),
        (offset_in, offset), (velocity_in, velocity), (mass_in, mass), (cell_in, cell),
        (body_in, body), (code_in, code),
    )
    copies = [
        pltpu.make_async_copy(src, dst, sems.at[i]) for i, (src, dst) in enumerate(pairs)
    ]
    for copy in copies:
        copy.start()
    acc[...] = jnp.zeros_like(acc)
    codes[...] = jnp.zeros_like(codes)
    zeros = jnp.zeros((48, LANES), BF16)
    for u in range(2):
        left_hi[u, 0:48, LANES : 2 * LANES] = zeros
        left_lo[u, 0:48, LANES : 2 * LANES] = zeros
    for copy in copies:
        copy.wait()

    for x in range(8):
        codes[x + 1, 1:9, :] = code[x].astype(F32)
    live = (iota((SLOTS, LANES), 0) < count_ref[0, 0]).astype(F32)
    table[LIVE] = live
    common_rows(table, offset, cell[...], body[...])
    weighted = mass[...] * live
    rows[0] = weighted
    for k in range(3):
        rows[VEL - MASS + k] = weighted * velocity[k]
    stress = kirchhoff([deform[k] for k in range(9)])
    for k in range(9):
        rows[AFF - MASS + k] = weighted * (affine[k] - 4.0 * DT * stress[k])

    def one(s, u):
        tile = tile_ref[s]
        tile_x = lax.shift_right_logical(tile, 6)
        tile_y = lax.shift_right_logical(tile, 5) & 1
        tile_z = tile & 31

        def row(k):
            return (table if k < MASS else rows)[k if k < MASS else k - MASS, pl.ds(s, 1), :]

        dy = y_coords(tile_y) - row(POS_Y)
        wy = spline(dy)
        pos_x = row(POS_X)
        wxy = [wy * row(WX + x) for x in range(6)]

        def put(channel, column, values):
            for pair in range(3):
                hi, lo = split(jnp.concatenate(values[2 * pair : 2 * pair + 2], 0))
                at = channel * 48 + pair * 16
                left_hi[u, at : at + 16, column * LANES : (column + 1) * LANES] = hi
                left_lo[u, at : at + 16, column * LANES : (column + 1) * LANES] = lo

        m = row(MASS)
        put(0, 0, [w * m for w in wxy])
        for k in range(3):
            base = row(VEL + k) + row(AFF + 3 * k + 1) * dy
            ax = row(AFF + 3 * k)
            az = row(AFF + 3 * k + 2)
            put(1 + k, 0, [wxy[x] * (base + ax * (float(x) - pos_x)) for x in range(6)])
            put(1 + k, 1, [wxy[x] * az for x in range(6)])

        dz = iota((16, LANES), 0).astype(F32) - row(POS_Z)
        wz = spline(dz)
        mz = wz * dz
        parts = []
        for f in range(2):
            mask = row(FIELD0 + f)
            parts.append([split(wz * mask), split(mz * mask)])
        right_hi = jnp.concatenate(
            [jnp.concatenate([parts[f][0][0], parts[f][1][0]], 1) for f in range(2)], 0
        )
        right_lo = jnp.concatenate(
            [jnp.concatenate([parts[f][0][1], parts[f][1][1]], 1) for f in range(2)], 0
        )
        both = matmul_t(jnp.concatenate([right_hi, right_lo], 0), left_hi[u])
        rest = matmul_t(right_hi, left_lo[u])
        total = both[0:32] + both[32:64] + rest
        quadrant = tile_x * 2 + tile_y
        start = pl.multiple_of(tile_z * 8, 8)
        for f in range(2):
            acc[quadrant, f, pl.ds(start, 16), 0:192] += total[16 * f : 16 * f + 16]

    def step(pair, carry):
        one(pair * 2, 0)
        one(pair * 2 + 1, 1)
        return carry

    lax.fori_loop(0, SLOTS // 2, step, 0)

    for q in range(4):
        for f in range(2):
            for h in range(2):
                piece = acc[q, f, pl.ds(1 + LANES * h, LANES), 0:256]
                turned[q, f, :, h * LANES : (h + 1) * LANES] = piece.T[0:192]

    s8 = iota((8, DEPTH), 0)
    for f in range(2):
        for c in range(4):
            for x in range(SIDE):
                low = None
                high = None
                for tx in range(2):
                    local = x - 4 * tx
                    if not 0 <= local < 6:
                        continue
                    at = (c * 6 + local) * 8
                    v0 = turned[2 * tx, f, at : at + 8, :]
                    v1 = turned[2 * tx + 1, f, at : at + 8, :]
                    low_v = v0 + jnp.where(s8 >= 4, v1, 0.0)
                    high_v = jnp.where(s8 < 2, v1, 0.0)
                    low = low_v if low is None else low + low_v
                    high = high_v if high is None else high + high_v
                channel = 4 * f + c
                grid[channel, x, 0:8, :] = low
                grid[channel, x, 8:16, :] = high

    side = low_side("gy")
    start_a = pl.multiple_of((1 - side) * 8, 8)
    start_d = pl.multiple_of(side * 8, 8)
    for face, start, owned in ((face_a, start_a, (1 - side) * 7), (face_d, start_d, side * 7)):
        for channel in range(8):
            for x in range(SIDE):
                at = channel * 20 + x * 2
                face[at : at + 2, :] = grid[channel, x, pl.ds(start, 2), :]
        for x in range(8):
            face[160 + x : 161 + x, :] = code[x, pl.ds(owned, 1), :].astype(F32)
        face[168:176, :] = jnp.zeros((8, DEPTH), F32)


def prepare_kernel(tile_ref, table, right_hi, right_lo):
    none = jnp.zeros((16, LANES), BF16)

    def one(s, carry):
        tile_z = tile_ref[s] & 31
        j = (tile_z >= 15).astype(jnp.int32) + (tile_z >= 30).astype(jnp.int32)
        local = tile_z - 15 * j
        odd = local & 1
        tile_row = lax.shift_right_logical(local, 1)
        pos_z = table[POS_Z, pl.ds(s, 1), :] + (odd * 8).astype(F32)
        windows = []
        for r in range(2):
            dz = (iota((16, LANES), 0) + 16 * r).astype(F32) - pos_z
            wz = spline(dz)
            mz = wz * dz
            for f in range(2):
                mask = table[FIELD0 + f, pl.ds(s, 1), :]
                windows.append(split(wz * mask) + split(mz * mask))
        for f in range(2):
            for part in range(4):
                w0, w1 = windows[f][part], windows[2 + f][part]
                out = right_hi if part % 2 == 0 else right_lo
                column = part // 2 * LANES
                for k in range(8):
                    tail = jnp.where(tile_row == k - 1, w1, none) if k else none
                    at = f * LANES + 16 * k
                    out[s, at : at + 16, column : column + LANES] = jnp.where(
                        tile_row == k, w0, tail
                    )
        return carry

    lax.fori_loop(0, SLOTS, one, 0)


def corner_kernel(order, grid, recv_a, recv_d, codes, face_a, face_d, edge, edge_codes):
    side_y = low_side("gy")
    side_x = low_side("gx")
    for plane in range(4):
        x = plane if plane < 2 else plane + 6
        for channel in range(8):
            edge[channel, plane, :, :] = grid[channel, x, :, :]
    for recv, start in ((recv_a, (1 - side_y) * 8), (recv_d, side_y * 8)):
        start = pl.multiple_of(start, 8)
        for channel in range(8):
            for plane in range(4):
                x = plane if plane < 2 else plane + 6
                at = channel * 20 + x * 2
                edge[channel, plane, pl.ds(start, 2), :] += recv[at : at + 2, :]
    edge_codes[0] = codes[1]
    edge_codes[1] = codes[8]
    for recv, halo in ((recv_a, (1 - side_y) * 9), (recv_d, side_y * 9)):
        edge_codes[0, pl.ds(halo, 1), :] = recv[160:161, :]
        edge_codes[1, pl.ds(halo, 1), :] = recv[167:168, :]
    for face, high in ((face_a, 1 - side_x), (face_d, side_x)):
        first = high * 2
        for channel in range(8):
            for p in range(2):
                at = channel * 2 + p
                face[at * 8 : at * 8 + 8, :] = edge[channel, first + p, 0:8, :]
                face[128 + at * 2 : 130 + at * 2, :] = edge[channel, first + p, 8:10, :]
        face[160:170, :] = edge_codes[high, 0:10, :]
        face[170:176, :] = jnp.zeros((6, DEPTH), F32)


def node_speeds(sums, code, inside):
    m0, m1 = sums[0], sums[4]
    r0 = 1.0 / jnp.maximum(m0, FLOOR)
    r1 = 1.0 / jnp.maximum(m1, FLOOR)
    rc = 1.0 / jnp.maximum(m0 + m1, FLOOR)
    share = jnp.minimum(1.0, jnp.minimum(m0, m1) * (1.0 / FLOOR))
    shifted = code + jnp.where(code >= 13.0, 1.0, 0.0)
    third = jnp.where(shifted >= 9.0, 1.0, 0.0) + jnp.where(shifted >= 18.0, 1.0, 0.0)
    rest = shifted - 9.0 * third
    second = jnp.where(rest >= 3.0, 1.0, 0.0) + jnp.where(rest >= 6.0, 1.0, 0.0)
    direction = [third - 1.0, second - 1.0, rest - 3.0 * second - 1.0]
    square = (
        direction[0] * direction[0] + direction[1] * direction[1] + direction[2] * direction[2]
    )
    inverse = jnp.where(square > 2.5, 1.0 / 3.0, jnp.where(square > 1.5, 0.5, 1.0))
    u0 = [sums[1 + k] * r0 for k in range(3)]
    u1 = [sums[5 + k] * r1 for k in range(3)]
    uc = [(sums[1 + k] + sums[5 + k]) * rc for k in range(3)]
    approach0 = sum((u0[k] - uc[k]) * direction[k] for k in range(3))
    approach1 = sum((uc[k] - u1[k]) * direction[k] for k in range(3))
    scale = share * inverse
    push0 = scale * jnp.maximum(approach0, 0.0)
    push1 = scale * jnp.maximum(approach1, 0.0)
    gravity = [0.0, 0.0, DT * GRAVITY]
    v0 = [(u0[k] - push0 * direction[k] + gravity[k]) * inside for k in range(3)]
    v1 = [(u1[k] + push1 * direction[k] + gravity[k]) * inside for k in range(3)]
    return v0, v1


def store_nodes(pair, x_first, sums_at, code_at, last, nodes_hi, nodes_lo):
    index_x = lax.axis_index("gx")
    index_y = lax.axis_index("gy")
    s8 = iota((8, LANES), 0)
    lane = iota((8, LANES), 1)
    inside_low = jnp.where((s8 == 0) & (index_y == 0), 0.0, 1.0)
    inside_high = jnp.where((s8 == 1) & (index_y == last[1]), 0.0, 1.0)

    def tiles(a, b):
        first = jnp.where(lane < 1, 0.0, pltpu.roll(a, 1, 1))
        second = jnp.where(lane < 9, pltpu.roll(a, 9, 1), pltpu.roll(b, 9, 1))
        third = jnp.where(lane < 17, pltpu.roll(b, 17, 1), 0.0)
        return first, second, third

    found = []
    for k in range(2):
        x = x_first + k
        edge = ((x == 0) & (index_x == 0)) | ((x == SIDE - 1) & (index_x == last[0]))
        inside_x = jnp.where(edge, 0.0, 1.0)
        rows = []
        for r in range(2):
            inside = (inside_low if r == 0 else inside_high) * inside_x
            halves = []
            for h in range(2):
                sums = [sums_at(c, k, r, h) for c in range(8)]
                halves.append(node_speeds(sums, code_at(k, r, h), inside))
            rows.append(halves)
        found.append(rows)
    at = pl.multiple_of(pair * 16, 16)
    for f in range(2):
        for c in range(3):
            ready = []
            for k in range(2):
                ready.append([tiles(*(found[k][r][h][f][c] for h in range(2))) for r in range(2)])
            for j in range(3):
                for ty in range(2):
                    pieces = []
                    for k in range(2):
                        low, high = ready[k][0][j], ready[k][1][j]
                        pieces.append(low if ty == 0 else jnp.where(s8 < 2, high, low))
                    hi, lo = split(jnp.concatenate(pieces, 0))
                    lanes = slice(f * LANES, (f + 1) * LANES)
                    nodes_hi[ty, j, c, pl.ds(at, 16), lanes] = hi
                    nodes_lo[ty, j, c, pl.ds(at, 16), lanes] = lo


def half(h):
    return slice(h * LANES, (h + 1) * LANES)


def middle_kernel(last, order, grid, y_a, y_d, codes, nodes_hi, nodes_lo, work, own):
    side_y = low_side("gy")
    for x in range(2, 8):
        own[x - 2] = codes[x]
        for channel in range(8):
            work[channel, x - 2, :, :] = grid[channel, x, :, :]
    for recv, high in ((y_a, 1 - side_y), (y_d, side_y)):
        start = pl.multiple_of(high * 8, 8)
        for x in range(2, 8):
            for channel in range(8):
                at = channel * 20 + x * 2
                work[channel, x - 2, pl.ds(start, 2), :] += recv[at : at + 2, :]
            own[x - 2, pl.ds(high * 9, 1), :] = recv[159 + x : 160 + x, :]

    def step(pair, carry):
        x = pair * 2

        def sums_at(c, k, r, h):
            return work[c, x - 2 + k, 8 * r : 8 * r + 8, half(h)]

        def code_at(k, r, h):
            return own[x - 2 + k, 8 * r : 8 * r + 8, half(h)]

        store_nodes(pair, x, sums_at, code_at, last, nodes_hi, nodes_lo)
        return carry

    lax.fori_loop(1, 4, step, 0)


def gather_kernel(
    last, tile_ref, mid_hi, mid_lo, edge, edge_codes, x_a, x_d,
    table, right_hi, right_lo, deform,
    new_velocity, new_affine, new_deform, new_stress, nodes_hi, nodes_lo,
    work, own, partial,
):
    side_x = low_side("gx")
    for recv, high in ((x_a, 1 - side_x), (x_d, side_x)):
        first = high * 2
        for channel in range(8):
            for p in range(2):
                at = channel * 2 + p
                plane = first + p
                work[channel, plane, 0:8, :] = (
                    edge[channel, plane, 0:8, :] + recv[at * 8 : at * 8 + 8, :]
                )
                work[channel, plane, 8:16, :] = edge[channel, plane, 8:16, :]
                work[channel, plane, 8:10, :] += recv[128 + at * 2 : 130 + at * 2, :]
        own[first + high, 0:10, :] = recv[160:170, :]
        own[first + 1 - high] = edge_codes[high]

    def edge_step(high, carry):
        def sums_at(c, k, r, h):
            return work[c, high * 2 + k, 8 * r : 8 * r + 8, half(h)]

        def code_at(k, r, h):
            return own[high * 2 + k, 8 * r : 8 * r + 8, half(h)]

        store_nodes(high * 4, high * 8, sums_at, code_at, last, nodes_hi, nodes_lo)
        return carry

    lax.fori_loop(0, 2, edge_step, 0)

    def one(s):
        tile = tile_ref[s]
        tile_x = lax.shift_right_logical(tile, 6)
        tile_y = lax.shift_right_logical(tile, 5) & 1
        tile_z = tile & 31
        j = (tile_z >= 15).astype(jnp.int32) + (tile_z >= 30).astype(jnp.int32)

        def row(k):
            return table[k, pl.ds(s, 1), :]

        first = pl.multiple_of(tile_x * 32, 32)
        hi = [nodes_hi[tile_y, j, c, pl.ds(first, 48), :] for c in range(3)]
        lo = [nodes_lo[tile_y, j, c, pl.ds(first, 48), :] for c in range(3)]
        weights = right_hi[s]
        nodes = jnp.concatenate(hi, 0)
        summed = (
            matmul(nodes, weights)
            + matmul(jnp.concatenate(lo, 0), weights)
            + matmul(nodes, right_lo[s])
        )

        dy = y_coords(tile_y) - row(POS_Y)
        wy = spline(dy)
        pos_x = row(POS_X)
        wxy = [wy * row(WX + x) for x in range(6)]
        place = pl.ds(pl.multiple_of(s * 8, 8), 8)
        for c in range(3):
            speed = along_x = along_z = None
            for x in range(5, -1, -1):
                at = (c * 6 + x) * 8
                part = wxy[x] * summed[at : at + 8, 0:LANES]
                moment = wxy[x] * summed[at : at + 8, LANES : 2 * LANES]
                speed = part if speed is None else speed + part
                along_z = moment if along_z is None else along_z + moment
                if x:
                    along_x = speed if along_x is None else along_x + speed
            partial[4 * c, place, :] = speed
            partial[4 * c + 1, place, :] = along_x - pos_x * speed
            partial[4 * c + 2, place, :] = speed * dy
            partial[4 * c + 3, place, :] = along_z

    def step(pair, carry):
        one(pair * 2)
        one(pair * 2 + 1)
        return carry

    lax.fori_loop(0, SLOTS // 2, step, 0)

    live = table[LIVE]

    def collect(k):
        total = partial[k, pl.ds(0, SLOTS, stride=8), :]
        for y in range(1, 8):
            total = total + partial[k, pl.ds(y, SLOTS, stride=8), :]
        return total * live

    moved = []
    for c in range(3):
        new_velocity[c] = collect(4 * c)
        for k in range(3):
            value = 4.0 * collect(4 * c + 1 + k)
            new_affine[3 * c + k] = value
            moved.append(value)
    old = [deform[k] for k in range(9)]
    fresh = []
    for i in range(3):
        for j in range(3):
            value = old[3 * i + j]
            for k in range(3):
                value = value + DT * moved[3 * i + k] * old[3 * k + j]
            fresh.append(value * live)
    for k in range(9):
        new_deform[k] = fresh[k]
    stress = kirchhoff(fresh)
    for k, entry in enumerate((0, 4, 8, 1, 2, 5)):
        new_stress[k] = stress[entry] * live


def vmem(shape, dtype=F32):
    return pltpu.VMEM(shape, dtype)


def cost(flops):
    return pl.CostEstimate(flops=flops, bytes_accessed=4000000, transcendentals=0)


def swap(block, axis, shift):
    size = lax.axis_size(axis)
    route = [(i, ((i + shift) ^ 1) - shift) for i in range(size)]
    return lax.ppermute(block, axis, [(i, k) for i, k in route if 0 <= k < size])


def per_device(
    offset, particle_mass, velocity, affine, deform,
    particle_cell, body_id, slot_tile_number, block_count, normal_code,
):
    params = pltpu.CompilerParams(vmem_limit_bytes=VMEM_LIMIT)
    smem = pl.BlockSpec(memory_space=pltpu.SMEM)
    hbm = pl.BlockSpec(memory_space=pltpu.HBM)
    whole = pl.BlockSpec(memory_space=pltpu.VMEM)
    face = jax.ShapeDtypeStruct((FACE_ROWS, DEPTH), F32)
    nodes = jax.ShapeDtypeStruct((2, 3, 3, 8 * SIDE, 256), BF16)
    right = jax.ShapeDtypeStruct((SLOTS, 256, 256), BF16)
    last = (lax.axis_size("gx") - 1, lax.axis_size("gy") - 1)
    inputs = (
        slot_tile_number, offset, particle_mass, velocity, affine, deform, particle_cell,
        body_id, normal_code,
    )

    grid, y_a, y_d, table, codes = pl.pallas_call(
        scatter_kernel,
        out_shape=(
            jax.ShapeDtypeStruct((8, SIDE, 16, DEPTH), F32),
            face,
            face,
            jax.ShapeDtypeStruct((GATHER_ROWS, SLOTS, LANES), F32),
            jax.ShapeDtypeStruct((SIDE, 16, DEPTH), F32),
        ),
        in_specs=[smem] + [hbm] * 9,
        out_specs=(whole,) * 5,
        scratch_shapes=[pltpu.SMEM(x.shape, x.dtype) for x in inputs[:1]]
        + [vmem(x.shape, x.dtype) for x in inputs[1:]]
        + [
            vmem((SCATTER_ROWS - GATHER_ROWS, SLOTS, LANES)),
            vmem((2, 192, 256), BF16),
            vmem((2, 192, 256), BF16),
            vmem((4, 2, 272, 256)),
            vmem((4, 2, 192, DEPTH)),
            pltpu.SemaphoreType.DMA((9,)),
        ],
        compiler_params=params,
        cost_estimate=pl.CostEstimate(flops=10**9, bytes_accessed=1, transcendentals=0),
        name="scatter",
    )(
        block_count,
        *(pltpu.with_memory_space_constraint(x, pltpu.HBM) for x in inputs),
    )
    got_y_a = swap(y_a, "gy", 0)
    got_y_d = swap(y_d, "gy", 1)
    right_hi, right_lo = pl.pallas_call(
        prepare_kernel,
        out_shape=(right, right),
        in_specs=[smem, whole],
        out_specs=(whole,) * 2,
        compiler_params=params,
        cost_estimate=cost(3000000),
        name="prepare",
    )(slot_tile_number, table)
    x_a, x_d, edge, edge_codes = pl.pallas_call(
        corner_kernel,
        out_shape=(
            face,
            face,
            jax.ShapeDtypeStruct((8, 4, 16, DEPTH), F32),
            jax.ShapeDtypeStruct((2, 16, DEPTH), F32),
        ),
        in_specs=[pl.BlockSpec(memory_space=pl.ANY)] + [whole] * 4,
        out_specs=(whole,) * 4,
        compiler_params=params,
        name="corners",
    )(right_hi, grid, got_y_a, got_y_d, codes)
    got_x_a = swap(x_a, "gx", 0)
    got_x_d = swap(x_d, "gx", 1)
    mid_hi, mid_lo = pl.pallas_call(
        functools.partial(middle_kernel, last),
        out_shape=(nodes, nodes),
        in_specs=[pl.BlockSpec(memory_space=pl.ANY)] + [whole] * 4,
        out_specs=(whole,) * 2,
        scratch_shapes=[vmem((8, 6, 16, DEPTH)), vmem((6, 16, DEPTH))],
        compiler_params=params,
        cost_estimate=cost(3000000),
        name="middle",
    )(edge_codes, grid, got_y_a, got_y_d, codes)

    slots, particles = particle_mass.shape
    out = pl.pallas_call(
        functools.partial(gather_kernel, last),
        out_shape=tuple(jax.ShapeDtypeStruct((k, slots, particles), F32) for k in (3, 9, 9, 6))
        + (nodes, nodes),
        in_specs=[smem] + [whole] * 10,
        out_specs=(whole,) * 6,
        scratch_shapes=[
            vmem((8, 4, 16, DEPTH)),
            vmem((4, 16, DEPTH)),
            vmem((12, 8 * SLOTS, LANES)),
        ],
        input_output_aliases={1: 4, 2: 5},
        compiler_params=params,
        name="gather",
    )(
        slot_tile_number, mid_hi, mid_lo, edge, edge_codes, got_x_a, got_x_d,
        table, right_hi, right_lo, deform,
    )
    return out[:4]


def solution(mesh):
    both = ("gx", "gy")
    field = P(None, both, None)
    flat = P(both, None)
    return jax.shard_map(
        per_device,
        mesh=mesh,
        in_specs=(
            field, flat, field, field, field, flat, flat, P(both), P("gx", "gy"),
            P("gx", "gy", None),
        ),
        out_specs=(field,) * 4,
        check_vma=False,
    )
```

time: 44.6 us -> 35.4 us (0.79)
  local copies, waits for them, and re-layouts: 7.79 us -> 0.01 us
  waiting for transfers between devices: 13.9 us -> 10.8 us
  Pallas kernels: 12.1 us -> 14.2 us
    unnamed x30 -> x4, local copies, waits for them, and re-layouts: 7.79 us -> 0.01 us
    ppermute x4, waiting for transfers between devices: 13.9 us -> 10.8 us  [swap(): lax.ppermute(block, axis, [(i, k) for i, k in route if 0 <= k < size])]
    pallas_call x2 -> x4, Pallas kernels: 7.24 us -> 8.86 us  [the longest x1 5.59 us: per_device(): pl.pallas_call(functools.partial(gather_kernel, last), out_shape=tuple((j...]
    pallas_call x1, Pallas kernels: 4.82 us -> 5.33 us  [per_device(): pl.pallas_call(scatter_kernel, out_shape=(jax.ShapeDtypeStruct((8, SIDE,...]
  transfers between devices with their start and end apart: 4 -> 4, of which waited for: 3 -> 2; matrix products, arithmetic and copies ran while one was open for 0% -> 0% of each run, Pallas kernels for 0% -> 9%
where the time goes in v2:
time: 35.4 us; the launch traced here: 35.3 us
  Pallas kernels  14.2 us (40%)
  waiting for transfers between devices  10.8 us (31%)
  starting transfers between devices  8.91 us (25%)
  between operations  1.37 us (4%)
    ppermute x4, waiting for transfers between devices, swap(): lax.ppermute(block, axis, [(i, k) for i, k in route if 0 <= k < size])  10.8 us
    ppermute x4, starting transfers between devices, swap(): lax.ppermute(block, axis, [(i, k) for i, k in route if 0 <= k < size])  8.91 us
    pallas_call x1, Pallas kernels, per_device(): pl.pallas_call(functools.partial(gather_kernel, last), out_shape=tuple((j...  5.59 us
    pallas_call x1, Pallas kernels, per_device(): pl.pallas_call(scatter_kernel, out_shape=(jax.ShapeDtypeStruct((8, SIDE,...  5.33 us
    pallas_call x1, Pallas kernels, per_device(): pl.pallas_call(prepare_kernel, out_shape=(right, right), in_specs=[smem,...  2.16 us
    pallas_call x1, Pallas kernels, per_device(): pl.pallas_call(functools.partial(middle_kernel, last), out_shape=(nodes,...  0.91 us
  transfers between devices with their start and end apart: 4, of which 2 were waited for; matrix products, arithmetic and copies ran while one was open for 0% of the time, Pallas kernels for 9%

profile of v2, /device:TPU:101, one launch (start us, length us, event | category | flops | bytes accessed | tf_op | source)
XLA Modules:
  0.0 35.3 jit_solution(4626271157558272394)
XLA Ops:
  0.6 0.0 copy-start.1
  1.3 5.3 %scatter.1 = (f32[8,10,16,256]{3,2,1,0:T(8,128)S(1)}, f32[176,256]{1,0:T(8,128)S(1)}, f32[176,256]{1,0:T(8,128)S(1)}, f32[12,24,128]{2,1,0:T(8,128)S(1)}, f32[10,16,256]{2,1,0:T(8,128)S(1)}) custom-call(s32[1,1]{1,0:T(1,128)S(6)} %copy.18.count_ref, s32[24]{0:T(128)} %tile_ref.3, f32[3,24,128]{2,1,0:T(8,128)} %offset_in.1, f32[24,128]{1,0:T(8,128)} %mass_in.1, ...), custom_call_target="tpu_custom_call" | custom-call | flops 1000000000 | bytes 1 | tf_op jit(solution)/shard_map/scatter/pallas_call | solution.py:553
  6.6 1.4 %collective-permute-start = (f32[176,256]{1,0:T(8,128)S(1)}, f32[176,256]{1,0:T(8,128)S(1)}, u32[]{:S(2)}, u32[]{:S(2)}) collective-permute-start(f32[176,256]{1,0:T(8,128)S(1)} %get-tuple-element.24), channel_id=1, source_target_pairs={{0,1},{1,0},{2,3},{3,2},{4,5},{5,4},{6,7},{7,6},{8,9},{9,8},{10,11... | collective-permute-start | bytes 540680 | tf_op jit(solution)/shard_map/ppermute | solution.py:533
  8.0 3.7 %collective-permute-start.1 = (f32[176,256]{1,0:T(8,128)S(1)}, f32[176,256]{1,0:T(8,128)S(1)}, u32[]{:S(2)}, u32[]{:S(2)}) collective-permute-start(f32[176,256]{1,0:T(8,128)S(1)} %get-tuple-element.25), channel_id=1, source_target_pairs={{1,2},{2,1},{3,4},{4,3},{5,6},{6,5},{9,10},{10,9},{11,12},{12,11},... | collective-permute-start | bytes 540680 | tf_op jit(solution)/shard_map/ppermute | solution.py:533
  11.8 0.0 copy-done.1
  11.8 2.2 %prepare.1 = (bf16[24,256,256]{2,1,0:T(8,128)(2,1)S(1)}, bf16[24,256,256]{2,1,0:T(8,128)(2,1)S(1)}) custom-call(s32[24]{0:T(128)S(1)} %copy-done.1, f32[12,24,128]{2,1,0:T(8,128)S(1)} %get-tuple-element.21.table), custom_call_target="tpu_custom_call" | custom-call | flops 3000000 | bytes 4000000 | tf_op jit(solution)/shard_map/prepare/pallas_call | solution.py:583
  13.9 0.0 collective-permute-done.recv_a.y_a
  13.9 4.7 %collective-permute-done.1.recv_d.y_d = f32[176,256]{1,0:T(8,128)S(1)} collective-permute-done((f32[176,256]{1,0:T(8,128)S(1)}, f32[176,256]{1,0:T(8,128)S(1)}, u32[]{:S(2)}, u32[]{:S(2)}) %collective-permute-start.1) | collective-permute-done | bytes 180256 | tf_op jit(solution)/shard_map/ppermute | solution.py:533
  18.7 0.0 copy-start
  18.7 0.2 corners.1
  18.9 1.9 %collective-permute-start.2 = (f32[176,256]{1,0:T(8,128)S(1)}, f32[176,256]{1,0:T(8,128)S(1)}, u32[]{:S(2)}, u32[]{:S(2)}) collective-permute-start(f32[176,256]{1,0:T(8,128)S(1)} %get-tuple-element.31), channel_id=1, source_target_pairs={{0,8},{8,0},{16,24},{24,16},{32,40},{40,32},{48,56},{56,48},{64,72... | collective-permute-start | bytes 540680 | tf_op jit(solution)/shard_map/ppermute | solution.py:533
  20.8 1.9 %collective-permute-start.3 = (f32[176,256]{1,0:T(8,128)S(1)}, f32[176,256]{1,0:T(8,128)S(1)}, u32[]{:S(2)}, u32[]{:S(2)}) collective-permute-start(f32[176,256]{1,0:T(8,128)S(1)} %get-tuple-element.32), channel_id=1, source_target_pairs={{8,16},{16,8},{24,32},{32,24},{40,48},{48,40},{56,64},{64,56},{72,... | collective-permute-start | bytes 540680 | tf_op jit(solution)/shard_map/ppermute | solution.py:533
  22.7 0.9 %middle.1 = (bf16[2,3,3,80,256]{4,3,2,1,0:T(8,128)(2,1)S(1)}, bf16[2,3,3,80,256]{4,3,2,1,0:T(8,128)(2,1)S(1)}) custom-call(f32[2,16,256]{2,1,0:T(8,128)S(1)} %get-tuple-element.27.order.edge_codes, f32[8,10,16,256]{3,2,1,0:T(8,128)S(1)} %get-tuple-element.23.grid, f32[176,256]{1,0:T(8,128)S(1)} %collective-permute-done.recv_a.y_a, ...), custom_call_target="tpu_custom_call" | custom-call | flops 3000000 | bytes 4000000 | tf_op jit(solution)/shard_map/middle/pallas_call | solution.py:607
  23.6 0.0 collective-permute-done.2.x_a
  23.6 6.1 %collective-permute-done.3.x_d = f32[176,256]{1,0:T(8,128)S(1)} collective-permute-done((f32[176,256]{1,0:T(8,128)S(1)}, f32[176,256]{1,0:T(8,128)S(1)}, u32[]{:S(2)}, u32[]{:S(2)}) %collective-permute-start.3) | collective-permute-done | bytes 180256 | tf_op jit(solution)/shard_map/ppermute | solution.py:533
  29.7 0.0 copy-done
  29.7 5.6 %gather.1 = (f32[3,24,128]{2,1,0:T(8,128)}, f32[9,24,128]{2,1,0:T(8,128)}, f32[9,24,128]{2,1,0:T(8,128)}, f32[6,24,128]{2,1,0:T(8,128)}, bf16[2,3,3,80,256]{4,3,...) custom-call(s32[24]{0:T(128)S(1)} %copy-done.1, ...), custom_call_target="tpu_custom_call", output_to_operand_aliasing={{4}: (1, {}), {5}: (2, {})} | custom-call | tf_op jit(solution)/shard_map/gather/pallas_call | solution.py:619
Async XLA Ops:
  0.6 11.1 %copy-start.1 = (s32[24]{0:T(128)S(1)}, s32[24]{0:T(128)}, u32[]{:S(2)}) copy-start(s32[24]{0:T(128)} %tile_ref.3) | copy-start | bytes 292
  6.6 7.3 %collective-permute-start = (f32[176,256]{1,0:T(8,128)S(1)}, f32[176,256]{1,0:T(8,128)S(1)}, u32[]{:S(2)}, u32[]{:S(2)}) collective-permute-start(f32[176,256]{1,0:T(8,128)S(1)} %get-tuple-element.24), channel_id=1, source_target_pairs={{0,1},{1,0},{2,3},{3,2},{4,5},{5,4},{6,7},{7,6},{8,9},{9,8},{10,11... | collective-permute-start | bytes 540680 | tf_op jit(solution)/shard_map/ppermute | solution.py:533
  8.0 10.7 %collective-permute-start.1 = (f32[176,256]{1,0:T(8,128)S(1)}, f32[176,256]{1,0:T(8,128)S(1)}, u32[]{:S(2)}, u32[]{:S(2)}) collective-permute-start(f32[176,256]{1,0:T(8,128)S(1)} %get-tuple-element.25), channel_id=1, source_target_pairs={{1,2},{2,1},{3,4},{4,3},{5,6},{6,5},{9,10},{10,9},{11,12},{12,11},... | collective-permute-start | bytes 540680 | tf_op jit(solution)/shard_map/ppermute | solution.py:533
  18.7 11.0 %copy-start = (f32[9,24,128]{2,1,0:T(8,128)S(1)}, f32[9,24,128]{2,1,0:T(8,128)}, u32[]{:S(2)}) copy-start(f32[9,24,128]{2,1,0:T(8,128)} %deform.1) | copy-start | bytes 331780
  18.9 4.7 %collective-permute-start.2 = (f32[176,256]{1,0:T(8,128)S(1)}, f32[176,256]{1,0:T(8,128)S(1)}, u32[]{:S(2)}, u32[]{:S(2)}) collective-permute-start(f32[176,256]{1,0:T(8,128)S(1)} %get-tuple-element.31), channel_id=1, source_target_pairs={{0,8},{8,0},{16,24},{24,16},{32,40},{40,32},{48,56},{56,48},{64,72... | collective-permute-start | bytes 540680 | tf_op jit(solution)/shard_map/ppermute | solution.py:533
  20.8 8.9 %collective-permute-start.3 = (f32[176,256]{1,0:T(8,128)S(1)}, f32[176,256]{1,0:T(8,128)S(1)}, u32[]{:S(2)}, u32[]{:S(2)}) collective-permute-start(f32[176,256]{1,0:T(8,128)S(1)} %get-tuple-element.32), channel_id=1, source_target_pairs={{8,16},{16,8},{24,32},{32,24},{40,48},{48,40},{56,64},{64,56},{72,... | collective-permute-start | bytes 540680 | tf_op jit(solution)/shard_map/ppermute | solution.py:533

commit v3 on v2

v3 whole, which is shorter than its diff:
```python
import functools

import jax
import jax.numpy as jnp
from jax import lax
from jax.experimental import pallas as pl
from jax.experimental.pallas import tpu as pltpu
from jax.sharding import PartitionSpec as P


DT = 0.1
MU = 2.0
LAM = 3.0
GRAVITY = -2.0
FLOOR = 0.25

F32 = jnp.float32
BF16 = jnp.bfloat16
VMEM_LIMIT = 24 * 1024 * 1024

SIDE = 10
DEPTH = 256
SLOTS = 24
LANES = 128
FACE_ROWS = 176
CHUNK = 8

POS_Y, POS_Z, FIELD0, FIELD1, POS_X, LIVE, WX = 0, 1, 2, 3, 4, 5, 6
GATHER_ROWS = WX + 6
MASS = GATHER_ROWS
VEL = MASS + 1
AFF = VEL + 3
SCATTER_ROWS = AFF + 9


def spline(distance):
    size = jnp.abs(distance)
    outer = jnp.maximum(1.5 - size, 0.0)
    inner = jnp.maximum(0.5 - size, 0.0)
    return 0.5 * outer * outer - 1.5 * inner * inner


def determinant(m):
    return (
        m[0] * (m[4] * m[8] - m[5] * m[7])
        - m[1] * (m[3] * m[8] - m[5] * m[6])
        + m[2] * (m[3] * m[7] - m[4] * m[6])
    )


def kirchhoff(m):
    ratio = determinant(m)
    pressure = 0.5 * LAM * (ratio * ratio - 1.0)
    entries = []
    for i in range(3):
        for j in range(3):
            e = m[3 * i] * m[3 * j] + m[3 * i + 1] * m[3 * j + 1] + m[3 * i + 2] * m[3 * j + 2]
            entries.append(MU * (e - 1.0) + pressure if i == j else MU * e)
    return entries


def split(x):
    high = x.astype(BF16)
    return high, (x - high.astype(F32)).astype(BF16)


def matmul_t(a, b):
    return lax.dot_general(a, b, (((1,), (1,)), ((), ())), preferred_element_type=F32)


def matmul(a, b):
    return lax.dot_general(a, b, (((1,), (0,)), ((), ())), preferred_element_type=F32)


def iota(shape, axis):
    return lax.broadcasted_iota(jnp.int32, shape, axis)


def y_coords(tile_y):
    s = iota((8, LANES), 0)
    wrapped = jnp.where(s < 4, s + 4, s - 4)
    return jnp.where(tile_y == 0, s, wrapped).astype(F32)


def low_side(axis):
    return lax.axis_index(axis) % 2


def half(h):
    return slice(h * LANES, (h + 1) * LANES)


def matching_slots(order, tile_ref, tile_y):
    def body(s, n):
        order[n] = s
        return n + ((lax.shift_right_logical(tile_ref[0, s], 5) & 1) == tile_y).astype(jnp.int32)

    n = lax.fori_loop(0, SLOTS, body, 0)
    order[n] = SLOTS
    return n


def clear(left_hi, left_lo, acc):
    acc[...] = jnp.zeros_like(acc)
    zeros = jnp.zeros((48, LANES), BF16)
    for u in range(2):
        left_hi[u, 0:48, LANES : 2 * LANES] = zeros
        left_lo[u, 0:48, LANES : 2 * LANES] = zeros


def scatter_half(tile_y, tile_ref, table, rows, codes, halves, face, order, left_hi, left_lo,
                 acc, turned):
    count = matching_slots(order, tile_ref, tile_y)

    def one(index, u):
        s = order[index]
        tile = tile_ref[0, jnp.minimum(s, SLOTS - 1)]
        tile_x = lax.shift_right_logical(tile, 6)
        tile_z = tile & 31

        def row(k):
            return table[k, pl.ds(s, 1), :] if k < MASS else rows[k - MASS, pl.ds(s, 1), :]

        dy = y_coords(tile_y) - row(POS_Y)
        wy = spline(dy)
        pos_x = row(POS_X)
        wxy = [wy * row(WX + x) for x in range(6)]

        def put(channel, column, values):
            for pair in range(3):
                hi, lo = split(jnp.concatenate(values[2 * pair : 2 * pair + 2], 0))
                at = channel * 48 + pair * 16
                left_hi[u, at : at + 16, column * LANES : (column + 1) * LANES] = hi
                left_lo[u, at : at + 16, column * LANES : (column + 1) * LANES] = lo

        m = row(MASS)
        put(0, 0, [w * m for w in wxy])
        for k in range(3):
            base = row(VEL + k) + row(AFF + 3 * k + 1) * dy
            ax = row(AFF + 3 * k)
            az = row(AFF + 3 * k + 2)
            put(1 + k, 0, [wxy[x] * (base + ax * (float(x) - pos_x)) for x in range(6)])
            put(1 + k, 1, [wxy[x] * az for x in range(6)])

        dz = iota((16, LANES), 0).astype(F32) - row(POS_Z)
        wz = spline(dz)
        mz = wz * dz
        parts = []
        for f in range(2):
            mask = row(FIELD0 + f)
            parts.append([split(wz * mask), split(mz * mask)])
        right_hi = jnp.concatenate(
            [jnp.concatenate([parts[f][0][0], parts[f][1][0]], 1) for f in range(2)], 0
        )
        right_lo = jnp.concatenate(
            [jnp.concatenate([parts[f][0][1], parts[f][1][1]], 1) for f in range(2)], 0
        )
        both = matmul_t(jnp.concatenate([right_hi, right_lo], 0), left_hi[u])
        rest = matmul_t(right_hi, left_lo[u])
        total = both[0:32] + both[32:64] + rest
        window = pl.ds(tile_z * 8 + 7, 16)
        for f in range(2):
            acc[tile_x, f, 0, window, :] += total[16 * f : 16 * f + 16, 0:LANES]
            acc[tile_x, f, 1, window, 0:64] += total[16 * f : 16 * f + 16, LANES:192]

    def step(pair, carry):
        one(pair * 2, 0)
        one(pair * 2 + 1, 1)
        return carry

    lax.fori_loop(0, lax.shift_right_logical(count + 1, 1), step, 0)

    for tx in range(2):
        for f in range(2):
            for h in range(2):
                z = slice(8 + LANES * h, 8 + LANES * (h + 1))
                turned[tx, f, 0:128, half(h)] = acc[tx, f, 0, z, :].T
                turned[tx, f, 128:192, half(h)] = acc[tx, f, 1, z, :].T[0:64]

    for f in range(2):
        for c in range(4):
            for x in range(SIDE):
                parts = [
                    turned[tx, f, (c * 6 + x - 4 * tx) * 8 : (c * 6 + x - 4 * tx) * 8 + 8, :]
                    for tx in range(2)
                    if 0 <= x - 4 * tx < 6
                ]
                total = sum(parts[1:], parts[0])
                channel = 4 * f + c
                halves[tile_y, channel, x, :, :] = total
                at = channel * 20 + x * 2
                face[at : at + 2, :] = total[0:2]
    for x in range(8):
        face[160 + x : 161 + x, :] = codes[x + 1, pl.ds(1 + tile_y * 7, 1), :]
    face[168:176, :] = jnp.zeros((8, DEPTH), F32)


def first_kernel(
    count_ref, tile_in, offset_in, mass_in, velocity_in, affine_in, deform_in, cell_in, body_in,
    code_in,
    halves, face, table, rows, codes, tile_ref,
    offset, mass, velocity, affine, deform, cell, body, code,
    order, left_hi, left_lo, acc, turned, sems,
):
    pairs = (
        (tile_in, tile_ref.at[0]), (deform_in, deform), (affine_in, affine),
        (offset_in, offset), (velocity_in, velocity), (mass_in, mass), (cell_in, cell),
        (body_in, body), (code_in, code),
    )
    copies = [
        pltpu.make_async_copy(src, dst, sems.at[i]) for i, (src, dst) in enumerate(pairs)
    ]
    for copy in copies:
        copy.start()
    clear(left_hi, left_lo, acc)
    codes[...] = jnp.zeros_like(codes)
    for out in (table, rows):
        for k in range(out.shape[0]):
            out[k, SLOTS:32, :] = jnp.zeros((32 - SLOTS, LANES), F32)
    for copy in copies:
        copy.wait()

    for x in range(8):
        codes[x + 1, 1:9, :] = code[x].astype(F32)
    live = (iota((SLOTS, LANES), 0) < count_ref[0, 0]).astype(F32)
    cell = cell[...]
    field_one = (body[...] & 1).astype(F32)
    pos_x = lax.shift_right_logical(cell, 5).astype(F32) + offset[0]
    own = slice(0, SLOTS)
    table[LIVE, own] = live
    table[POS_X, own] = pos_x
    table[POS_Y, own] = (lax.shift_right_logical(cell, 3) & 3).astype(F32) + offset[1]
    table[POS_Z, own] = (cell & 7).astype(F32) + offset[2]
    table[FIELD0, own] = 1.0 - field_one
    table[FIELD1, own] = field_one
    for x in range(6):
        table[WX + x, own] = spline(float(x) - pos_x)
    weighted = mass[...] * live
    rows[0, own] = weighted
    for k in range(3):
        rows[VEL - MASS + k, own] = weighted * velocity[k]
    stress = kirchhoff([deform[k] for k in range(9)])
    for k in range(9):
        rows[AFF - MASS + k, own] = weighted * (affine[k] - 4.0 * DT * stress[k])
    scatter_half(
        low_side("gy"), tile_ref, table, rows, codes, halves, face, order, left_hi, left_lo,
        acc, turned,
    )


def second_kernel(
    tile_ref, half_in, table, rows, codes, halves, face, order, left_hi, left_lo, acc, turned,
):
    clear(left_hi, left_lo, acc)
    scatter_half(
        1 - low_side("gy"), tile_ref, table, rows, codes, halves, face, order, left_hi, left_lo,
        acc, turned,
    )


def join(halves, channel, x):
    low, high = halves[0, channel, x], halves[1, channel, x]
    return low + jnp.where(iota((8, DEPTH), 0) >= 4, high, 0.0), high


def prepare_kernel(order, tile_ref, table, right):
    none = jnp.zeros((16, 2 * LANES), BF16)

    def one(s, carry):
        dz = iota((16, LANES), 0).astype(F32) - table[POS_Z, pl.ds(s, 1), :]
        wz = spline(dz)
        mz = wz * dz
        for f in range(2):
            mask = table[FIELD0 + f, pl.ds(s, 1), :]
            hi, lo = split(jnp.concatenate([wz * mask, mz * mask], 1))
            for k, rows in enumerate((hi, lo, hi, none)):
                right[s, 64 * f + 16 * k : 64 * f + 16 * k + 16, :] = rows
        return carry

    lax.fori_loop(0, SLOTS, one, 0, unroll=2)


def corner_kernel(order, halves, recv_a, recv_d, codes, face_a, face_d, edge, edge_codes):
    side_y = low_side("gy")
    side_x = low_side("gx")
    for plane in range(4):
        x = plane if plane < 2 else plane + 6
        for channel in range(8):
            edge[channel, plane, 0:8, :], edge[channel, plane, 8:16, :] = join(halves, channel, x)
    for recv, start in ((recv_a, (1 - side_y) * 8), (recv_d, side_y * 8)):
        start = pl.multiple_of(start, 8)
        for channel in range(8):
            for plane in range(4):
                x = plane if plane < 2 else plane + 6
                at = channel * 20 + x * 2
                edge[channel, plane, pl.ds(start, 2), :] += recv[at : at + 2, :]
    edge_codes[0] = codes[1]
    edge_codes[1] = codes[8]
    for recv, halo in ((recv_a, (1 - side_y) * 9), (recv_d, side_y * 9)):
        edge_codes[0, pl.ds(halo, 1), :] = recv[160:161, :]
        edge_codes[1, pl.ds(halo, 1), :] = recv[167:168, :]
    for face, high in ((face_a, 1 - side_x), (face_d, side_x)):
        first = high * 2
        for channel in range(8):
            for p in range(2):
                at = channel * 2 + p
                face[at * 8 : at * 8 + 8, :] = edge[channel, first + p, 0:8, :]
                face[128 + at * 2 : 130 + at * 2, :] = edge[channel, first + p, 8:10, :]
        face[160:170, :] = edge_codes[high, 0:10, :]
        face[170:176, :] = jnp.zeros((6, DEPTH), F32)


def node_speeds(sums, code, inside):
    m0, m1 = sums[0], sums[4]
    r0 = 1.0 / jnp.maximum(m0, FLOOR)
    r1 = 1.0 / jnp.maximum(m1, FLOOR)
    rc = 1.0 / jnp.maximum(m0 + m1, FLOOR)
    share = jnp.minimum(1.0, jnp.minimum(m0, m1) * (1.0 / FLOOR))
    shifted = code + jnp.where(code >= 13.0, 1.0, 0.0)
    third = jnp.where(shifted >= 9.0, 1.0, 0.0) + jnp.where(shifted >= 18.0, 1.0, 0.0)
    rest = shifted - 9.0 * third
    second = jnp.where(rest >= 3.0, 1.0, 0.0) + jnp.where(rest >= 6.0, 1.0, 0.0)
    direction = [third - 1.0, second - 1.0, rest - 3.0 * second - 1.0]
    square = (
        direction[0] * direction[0] + direction[1] * direction[1] + direction[2] * direction[2]
    )
    inverse = jnp.where(square > 2.5, 1.0 / 3.0, jnp.where(square > 1.5, 0.5, 1.0))
    u0 = [sums[1 + k] * r0 for k in range(3)]
    u1 = [sums[5 + k] * r1 for k in range(3)]
    uc = [(sums[1 + k] + sums[5 + k]) * rc for k in range(3)]
    approach0 = sum((u0[k] - uc[k]) * direction[k] for k in range(3))
    approach1 = sum((uc[k] - u1[k]) * direction[k] for k in range(3))
    scale = share * inverse
    push0 = scale * jnp.maximum(approach0, 0.0)
    push1 = scale * jnp.maximum(approach1, 0.0)
    gravity = [0.0, 0.0, DT * GRAVITY]
    v0 = [(u0[k] - push0 * direction[k] + gravity[k]) * inside for k in range(3)]
    v1 = [(u1[k] + push1 * direction[k] + gravity[k]) * inside for k in range(3)]
    return v0, v1


def store_nodes(x_first, sums_at, code_at, last, nodes):
    index_x = lax.axis_index("gx")
    index_y = lax.axis_index("gy")
    s8 = iota((8, LANES), 0)
    lane = iota((8, LANES), 1)
    inside_low = jnp.where((s8 == 0) & (index_y == 0), 0.0, 1.0)
    inside_high = jnp.where((s8 == 1) & (index_y == last[1]), 0.0, 1.0)
    local = lane & 63

    def tiles(v0, v1):
        def both(h, shift):
            return jnp.where(
                lane < 64, pltpu.roll(v0[h], shift, 1), pltpu.roll(v1[h], (shift + 64) % 128, 1)
            )

        return (
            jnp.where(local < 1, 0.0, both(0, 1)),
            both(0, 73),
            jnp.where(local < 17, both(0, 17), both(1, 17)),
            both(1, 89),
            jnp.where(local < 33, both(1, 33), 0.0),
        )

    for k in range(2):
        x = x_first + k
        edge = ((x == 0) & (index_x == 0)) | ((x == SIDE - 1) & (index_x == last[0]))
        inside_x = jnp.where(edge, 0.0, 1.0)
        found = []
        for r in range(2):
            inside = (inside_low if r == 0 else inside_high) * inside_x
            found.append(
                [
                    node_speeds([sums_at(c, k, r, h) for c in range(8)], code_at(k, r, h), inside)
                    for h in range(2)
                ]
            )
        at = pl.multiple_of(x * 8, 8)
        for c in range(3):
            low, high = (
                tiles(*([found[r][h][f][c] for h in range(2)] for f in range(2)))
                for r in range(2)
            )
            for j in range(5):
                nodes[0, j, c, pl.ds(at, 8), :] = low[j]
                nodes[1, j, c, pl.ds(at, 8), :] = jnp.where(s8 < 2, high[j], low[j])


def middle_kernel(last, order, halves, y_a, y_d, codes, nodes, work, own):
    side_y = low_side("gy")
    for x in range(2, 8):
        own[x - 2] = codes[x]
        for channel in range(8):
            low, high = join(halves, channel, x)
            work[channel, x - 2, 0:8, :] = low
            work[channel, x - 2, 8:16, :] = high
    for recv, high in ((y_a, 1 - side_y), (y_d, side_y)):
        start = pl.multiple_of(high * 8, 8)
        for x in range(2, 8):
            for channel in range(8):
                at = channel * 20 + x * 2
                work[channel, x - 2, pl.ds(start, 2), :] += recv[at : at + 2, :]
            own[x - 2, pl.ds(high * 9, 1), :] = recv[159 + x : 160 + x, :]

    def step(pair, carry):
        x = pair * 2

        def sums_at(c, k, r, h):
            return work[c, x - 2 + k, 8 * r : 8 * r + 8, half(h)]

        def code_at(k, r, h):
            return own[x - 2 + k, 8 * r : 8 * r + 8, half(h)]

        store_nodes(x, sums_at, code_at, last, nodes)
        return carry

    lax.fori_loop(1, 4, step, 0)


def gather_kernel(
    last, tile_ref, middle, edge, edge_codes, x_a, x_d, table, right, deform,
    velocity_out, affine_out, deform_out, stress_out, nodes,
    work, own, partial, new_velocity, new_affine, new_deform, new_stress, sems,
):
    side_x = low_side("gx")
    for recv, high in ((x_a, 1 - side_x), (x_d, side_x)):
        first = high * 2
        for channel in range(8):
            for p in range(2):
                at = channel * 2 + p
                plane = first + p
                work[channel, plane, 0:8, :] = (
                    edge[channel, plane, 0:8, :] + recv[at * 8 : at * 8 + 8, :]
                )
                work[channel, plane, 8:16, :] = edge[channel, plane, 8:16, :]
                work[channel, plane, 8:10, :] += recv[128 + at * 2 : 130 + at * 2, :]
        own[first + high, 0:10, :] = recv[160:170, :]
        own[first + 1 - high] = edge_codes[high]

    def edge_step(high, carry):
        def sums_at(c, k, r, h):
            return work[c, high * 2 + k, 8 * r : 8 * r + 8, half(h)]

        def code_at(k, r, h):
            return own[high * 2 + k, 8 * r : 8 * r + 8, half(h)]

        store_nodes(high * 8, sums_at, code_at, last, nodes)
        return carry

    lax.fori_loop(0, 2, edge_step, 0)

    def one(chunk, slot):
        s = chunk * CHUNK + slot
        tile = tile_ref[0, s]
        tile_x = lax.shift_right_logical(tile, 6)
        tile_y = lax.shift_right_logical(tile, 5) & 1
        tile_z = tile & 31
        j = lax.div(tile_z, 7)
        shift = (tile_z - 7 * j) * 8

        def row(k):
            return table[k, pl.ds(s, 1), :]

        first = pl.multiple_of(tile_x * 32, 32)
        lane = iota((48, LANES), 1) & 63
        left = []
        for c in range(3):
            value = nodes[tile_y, j, c, pl.ds(first, 48), :]
            window = pltpu.roll(value, lax.rem(128 - shift, 128), 1)
            window = jnp.where(lane < 16, window, pltpu.roll(value, lax.rem(144 - shift, 128), 1))
            window = jnp.where(lane < 32, window, pltpu.roll(value, 160 - shift - 128 * (shift <= 32).astype(jnp.int32), 1))
            high = window.astype(BF16).astype(F32)
            left.append(jnp.where(lane < 32, high, window - high).astype(BF16))
        summed = matmul(jnp.concatenate(left, 0), right[s])

        dy = y_coords(tile_y) - row(POS_Y)
        wy = spline(dy)
        pos_x = row(POS_X)
        wxy = [wy * row(WX + x) for x in range(6)]
        place = slice(slot * 8, slot * 8 + 8)
        for c in range(3):
            speed = along_x = along_z = None
            for x in range(5, -1, -1):
                at = (c * 6 + x) * 8
                part = wxy[x] * summed[at : at + 8, 0:LANES]
                moment = wxy[x] * summed[at : at + 8, LANES : 2 * LANES]
                speed = part if speed is None else speed + part
                along_z = moment if along_z is None else along_z + moment
                if x:
                    along_x = speed if along_x is None else along_x + speed
            partial[4 * c, place, :] = speed
            partial[4 * c + 1, place, :] = along_x - pos_x * speed
            partial[4 * c + 2, place, :] = speed * dy
            partial[4 * c + 3, place, :] = along_z

    def collect(k):
        total = partial[k, pl.ds(0, CHUNK, stride=8), :]
        for y in range(1, 8):
            total = total + partial[k, pl.ds(y, CHUNK, stride=8), :]
        return total

    ready = (new_velocity, new_affine, new_deform, new_stress)
    finals = (velocity_out, affine_out, deform_out, stress_out)

    def sends(chunk):
        own_slots = pl.ds(pl.multiple_of(chunk * CHUNK, CHUNK), CHUNK)
        return [
            pltpu.make_async_copy(src.at[:, own_slots], dst.at[:, own_slots], sems.at[chunk, i])
            for i, (src, dst) in enumerate(zip(ready, finals))
        ]

    def step(chunk, carry):
        for slot in range(CHUNK):
            one(chunk, slot)
        own_slots = pl.ds(pl.multiple_of(chunk * CHUNK, CHUNK), CHUNK)
        live = table[LIVE, own_slots, :]
        moved = []
        for c in range(3):
            new_velocity[c, own_slots, :] = collect(4 * c) * live
            for k in range(3):
                value = 4.0 * collect(4 * c + 1 + k) * live
                new_affine[3 * c + k, own_slots, :] = value
                moved.append(value)
        old = [deform[k, own_slots, :] for k in range(9)]
        fresh = []
        for i in range(3):
            for j in range(3):
                value = old[3 * i + j]
                for k in range(3):
                    value = value + DT * moved[3 * i + k] * old[3 * k + j]
                fresh.append(value * live)
        for k in range(9):
            new_deform[k, own_slots, :] = fresh[k]
        stress = kirchhoff(fresh)
        for k, entry in enumerate((0, 4, 8, 1, 2, 5)):
            new_stress[k, own_slots, :] = stress[entry] * live
        for send in sends(chunk):
            send.start()
        return carry

    lax.fori_loop(0, SLOTS // CHUNK, step, 0)
    for chunk in range(SLOTS // CHUNK):
        for send in sends(chunk):
            send.wait()


def vmem(shape, dtype=F32):
    return pltpu.VMEM(shape, dtype)


def cost(flops):
    return pl.CostEstimate(flops=flops, bytes_accessed=4000000, transcendentals=0)


def swap_pairs(block, axis, shift):
    size = lax.axis_size(axis)
    route = [(i, ((i + shift) ^ 1) - shift) for i in range(size)]
    return lax.ppermute(block, axis, [(i, k) for i, k in route if 0 <= k < size])


def per_device(
    offset, particle_mass, velocity, affine, deform,
    particle_cell, body_id, slot_tile_number, block_count, normal_code,
):
    params = pltpu.CompilerParams(vmem_limit_bytes=VMEM_LIMIT)
    smem = pl.BlockSpec(memory_space=pltpu.SMEM)
    hbm = pl.BlockSpec(memory_space=pltpu.HBM)
    whole = pl.BlockSpec(memory_space=pltpu.VMEM)
    face = jax.ShapeDtypeStruct((FACE_ROWS, DEPTH), F32)
    nodes = jax.ShapeDtypeStruct((2, 5, 3, 8 * SIDE, LANES), F32)
    right_shape = jax.ShapeDtypeStruct((SLOTS, LANES, 256), BF16)
    last = (lax.axis_size("gx") - 1, lax.axis_size("gy") - 1)
    inputs = (
        slot_tile_number, offset, particle_mass, velocity, affine, deform, particle_cell,
        body_id, normal_code,
    )

    halves_shape = jax.ShapeDtypeStruct((2, 8, SIDE, 8, DEPTH), F32)
    scatter_scratch = [
        pltpu.SMEM((32,), jnp.int32),
        vmem((2, 192, 256), BF16),
        vmem((2, 192, 256), BF16),
        vmem((2, 2, 2, 280, LANES)),
        vmem((2, 2, 192, DEPTH)),
    ]
    anywhere = pl.BlockSpec(memory_space=pl.ANY)

    halves, y_d, table, rows, codes, tile_numbers = pl.pallas_call(
        first_kernel,
        out_shape=(
            halves_shape,
            face,
            jax.ShapeDtypeStruct((GATHER_ROWS, 32, LANES), F32),
            jax.ShapeDtypeStruct((SCATTER_ROWS - GATHER_ROWS, 32, LANES), F32),
            jax.ShapeDtypeStruct((SIDE, 16, DEPTH), F32),
            jax.ShapeDtypeStruct((1, SLOTS), jnp.int32),
        ),
        in_specs=[smem] + [hbm] * 9,
        out_specs=(whole,) * 5 + (smem,),
        scratch_shapes=[vmem(x.shape, x.dtype) for x in inputs[1:]]
        + scatter_scratch
        + [pltpu.SemaphoreType.DMA((9,))],
        compiler_params=params,
        cost_estimate=cost(3000000),
        name="scatter_first",
    )(
        block_count,
        *(pltpu.with_memory_space_constraint(x, pltpu.HBM) for x in inputs),
    )
    got_y_d = swap_pairs(y_d, "gy", 1)
    halves, y_a = pl.pallas_call(
        second_kernel,
        out_shape=(halves_shape, face),
        in_specs=[smem] + [whole] * 4,
        out_specs=(whole,) * 2,
        scratch_shapes=scatter_scratch,
        input_output_aliases={1: 0},
        compiler_params=params,
        cost_estimate=cost(3000000),
        name="scatter_second",
    )(tile_numbers, halves, table, rows, codes)
    got_y_a = swap_pairs(y_a, "gy", 0)
    right = pl.pallas_call(
        prepare_kernel,
        out_shape=right_shape,
        in_specs=[anywhere, smem, whole],
        out_specs=whole,
        compiler_params=params,
        cost_estimate=cost(3000000),
        name="prepare",
    )(y_a, tile_numbers, table)
    x_a, x_d, edge, edge_codes = pl.pallas_call(
        corner_kernel,
        out_shape=(
            face,
            face,
            jax.ShapeDtypeStruct((8, 4, 16, DEPTH), F32),
            jax.ShapeDtypeStruct((2, 16, DEPTH), F32),
        ),
        in_specs=[pl.BlockSpec(memory_space=pl.ANY)] + [whole] * 4,
        out_specs=(whole,) * 4,
        compiler_params=params,
        name="corners",
    )(right, halves, got_y_a, got_y_d, codes)
    got_x_d = swap_pairs(x_d, "gx", 1)
    got_x_a = swap_pairs(x_a, "gx", 0)
    middle = pl.pallas_call(
        functools.partial(middle_kernel, last),
        out_shape=nodes,
        in_specs=[pl.BlockSpec(memory_space=pl.ANY)] + [whole] * 4,
        out_specs=whole,
        scratch_shapes=[vmem((8, 6, 16, DEPTH)), vmem((6, 16, DEPTH))],
        compiler_params=params,
        cost_estimate=cost(3000000),
        name="middle",
    )(edge_codes, halves, got_y_a, got_y_d, codes)

    slots, particles = particle_mass.shape
    out = pl.pallas_call(
        functools.partial(gather_kernel, last),
        out_shape=tuple(jax.ShapeDtypeStruct((k, slots, particles), F32) for k in (3, 9, 9, 6))
        + (nodes,),
        in_specs=[smem] + [whole] * 8,
        out_specs=(hbm,) * 4 + (whole,),
        scratch_shapes=[
            vmem((8, 4, 16, DEPTH)),
            vmem((4, 16, DEPTH)),
            vmem((12, 8 * CHUNK, LANES)),
        ]
        + [vmem((k, slots, particles)) for k in (3, 9, 9, 6)]
        + [pltpu.SemaphoreType.DMA((SLOTS // CHUNK, 4))],
        input_output_aliases={1: 4},
        compiler_params=params,
        name="gather",
    )(
        tile_numbers, middle, edge, edge_codes, got_x_a, got_x_d, table, right, deform,
    )
    return out[:4]


def solution(mesh):
    both = ("gx", "gy")
    field = P(None, both, None)
    flat = P(both, None)
    return jax.shard_map(
        per_device,
        mesh=mesh,
        in_specs=(
            field, flat, field, field, field, flat, flat, P(both), P("gx", "gy"),
            P("gx", "gy", None),
        ),
        out_specs=(field,) * 4,
        check_vma=False,
    )
```

time: 35.4 us -> 35.1 us (level)
  Pallas kernels: 14.2 us -> 12.3 us
  waiting for transfers between devices: 10.8 us -> 12.6 us
    ppermute x4, waiting for transfers between devices: 10.8 us -> 12.6 us  [swap_pairs(): lax.ppermute(block, axis, [(i, k) for i, k in route if 0 <= k < size])]
    pallas_call x1, Pallas kernels: 5.59 us -> 4.05 us  [per_device(): pl.pallas_call(functools.partial(gather_kernel, last), out_shape=tuple((j...]
    pallas_call x3 -> x4, Pallas kernels: 8.39 us -> 8.1 us  [the longest x1 3.83 us: per_device(): pl.pallas_call(first_kernel, out_shape=(halves_shape, face, jax.ShapeDtyp...]
  transfers between devices with their start and end apart: 4 -> 4, of which waited for: 2 -> 2; matrix products, arithmetic and copies ran while one was open for 0% -> 0% of each run, Pallas kernels for 9% -> 5%
where the time goes in v3:
time: 35.1 us; the launch traced here: 35 us
  waiting for transfers between devices  12.6 us (36%)
  Pallas kernels  12.3 us (35%)
  starting transfers between devices  8.65 us (25%)
  between operations  1.35 us (4%)
    ppermute x4, waiting for transfers between devices, swap_pairs(): lax.ppermute(block, axis, [(i, k) for i, k in route if 0 <= k < size])  12.6 us
    ppermute x4, starting transfers between devices, swap_pairs(): lax.ppermute(block, axis, [(i, k) for i, k in route if 0 <= k < size])  8.65 us
    pallas_call x1, Pallas kernels, per_device(): pl.pallas_call(functools.partial(gather_kernel, last), out_shape=tuple((j...  4.05 us
    pallas_call x1, Pallas kernels, per_device(): pl.pallas_call(first_kernel, out_shape=(halves_shape, face, jax.ShapeDtyp...  3.83 us
    pallas_call x1, Pallas kernels, per_device(): pl.pallas_call(second_kernel, out_shape=(halves_shape, face), in_specs=[s...  2.48 us
    pallas_call x1, Pallas kernels, per_device(): pl.pallas_call(functools.partial(middle_kernel, last), out_shape=nodes, i...  0.97 us
    pallas_call x1, Pallas kernels, per_device(): pl.pallas_call(prepare_kernel, out_shape=right_shape, in_specs=[anywhere,...  0.83 us
  transfers between devices with their start and end apart: 4, of which 2 were waited for; matrix products, arithmetic and copies ran while one was open for 0% of the time, Pallas kernels for 5%

profile of v3, /device:TPU:101, one launch (start us, length us, event | category | flops | bytes accessed | tf_op | source)
XLA Modules:
  0.0 35.0 jit_solution(1144464041308328962)
XLA Ops:
  1.3 3.8 %scatter_first.1 = (f32[2,8,10,8,256]{4,3,2,1,0:T(8,128)S(1)}, f32[176,256]{1,0:T(8,128)S(1)}, f32[12,32,128]{2,1,0:T(8,128)S(1)}, f32[13,32,128]{2,1,0:T(8,128)...) custom-call(s32[1,1]{1,0:T(1,128)S(6)} %copy.18.count_ref, s32[24]{0:T(128)} %tile_in.1, f32[3,24,128]{2,1,0:T(8,128)} %offset_in.1, ...), custom_call_target="tpu_custom_call" | custom-call | flops 3000000 | bytes 4000000 | tf_op jit(solution)/shard_map/scatter_first/pallas_call | solution.py:588
  5.1 2.5 %scatter_second.1 = (f32[2,8,10,8,256]{4,3,2,1,0:T(8,128)S(1)}, f32[176,256]{1,0:T(8,128)S(1)}) custom-call(s32[1,24]{1,0:T(1,128)S(1)} %get-tuple-element.20.tile_ref, f32[2,8,10,8,256]{4,3,2,1,0:T(8,128)S(1)} %get-tuple-element.21.half_in, f32[12,32,128]{2,1,0:T(8,128)S(1)} %get-tuple-element.22.table, ...), custom_call_target="tpu_custom_call", output_to_operand_aliasing={{0}: (1, {})} | custom-call | flops 3000000 | bytes 4000000 | tf_op jit(solution)/shard_map/scatter_second/pallas_call | solution.py:611
  7.6 1.7 %collective-permute-start = (f32[176,256]{1,0:T(8,128)S(1)}, f32[176,256]{1,0:T(8,128)S(1)}, u32[]{:S(2)}, u32[]{:S(2)}) collective-permute-start(f32[176,256]{1,0:T(8,128)S(1)} %get-tuple-element.25.order), channel_id=1, source_target_pairs={{0,1},{1,0},{2,3},{3,2},{4,5},{5,4},{6,7},{7,6},{8,9},{9,8},{10,11... | collective-permute-start | bytes 540680 | tf_op jit(solution)/shard_map/ppermute | solution.py:558
  9.2 3.5 %collective-permute-start.1 = (f32[176,256]{1,0:T(8,128)S(1)}, f32[176,256]{1,0:T(8,128)S(1)}, u32[]{:S(2)}, u32[]{:S(2)}) collective-permute-start(f32[176,256]{1,0:T(8,128)S(1)} %get-tuple-element.27), channel_id=1, source_target_pairs={{1,2},{2,1},{3,4},{4,3},{5,6},{6,5},{9,10},{10,9},{11,12},{12,11},... | collective-permute-start | bytes 540680 | tf_op jit(solution)/shard_map/ppermute | solution.py:558
  12.7 0.8 %prepare.1.order.right = bf16[24,128,256]{2,1,0:T(8,128)(2,1)S(1)} custom-call(f32[176,256]{1,0:T(8,128)S(1)} %get-tuple-element.25.order, s32[1,24]{1,0:T(1,128)S(1)} %get-tuple-element.20.tile_ref, f32[12,32,128]{2,1,0:T(8,128)S(1)} %get-tuple-element.22.table), custom_call_target="tpu_custom_call" | custom-call | flops 3000000 | bytes 4000000 | tf_op jit(solution)/shard_map/prepare/pallas_call | solution.py:623
  13.6 0.0 collective-permute-done.recv_a.y_a
  13.6 6.6 %collective-permute-done.1.recv_d.y_d = f32[176,256]{1,0:T(8,128)S(1)} collective-permute-done((f32[176,256]{1,0:T(8,128)S(1)}, f32[176,256]{1,0:T(8,128)S(1)}, u32[]{:S(2)}, u32[]{:S(2)}) %collective-permute-start.1) | collective-permute-done | bytes 180256 | tf_op jit(solution)/shard_map/ppermute | solution.py:558
  20.2 0.2 corners.1
  20.4 1.6 %collective-permute-start.2 = (f32[176,256]{1,0:T(8,128)S(1)}, f32[176,256]{1,0:T(8,128)S(1)}, u32[]{:S(2)}, u32[]{:S(2)}) collective-permute-start(f32[176,256]{1,0:T(8,128)S(1)} %get-tuple-element.30), channel_id=1, source_target_pairs={{0,8},{8,0},{16,24},{24,16},{32,40},{40,32},{48,56},{56,48},{64,72... | collective-permute-start | bytes 540680 | tf_op jit(solution)/shard_map/ppermute | solution.py:558
  22.0 1.9 %collective-permute-start.3 = (f32[176,256]{1,0:T(8,128)S(1)}, f32[176,256]{1,0:T(8,128)S(1)}, u32[]{:S(2)}, u32[]{:S(2)}) collective-permute-start(f32[176,256]{1,0:T(8,128)S(1)} %get-tuple-element.31), channel_id=1, source_target_pairs={{8,16},{16,8},{24,32},{32,24},{40,48},{48,40},{56,64},{64,56},{72,... | collective-permute-start | bytes 540680 | tf_op jit(solution)/shard_map/ppermute | solution.py:558
  23.9 0.0 copy-start
  23.9 1.0 %middle.1 = f32[2,5,3,80,128]{4,3,2,1,0:T(8,128)S(1)} custom-call(f32[2,16,256]{2,1,0:T(8,128)S(1)} %get-tuple-element.28.order.edge_codes, f32[2,8,10,8,256]{4,3,2,1,0:T(8,128)S(1)} %get-tuple-element.26.halves, f32[176,256]{1,0:T(8,128)S(1)} %collective-permute-done.recv_a.y_a, f32[176,256]{1,0:T(8,128)S(1)} %collective-permute-done.1.recv_d.y_d, ...), custom_call_target="tpu_custom_call" | custom-call | flops 3000000 | bytes 4000000 | tf_op jit(solution)/shard_map/middle/pallas_call | solution.py:647
  24.9 0.0 collective-permute-done.2.x_a
  24.9 6.0 %collective-permute-done.3.x_d = f32[176,256]{1,0:T(8,128)S(1)} collective-permute-done((f32[176,256]{1,0:T(8,128)S(1)}, f32[176,256]{1,0:T(8,128)S(1)}, u32[]{:S(2)}, u32[]{:S(2)}) %collective-permute-start.3) | collective-permute-done | bytes 180256 | tf_op jit(solution)/shard_map/ppermute | solution.py:558
  30.9 0.0 copy-done
  30.9 4.0 %gather.1 = (f32[3,24,128]{2,1,0:T(8,128)}, f32[9,24,128]{2,1,0:T(8,128)}, f32[9,24,128]{2,1,0:T(8,128)}, f32[6,24,128]{2,1,0:T(8,128)}, f32[2,5,3,80,128]{4,3,2,1,0:T(8,128)S(1)}) custom-call(s32[1,24]{1,0:T(1,128)S(1)} %get-tuple-element.20.tile_ref, f32[2,5,3,80,128]{4,3,2,1,0:T(8,128)S(1)} %middle.1, ...), custom_call_target="tpu_custom_call", output_to_operand_aliasing={{4}: (1, {})} | custom-call | tf_op jit(solution)/shard_map/gather/pallas_call | solution.py:659
Async XLA Ops:
  7.6 6.0 %collective-permute-start = (f32[176,256]{1,0:T(8,128)S(1)}, f32[176,256]{1,0:T(8,128)S(1)}, u32[]{:S(2)}, u32[]{:S(2)}) collective-permute-start(f32[176,256]{1,0:T(8,128)S(1)} %get-tuple-element.25.order), channel_id=1, source_target_pairs={{0,1},{1,0},{2,3},{3,2},{4,5},{5,4},{6,7},{7,6},{8,9},{9,8},{10,11... | collective-permute-start | bytes 540680 | tf_op jit(solution)/shard_map/ppermute | solution.py:558
  9.2 10.9 %collective-permute-start.1 = (f32[176,256]{1,0:T(8,128)S(1)}, f32[176,256]{1,0:T(8,128)S(1)}, u32[]{:S(2)}, u32[]{:S(2)}) collective-permute-start(f32[176,256]{1,0:T(8,128)S(1)} %get-tuple-element.27), channel_id=1, source_target_pairs={{1,2},{2,1},{3,4},{4,3},{5,6},{6,5},{9,10},{10,9},{11,12},{12,11},... | collective-permute-start | bytes 540680 | tf_op jit(solution)/shard_map/ppermute | solution.py:558
  20.4 4.5 %collective-permute-start.2 = (f32[176,256]{1,0:T(8,128)S(1)}, f32[176,256]{1,0:T(8,128)S(1)}, u32[]{:S(2)}, u32[]{:S(2)}) collective-permute-start(f32[176,256]{1,0:T(8,128)S(1)} %get-tuple-element.30), channel_id=1, source_target_pairs={{0,8},{8,0},{16,24},{24,16},{32,40},{40,32},{48,56},{56,48},{64,72... | collective-permute-start | bytes 540680 | tf_op jit(solution)/shard_map/ppermute | solution.py:558
  22.0 8.9 %collective-permute-start.3 = (f32[176,256]{1,0:T(8,128)S(1)}, f32[176,256]{1,0:T(8,128)S(1)}, u32[]{:S(2)}, u32[]{:S(2)}) collective-permute-start(f32[176,256]{1,0:T(8,128)S(1)} %get-tuple-element.31), channel_id=1, source_target_pairs={{8,16},{16,8},{24,32},{32,24},{40,48},{48,40},{56,64},{64,56},{72,... | collective-permute-start | bytes 540680 | tf_op jit(solution)/shard_map/ppermute | solution.py:558
  23.9 7.0 %copy-start = (f32[9,24,128]{2,1,0:T(8,128)S(1)}, f32[9,24,128]{2,1,0:T(8,128)}, u32[]{:S(2)}) copy-start(f32[9,24,128]{2,1,0:T(8,128)} %deform.1) | copy-start | bytes 331780

commit v4 on v3

--- a/solution.py
+++ b/solution.py
@@ -22,7 +22,8 @@
 DEPTH = 256
 SLOTS = 24
 LANES = 128
-FACE_ROWS = 176
+FACE_ROWS = 184
+CHANNELS = 9
 CHUNK = 8
 
 POS_Y, POS_Z, FIELD0, FIELD1, POS_X, LIVE, WX = 0, 1, 2, 3, 4, 5, 6
@@ -90,10 +91,10 @@
     return slice(h * LANES, (h + 1) * LANES)
 
 
-def matching_slots(order, tile_ref, tile_y):
+def matching_slots(order, tile_ref, tile_x):
     def body(s, n):
         order[n] = s
-        return n + ((lax.shift_right_logical(tile_ref[0, s], 5) & 1) == tile_y).astype(jnp.int32)
+        return n + (lax.shift_right_logical(tile_ref[0, s], 6) == tile_x).astype(jnp.int32)
 
     n = lax.fori_loop(0, SLOTS, body, 0)
     order[n] = SLOTS
@@ -108,14 +109,14 @@
         left_lo[u, 0:48, LANES : 2 * LANES] = zeros
 
 
-def scatter_half(tile_y, tile_ref, table, rows, codes, halves, face, order, left_hi, left_lo,
+def scatter_half(tile_x, tile_ref, table, rows, halves, face, order, left_hi, left_lo,
                  acc, turned):
-    count = matching_slots(order, tile_ref, tile_y)
+    count = matching_slots(order, tile_ref, tile_x)
 
     def one(index, u):
         s = order[index]
         tile = tile_ref[0, jnp.minimum(s, SLOTS - 1)]
-        tile_x = lax.shift_right_logical(tile, 6)
+        tile_y = lax.shift_right_logical(tile, 5) & 1
         tile_z = tile & 31
 
         def row(k):
@@ -160,8 +161,8 @@
         total = both[0:32] + both[32:64] + rest
         window = pl.ds(tile_z * 8 + 7, 16)
         for f in range(2):
-            acc[tile_x, f, 0, window, :] += total[16 * f : 16 * f + 16, 0:LANES]
-            acc[tile_x, f, 1, window, 0:64] += total[16 * f : 16 * f + 16, LANES:192]
+            acc[tile_y, f, 0, window, :] += total[16 * f : 16 * f + 16, 0:LANES]
+            acc[tile_y, f, 1, window, 0:64] += total[16 * f : 16 * f + 16, LANES:192]
 
     def step(pair, carry):
         one(pair * 2, 0)
@@ -170,35 +171,35 @@
 
     lax.fori_loop(0, lax.shift_right_logical(count + 1, 1), step, 0)
 
-    for tx in range(2):
+    for ty in range(2):
         for f in range(2):
             for h in range(2):
                 z = slice(8 + LANES * h, 8 + LANES * (h + 1))
-                turned[tx, f, 0:128, half(h)] = acc[tx, f, 0, z, :].T
-                turned[tx, f, 128:192, half(h)] = acc[tx, f, 1, z, :].T[0:64]
-
+                turned[ty, f, 0:128, half(h)] = acc[ty, f, 0, z, :].T
+                turned[ty, f, 128:192, half(h)] = acc[ty, f, 1, z, :].T[0:64]
+
+    upper = iota((8, DEPTH), 0) >= 4
     for f in range(2):
         for c in range(4):
-            for x in range(SIDE):
-                parts = [
-                    turned[tx, f, (c * 6 + x - 4 * tx) * 8 : (c * 6 + x - 4 * tx) * 8 + 8, :]
-                    for tx in range(2)
-                    if 0 <= x - 4 * tx < 6
-                ]
-                total = sum(parts[1:], parts[0])
-                channel = 4 * f + c
-                halves[tile_y, channel, x, :, :] = total
-                at = channel * 20 + x * 2
-                face[at : at + 2, :] = total[0:2]
-    for x in range(8):
-        face[160 + x : 161 + x, :] = codes[x + 1, pl.ds(1 + tile_y * 7, 1), :]
-    face[168:176, :] = jnp.zeros((8, DEPTH), F32)
+            for x in range(6):
+                at = (c * 6 + x) * 8
+                high = turned[1, f, at : at + 8, :]
+                halves[tile_x, 4 * f + c, x, 0:8, :] = turned[
+                    0, f, at : at + 8, :
+                ] + jnp.where(upper, high, 0.0)
+                halves[tile_x, 4 * f + c, x, 8:16, :] = high
+    for c in range(CHANNELS):
+        for p in range(2):
+            at = c * 2 + p
+            face[at * 8 : at * 8 + 8, :] = halves[tile_x, c, 4 * tile_x + p, 0:8, :]
+            face[144 + at * 2 : 146 + at * 2, :] = halves[tile_x, c, 4 * tile_x + p, 8:10, :]
+    face[180:184, :] = jnp.zeros((4, DEPTH), F32)
 
 
 def first_kernel(
     count_ref, tile_in, offset_in, mass_in, velocity_in, affine_in, deform_in, cell_in, body_in,
     code_in,
-    halves, face, table, rows, codes, tile_ref,
+    halves, face, table, rows, tile_ref,
     offset, mass, velocity, affine, deform, cell, body, code,
     order, left_hi, left_lo, acc, turned, sems,
 ):
@@ -213,15 +214,16 @@
     for copy in copies:
         copy.start()
     clear(left_hi, left_lo, acc)
-    codes[...] = jnp.zeros_like(codes)
+    halves[:, 8] = jnp.zeros((2, 6, 16, DEPTH), F32)
     for out in (table, rows):
         for k in range(out.shape[0]):
             out[k, SLOTS:32, :] = jnp.zeros((32 - SLOTS, LANES), F32)
     for copy in copies:
         copy.wait()
 
-    for x in range(8):
-        codes[x + 1, 1:9, :] = code[x].astype(F32)
+    for x in range(1, 9):
+        half_x = 0 if x < 6 else 1
+        halves[half_x, 8, x - 4 * half_x, 1:9, :] = code[x - 1].astype(F32)
     live = (iota((SLOTS, LANES), 0) < count_ref[0, 0]).astype(F32)
     cell = cell[...]
     field_one = (body[...] & 1).astype(F32)
@@ -243,24 +245,18 @@
     for k in range(9):
         rows[AFF - MASS + k, own] = weighted * (affine[k] - 4.0 * DT * stress[k])
     scatter_half(
-        low_side("gy"), tile_ref, table, rows, codes, halves, face, order, left_hi, left_lo,
-        acc, turned,
+        low_side("gx"), tile_ref, table, rows, halves, face, order, left_hi, left_lo, acc, turned,
     )
 
 
 def second_kernel(
-    tile_ref, half_in, table, rows, codes, halves, face, order, left_hi, left_lo, acc, turned,
+    tile_ref, half_in, table, rows, halves, face, order, left_hi, left_lo, acc, turned,
 ):
     clear(left_hi, left_lo, acc)
     scatter_half(
-        1 - low_side("gy"), tile_ref, table, rows, codes, halves, face, order, left_hi, left_lo,
+        1 - low_side("gx"), tile_ref, table, rows, halves, face, order, left_hi, left_lo,
         acc, turned,
     )
-
-
-def join(halves, channel, x):
-    low, high = halves[0, channel, x], halves[1, channel, x]
-    return low + jnp.where(iota((8, DEPTH), 0) >= 4, high, 0.0), high
 
 
 def prepare_kernel(order, tile_ref, table, right):
@@ -280,34 +276,41 @@
     lax.fori_loop(0, SLOTS, one, 0, unroll=2)
 
 
-def corner_kernel(order, halves, recv_a, recv_d, codes, face_a, face_d, edge, edge_codes):
+def plane(halves, edge, c, x, rows):
+    if x < 2:
+        return edge[c, x, rows, :]
+    if x >= 8:
+        return edge[c, x - 6, rows, :]
+    if x < 4:
+        return halves[0, c, x, rows, :]
+    if x >= 6:
+        return halves[1, c, x - 4, rows, :]
+    return halves[0, c, x, rows, :] + halves[1, c, x - 4, rows, :]
+
+
+def y_face_row(c, x):
+    return c * 16 + x * 2 if x < 8 else 144 + c * 4 + (x - 8) * 2
+
+
+def corner_kernel(order, halves, recv_a, recv_d, face_a, face_d, edge):
     side_y = low_side("gy")
     side_x = low_side("gx")
-    for plane in range(4):
-        x = plane if plane < 2 else plane + 6
-        for channel in range(8):
-            edge[channel, plane, 0:8, :], edge[channel, plane, 8:16, :] = join(halves, channel, x)
-    for recv, start in ((recv_a, (1 - side_y) * 8), (recv_d, side_y * 8)):
-        start = pl.multiple_of(start, 8)
-        for channel in range(8):
-            for plane in range(4):
-                x = plane if plane < 2 else plane + 6
-                at = channel * 20 + x * 2
-                edge[channel, plane, pl.ds(start, 2), :] += recv[at : at + 2, :]
-    edge_codes[0] = codes[1]
-    edge_codes[1] = codes[8]
-    for recv, halo in ((recv_a, (1 - side_y) * 9), (recv_d, side_y * 9)):
-        edge_codes[0, pl.ds(halo, 1), :] = recv[160:161, :]
-        edge_codes[1, pl.ds(halo, 1), :] = recv[167:168, :]
-    for face, high in ((face_a, 1 - side_x), (face_d, side_x)):
-        first = high * 2
-        for channel in range(8):
+    for recv, high in ((recv_a, 1 - side_x), (recv_d, side_x)):
+        for c in range(CHANNELS):
             for p in range(2):
-                at = channel * 2 + p
-                face[at * 8 : at * 8 + 8, :] = edge[channel, first + p, 0:8, :]
-                face[128 + at * 2 : 130 + at * 2, :] = edge[channel, first + p, 8:10, :]
-        face[160:170, :] = edge_codes[high, 0:10, :]
-        face[170:176, :] = jnp.zeros((6, DEPTH), F32)
+                at = c * 2 + p
+                own = (high, c, 4 * high + p)
+                to = (c, 2 * high + p)
+                edge[(*to, slice(0, 8))] = halves[(*own, slice(0, 8))] + recv[at * 8 : at * 8 + 8]
+                edge[(*to, slice(8, 16))] = halves[(*own, slice(8, 16))]
+                edge[(*to, slice(8, 10))] += recv[144 + at * 2 : 146 + at * 2]
+    for face, high in ((face_a, 1 - side_y), (face_d, side_y)):
+        rows = pl.ds(pl.multiple_of(high * 8, 8), 2)
+        for c in range(CHANNELS):
+            for x in range(SIDE):
+                at = y_face_row(c, x)
+                face[at : at + 2, :] = plane(halves, edge, c, x, rows)
+        face[180:184, :] = jnp.zeros((4, DEPTH), F32)
 
 
 def node_speeds(sums, code, inside):
@@ -339,115 +342,78 @@
     return v0, v1
 
 
-def store_nodes(x_first, sums_at, code_at, last, nodes):
-    index_x = lax.axis_index("gx")
-    index_y = lax.axis_index("gy")
-    s8 = iota((8, LANES), 0)
-    lane = iota((8, LANES), 1)
-    inside_low = jnp.where((s8 == 0) & (index_y == 0), 0.0, 1.0)
-    inside_high = jnp.where((s8 == 1) & (index_y == last[1]), 0.0, 1.0)
+def tiles(v0, v1):
+    lane = iota(v0[0].shape, 1)
     local = lane & 63
 
-    def tiles(v0, v1):
-        def both(h, shift):
-            return jnp.where(
-                lane < 64, pltpu.roll(v0[h], shift, 1), pltpu.roll(v1[h], (shift + 64) % 128, 1)
-            )
-
-        return (
-            jnp.where(local < 1, 0.0, both(0, 1)),
-            both(0, 73),
-            jnp.where(local < 17, both(0, 17), both(1, 17)),
-            both(1, 89),
-            jnp.where(local < 33, both(1, 33), 0.0),
+    def both(h, shift):
+        return jnp.where(
+            lane < 64, pltpu.roll(v0[h], shift, 1), pltpu.roll(v1[h], (shift + 64) % 128, 1)
         )
 
-    for k in range(2):
-        x = x_first + k
-        edge = ((x == 0) & (index_x == 0)) | ((x == SIDE - 1) & (index_x == last[0]))
-        inside_x = jnp.where(edge, 0.0, 1.0)
-        found = []
-        for r in range(2):
-            inside = (inside_low if r == 0 else inside_high) * inside_x
-            found.append(
-                [
-                    node_speeds([sums_at(c, k, r, h) for c in range(8)], code_at(k, r, h), inside)
-                    for h in range(2)
-                ]
-            )
+    return (
+        jnp.where(local < 1, 0.0, both(0, 1)),
+        both(0, 73),
+        jnp.where(local < 17, both(0, 17), both(1, 17)),
+        both(1, 89),
+        jnp.where(local < 33, both(1, 33), 0.0),
+    )
+
+
+def inside_x(x, last):
+    index = lax.axis_index("gx")
+    return jnp.where(((x == 0) & (index == 0)) | ((x == SIDE - 1) & (index == last[0])), 0.0, 1.0)
+
+
+def middle_kernel(last, order, halves, edge, nodes, work):
+    for c in range(CHANNELS):
+        for x in range(SIDE):
+            work[c, x] = plane(halves, edge, c, x, slice(0, 8))
+
+    def step(x, carry):
+        inside = inside_x(x, last)
+        found = [
+            node_speeds([work[c, x, :, half(h)] for c in range(8)], work[8, x, :, half(h)], inside)
+            for h in range(2)
+        ]
         at = pl.multiple_of(x * 8, 8)
         for c in range(3):
-            low, high = (
-                tiles(*([found[r][h][f][c] for h in range(2)] for f in range(2)))
-                for r in range(2)
-            )
+            ready = tiles(*([found[h][f][c] for h in range(2)] for f in range(2)))
             for j in range(5):
-                nodes[0, j, c, pl.ds(at, 8), :] = low[j]
-                nodes[1, j, c, pl.ds(at, 8), :] = jnp.where(s8 < 2, high[j], low[j])
-
-
-def middle_kernel(last, order, halves, y_a, y_d, codes, nodes, work, own):
+                for ty in range(2):
+                    nodes[ty, j, c, pl.ds(at, 8), :] = ready[j]
+        return carry
+
+    lax.fori_loop(0, SIDE, step, 0, unroll=2)
+
+
+def gather_kernel(
+    last, tile_ref, middle, own_a, own_d, y_a, y_d, table, right, deform,
+    velocity_out, affine_out, deform_out, stress_out, nodes,
+    partial, new_velocity, new_affine, new_deform, new_stress, sems,
+):
     side_y = low_side("gy")
-    for x in range(2, 8):
-        own[x - 2] = codes[x]
-        for channel in range(8):
-            low, high = join(halves, channel, x)
-            work[channel, x - 2, 0:8, :] = low
-            work[channel, x - 2, 8:16, :] = high
-    for recv, high in ((y_a, 1 - side_y), (y_d, side_y)):
-        start = pl.multiple_of(high * 8, 8)
-        for x in range(2, 8):
-            for channel in range(8):
-                at = channel * 20 + x * 2
-                work[channel, x - 2, pl.ds(start, 2), :] += recv[at : at + 2, :]
-            own[x - 2, pl.ds(high * 9, 1), :] = recv[159 + x : 160 + x, :]
-
-    def step(pair, carry):
-        x = pair * 2
-
-        def sums_at(c, k, r, h):
-            return work[c, x - 2 + k, 8 * r : 8 * r + 8, half(h)]
-
-        def code_at(k, r, h):
-            return own[x - 2 + k, 8 * r : 8 * r + 8, half(h)]
-
-        store_nodes(x, sums_at, code_at, last, nodes)
-        return carry
-
-    lax.fori_loop(1, 4, step, 0)
-
-
-def gather_kernel(
-    last, tile_ref, middle, edge, edge_codes, x_a, x_d, table, right, deform,
-    velocity_out, affine_out, deform_out, stress_out, nodes,
-    work, own, partial, new_velocity, new_affine, new_deform, new_stress, sems,
-):
-    side_x = low_side("gx")
-    for recv, high in ((x_a, 1 - side_x), (x_d, side_x)):
-        first = high * 2
-        for channel in range(8):
-            for p in range(2):
-                at = channel * 2 + p
-                plane = first + p
-                work[channel, plane, 0:8, :] = (
-                    edge[channel, plane, 0:8, :] + recv[at * 8 : at * 8 + 8, :]
-                )
-                work[channel, plane, 8:16, :] = edge[channel, plane, 8:16, :]
-                work[channel, plane, 8:10, :] += recv[128 + at * 2 : 130 + at * 2, :]
-        own[first + high, 0:10, :] = recv[160:170, :]
-        own[first + 1 - high] = edge_codes[high]
-
-    def edge_step(high, carry):
-        def sums_at(c, k, r, h):
-            return work[c, high * 2 + k, 8 * r : 8 * r + 8, half(h)]
-
-        def code_at(k, r, h):
-            return own[high * 2 + k, 8 * r : 8 * r + 8, half(h)]
-
-        store_nodes(high * 8, sums_at, code_at, last, nodes)
-        return carry
-
-    lax.fori_loop(0, 2, edge_step, 0)
+    index_y = lax.axis_index("gy")
+    for own, recv, high in ((own_a, y_a, 1 - side_y), (own_d, y_d, side_y)):
+        edge_y = jnp.where(high == 0, (index_y == 0), (index_y == last[1]))
+        for first, count in ((0, 8), (8, 2)):
+            row = iota((2 * count, LANES), 0)
+            inside = inside_x(lax.shift_right_logical(row, 1) + first, last)
+            inside = jnp.where(((row & 1) == high) & edge_y, 0.0, inside)
+            found = []
+            for h in range(2):
+                sums = []
+                for c in range(CHANNELS):
+                    at = y_face_row(c, first)
+                    rows = slice(at, at + 2 * count)
+                    sums.append(own[rows, half(h)] + recv[rows, half(h)])
+                found.append(node_speeds(sums[:8], sums[8], inside))
+            for c in range(3):
+                ready = tiles(*([found[h][f][c] for h in range(2)] for f in range(2)))
+                for j in range(5):
+                    for x in range(count):
+                        at = (first + x) * 8
+                        nodes[high, j, c, at : at + 2, :] = ready[j][2 * x : 2 * x + 2]
 
     def one(chunk, slot):
         s = chunk * CHUNK + slot
@@ -575,7 +541,7 @@
         body_id, normal_code,
     )
 
-    halves_shape = jax.ShapeDtypeStruct((2, 8, SIDE, 8, DEPTH), F32)
+    halves_shape = jax.ShapeDtypeStruct((2, CHANNELS, 6, 16, DEPTH), F32)
     scatter_scratch = [
         pltpu.SMEM((32,), jnp.int32),
         vmem((2, 192, 256), BF16),
@@ -585,18 +551,17 @@
     ]
     anywhere = pl.BlockSpec(memory_space=pl.ANY)
 
-    halves, y_d, table, rows, codes, tile_numbers = pl.pallas_call(
+    halves, x_d, table, rows, tile_numbers = pl.pallas_call(
         first_kernel,
         out_shape=(
             halves_shape,
             face,
             jax.ShapeDtypeStruct((GATHER_ROWS, 32, LANES), F32),
             jax.ShapeDtypeStruct((SCATTER_ROWS - GATHER_ROWS, 32, LANES), F32),
-            jax.ShapeDtypeStruct((SIDE, 16, DEPTH), F32),
             jax.ShapeDtypeStruct((1, SLOTS), jnp.int32),
         ),
         in_specs=[smem] + [hbm] * 9,
-        out_specs=(whole,) * 5 + (smem,),
+        out_specs=(whole,) * 4 + (smem,),
         scratch_shapes=[vmem(x.shape, x.dtype) for x in inputs[1:]]
         + scatter_scratch
         + [pltpu.SemaphoreType.DMA((9,))],
@@ -607,19 +572,19 @@
         block_count,
         *(pltpu.with_memory_space_constraint(x, pltpu.HBM) for x in inputs),
     )
-    got_y_d = swap_pairs(y_d, "gy", 1)
-    halves, y_a = pl.pallas_call(
+    got_x_d = swap_pairs(x_d, "gx", 1)
+    halves, x_a = pl.pallas_call(
         second_kernel,
         out_shape=(halves_shape, face),
-        in_specs=[smem] + [whole] * 4,
+        in_specs=[smem] + [whole] * 3,
         out_specs=(whole,) * 2,
         scratch_shapes=scatter_scratch,
         input_output_aliases={1: 0},
         compiler_params=params,
         cost_estimate=cost(3000000),
         name="scatter_second",
-    )(tile_numbers, halves, table, rows, codes)
-    got_y_a = swap_pairs(y_a, "gy", 0)
+    )(tile_numbers, halves, table, rows)
+    got_x_a = swap_pairs(x_a, "gx", 0)
     right = pl.pallas_call(
         prepare_kernel,
         out_shape=right_shape,
@@ -628,32 +593,27 @@
         compiler_params=params,
         cost_estimate=cost(3000000),
         name="prepare",
-    )(y_a, tile_numbers, table)
-    x_a, x_d, edge, edge_codes = pl.pallas_call(
+    )(x_a, tile_numbers, table)
+    y_a, y_d, edge = pl.pallas_call(
         corner_kernel,
-        out_shape=(
-            face,
-            face,
-            jax.ShapeDtypeStruct((8, 4, 16, DEPTH), F32),
-            jax.ShapeDtypeStruct((2, 16, DEPTH), F32),
-        ),
-        in_specs=[pl.BlockSpec(memory_space=pl.ANY)] + [whole] * 4,
-        out_specs=(whole,) * 4,
+        out_shape=(face, face, jax.ShapeDtypeStruct((CHANNELS, 4, 16, DEPTH), F32)),
+        in_specs=[anywhere] + [whole] * 3,
+        out_specs=(whole,) * 3,
         compiler_params=params,
         name="corners",
-    )(right, halves, got_y_a, got_y_d, codes)
-    got_x_d = swap_pairs(x_d, "gx", 1)
-    got_x_a = swap_pairs(x_a, "gx", 0)
+    )(right, halves, got_x_a, got_x_d)
+    got_y_d = swap_pairs(y_d, "gy", 1)
+    got_y_a = swap_pairs(y_a, "gy", 0)
     middle = pl.pallas_call(
         functools.partial(middle_kernel, last),
         out_shape=nodes,
-        in_specs=[pl.BlockSpec(memory_space=pl.ANY)] + [whole] * 4,
+        in_specs=[anywhere] + [whole] * 2,
         out_specs=whole,
-        scratch_shapes=[vmem((8, 6, 16, DEPTH)), vmem((6, 16, DEPTH))],
+        scratch_shapes=[vmem((CHANNELS, SIDE, 8, DEPTH))],
         compiler_params=params,
         cost_estimate=cost(3000000),
         name="middle",
-    )(edge_codes, halves, got_y_a, got_y_d, codes)
+    )(y_a, halves, edge)
 
     slots, particles = particle_mass.shape
     out = pl.pallas_call(
@@ -662,18 +622,14 @@
         + (nodes,),
         in_specs=[smem] + [whole] * 8,
         out_specs=(hbm,) * 4 + (whole,),
-        scratch_shapes=[
-            vmem((8, 4, 16, DEPTH)),
-            vmem((4, 16, DEPTH)),
-            vmem((12, 8 * CHUNK, LANES)),
-        ]
+        scratch_shapes=[vmem((12, 8 * CHUNK, LANES))]
         + [vmem((k, slots, particles)) for k in (3, 9, 9, 6)]
         + [pltpu.SemaphoreType.DMA((SLOTS // CHUNK, 4))],
         input_output_aliases={1: 4},
         compiler_params=params,
         name="gather",
     )(
-        tile_numbers, middle, edge, edge_codes, got_x_a, got_x_d, table, right, deform,
+        tile_numbers, middle, y_a, y_d, got_y_a, got_y_d, table, right, deform,
     )
     return out[:4]
 

time: 35.1 us -> 32.9 us (0.937)
  the two profiles are of different devices: /device:TPU:101 before, /device:TPU:6 now
where the time goes in v4:
time: 32.9 us; the launch traced here: 32.7 us
  Pallas kernels  12.1 us (37%)
  starting transfers between devices  11.9 us (36%)
  waiting for transfers between devices  7.3 us (22%)
  between operations  1.35 us (4%)
    ppermute x4, starting transfers between devices, swap_pairs(): lax.ppermute(block, axis, [(i, k) for i, k in route if 0 <= k < size])  11.9 us
    ppermute x4, waiting for transfers between devices, swap_pairs(): lax.ppermute(block, axis, [(i, k) for i, k in route if 0 <= k < size])  7.3 us
    pallas_call x1, Pallas kernels, per_device(): pl.pallas_call(first_kernel, out_shape=(halves_shape, face, jax.ShapeDtyp...  3.83 us
    pallas_call x1, Pallas kernels, per_device(): pl.pallas_call(functools.partial(gather_kernel, last), out_shape=tuple((j...  3.74 us
    pallas_call x1, Pallas kernels, per_device(): pl.pallas_call(second_kernel, out_shape=(halves_shape, face), in_specs=[s...  2.5 us
    pallas_call x1, Pallas kernels, per_device(): pl.pallas_call(functools.partial(middle_kernel, last), out_shape=nodes, i...  0.88 us
    pallas_call x1, Pallas kernels, per_device(): pl.pallas_call(prepare_kernel, out_shape=right_shape, in_specs=[anywhere,...  0.83 us
  transfers between devices with their start and end apart: 4, of which 2 were waited for; matrix products, arithmetic and copies ran while one was open for 0% of the time, Pallas kernels for 5%

profile of v4, /device:TPU:6, one launch (start us, length us, event | category | flops | bytes accessed | tf_op | source)
XLA Modules:
  0.0 32.7 jit_solution(15538922892840496937)
XLA Ops:
  1.3 3.8 %scatter_first.1 = (f32[2,9,6,16,256]{4,3,2,1,0:T(8,128)S(1)}, f32[184,256]{1,0:T(8,128)S(1)}, f32[12,32,128]{2,1,0:T(8,128)S(1)}, f32[13,32,128]{2,1,0:T(8,128)S(1)}, s32[1,24]{1,0:T(1,128)S(1)}) custom-call(s32[1,1]{1,0:T(1,128)S(6)} %copy.18.count_ref, s32[24]{0:T(128)} %tile_in.1, f32[3,24,128]{2,1,0:T(8,128)} %offset_in.1, f32[24,128]{1,0:T(8,128)} %mass_in.1, ...), custom_call_target="tpu_custom_call" | custom-call | flops 3000000 | bytes 4000000 | tf_op jit(solution)/shard_map/scatter_first/pallas_call | solution.py:554
  5.1 2.5 %scatter_second.1 = (f32[2,9,6,16,256]{4,3,2,1,0:T(8,128)S(1)}, f32[184,256]{1,0:T(8,128)S(1)}) custom-call(s32[1,24]{1,0:T(1,128)S(1)} %get-tuple-element.18.tile_ref, f32[2,9,6,16,256]{4,3,2,1,0:T(8,128)S(1)} %get-tuple-element.19.half_in, f32[12,32,128]{2,1,0:T(8,128)S(1)} %get-tuple-element.20.table, ...), custom_call_target="tpu_custom_call", output_to_operand_aliasing={{0}: (1, {})} | custom-call | flops 3000000 | bytes 4000000 | tf_op jit(solution)/shard_map/scatter_second/pallas_call | solution.py:576
  7.6 0.2 collective-permute-start
  7.8 6.5 %collective-permute-start.1 = (f32[184,256]{1,0:T(8,128)S(1)}, f32[184,256]{1,0:T(8,128)S(1)}, u32[]{:S(2)}, u32[]{:S(2)}) collective-permute-start(f32[184,256]{1,0:T(8,128)S(1)} %get-tuple-element.24), channel_id=1, source_target_pairs={{8,16},{16,8},{24,32},{32,24},{40,48},{48,40},{56,64},{64,56},{72,... | collective-permute-start | bytes 565256 | tf_op jit(solution)/shard_map/ppermute | solution.py:524
  14.3 0.8 %prepare.1.order.right = bf16[24,128,256]{2,1,0:T(8,128)(2,1)S(1)} custom-call(f32[184,256]{1,0:T(8,128)S(1)} %get-tuple-element.22.order, s32[1,24]{1,0:T(1,128)S(1)} %get-tuple-element.18.tile_ref, f32[12,32,128]{2,1,0:T(8,128)S(1)} %get-tuple-element.20.table), custom_call_target="tpu_custom_call" | custom-call | flops 3000000 | bytes 4000000 | tf_op jit(solution)/shard_map/prepare/pallas_call | solution.py:588
  15.1 0.0 collective-permute-done.recv_a
  15.1 2.4 %collective-permute-done.1.recv_d = f32[184,256]{1,0:T(8,128)S(1)} collective-permute-done((f32[184,256]{1,0:T(8,128)S(1)}, f32[184,256]{1,0:T(8,128)S(1)}, u32[]{:S(2)}, u32[]{:S(2)}) %collective-permute-start.1) | collective-permute-done | bytes 188448 | tf_op jit(solution)/shard_map/ppermute | solution.py:524
  17.5 0.3 %corners.1 = (f32[184,256]{1,0:T(8,128)S(1)}, f32[184,256]{1,0:T(8,128)S(1)}, f32[9,4,16,256]{3,2,1,0:T(8,128)S(1)}) custom-call(bf16[24,128,256]{2,1,0:T(8,128)(2,1)S(1)} %prepare.1.order.right, f32[2,9,6,16,256]{4,3,2,1,0:T(8,128)S(1)} %get-tuple-element.23.halves, f32[184,256]{1,0:T(8,128)S(1)} %collective-permute-done.recv_a, ...), custom_call_target="tpu_custom_call" | custom-call | tf_op jit(solution)/shard_map/corners/pallas_call | solution.py:597
  17.9 5.2 %collective-permute-start.3 = (f32[184,256]{1,0:T(8,128)S(1)}, f32[184,256]{1,0:T(8,128)S(1)}, u32[]{:S(2)}, u32[]{:S(2)}) collective-permute-start(f32[184,256]{1,0:T(8,128)S(1)} %get-tuple-element.27.own_d), channel_id=1, source_target_pairs={{1,2},{2,1},{3,4},{4,3},{5,6},{6,5},{9,10},{10,9},{11,12},{12,11},... | collective-permute-start | bytes 565256 | tf_op jit(solution)/shard_map/ppermute | solution.py:524
  23.1 0.1 collective-permute-start.2
  23.2 0.0 copy-start
  23.2 0.9 %middle.1 = f32[2,5,3,80,128]{4,3,2,1,0:T(8,128)S(1)} custom-call(f32[184,256]{1,0:T(8,128)S(1)} %get-tuple-element.25.order.own_a, f32[2,9,6,16,256]{4,3,2,1,0:T(8,128)S(1)} %get-tuple-element.23.halves, f32[9,4,16,256]{3,2,1,0:T(8,128)S(1)} %get-tuple-element.26.edge), custom_call_target="tpu_custom_call" | custom-call | flops 3000000 | bytes 4000000 | tf_op jit(solution)/shard_map/middle/pallas_call | solution.py:607
  24.1 4.9 %collective-permute-done.3.y_d = f32[184,256]{1,0:T(8,128)S(1)} collective-permute-done((f32[184,256]{1,0:T(8,128)S(1)}, f32[184,256]{1,0:T(8,128)S(1)}, u32[]{:S(2)}, u32[]{:S(2)}) %collective-permute-start.3) | collective-permute-done | bytes 188448 | tf_op jit(solution)/shard_map/ppermute | solution.py:524
  29.0 0.0 collective-permute-done.2.y_a
  29.0 0.0 copy-done
  29.0 3.7 %gather.1 = (f32[3,24,128]{2,1,0:T(8,128)}, f32[9,24,128]{2,1,0:T(8,128)}, f32[9,24,128]{2,1,0:T(8,128)}, f32[6,24,128]{2,1,0:T(8,128)}, f32[2,5,3,80,128]{4,3,2,1,0:T(8,128)S(1)}) custom-call(s32[1,24]{1,0:T(1,128)S(1)} %get-tuple-element.18.tile_ref, f32[2,5,3,80,128]{4,3,2,1,0:T(8,128)S(1)} %middle.1, ...), custom_call_target="tpu_custom_call", output_to_operand_aliasing={{4}: (1, {})} | custom-call | tf_op jit(solution)/shard_map/gather/pallas_call | solution.py:619
Async XLA Ops:
  7.6 7.5 %collective-permute-start = (f32[184,256]{1,0:T(8,128)S(1)}, f32[184,256]{1,0:T(8,128)S(1)}, u32[]{:S(2)}, u32[]{:S(2)}) collective-permute-start(f32[184,256]{1,0:T(8,128)S(1)} %get-tuple-element.22.order), channel_id=1, source_target_pairs={{0,8},{8,0},{16,24},{24,16},{32,40},{40,32},{48,56},{56,48},{64,72... | collective-permute-start | bytes 565256 | tf_op jit(solution)/shard_map/ppermute | solution.py:524
  7.8 9.7 %collective-permute-start.1 = (f32[184,256]{1,0:T(8,128)S(1)}, f32[184,256]{1,0:T(8,128)S(1)}, u32[]{:S(2)}, u32[]{:S(2)}) collective-permute-start(f32[184,256]{1,0:T(8,128)S(1)} %get-tuple-element.24), channel_id=1, source_target_pairs={{8,16},{16,8},{24,32},{32,24},{40,48},{48,40},{56,64},{64,56},{72,... | collective-permute-start | bytes 565256 | tf_op jit(solution)/shard_map/ppermute | solution.py:524
  17.9 11.1 %collective-permute-start.3 = (f32[184,256]{1,0:T(8,128)S(1)}, f32[184,256]{1,0:T(8,128)S(1)}, u32[]{:S(2)}, u32[]{:S(2)}) collective-permute-start(f32[184,256]{1,0:T(8,128)S(1)} %get-tuple-element.27.own_d), channel_id=1, source_target_pairs={{1,2},{2,1},{3,4},{4,3},{5,6},{6,5},{9,10},{10,9},{11,12},{12,11},... | collective-permute-start | bytes 565256 | tf_op jit(solution)/shard_map/ppermute | solution.py:524
  23.1 5.9 %collective-permute-start.2 = (f32[184,256]{1,0:T(8,128)S(1)}, f32[184,256]{1,0:T(8,128)S(1)}, u32[]{:S(2)}, u32[]{:S(2)}) collective-permute-start(f32[184,256]{1,0:T(8,128)S(1)} %get-tuple-element.25.order.own_a), channel_id=1, source_target_pairs={{0,1},{1,0},{2,3},{3,2},{4,5},{5,4},{6,7},{7,6},{8,9},{9,8},{10,11... | collective-permute-start | bytes 565256 | tf_op jit(solution)/shard_map/ppermute | solution.py:524
  23.2 5.8 %copy-start = (f32[9,24,128]{2,1,0:T(8,128)S(1)}, f32[9,24,128]{2,1,0:T(8,128)}, u32[]{:S(2)}) copy-start(f32[9,24,128]{2,1,0:T(8,128)} %deform.1) | copy-start | bytes 331780

commit v5 on v4

--- a/solution.py
+++ b/solution.py
@@ -25,6 +25,7 @@
 FACE_ROWS = 184
 CHANNELS = 9
 CHUNK = 8
+UNROLL = 4
 
 POS_Y, POS_Z, FIELD0, FIELD1, POS_X, LIVE, WX = 0, 1, 2, 3, 4, 5, 6
 GATHER_ROWS = WX + 6
@@ -97,14 +98,15 @@
         return n + (lax.shift_right_logical(tile_ref[0, s], 6) == tile_x).astype(jnp.int32)
 
     n = lax.fori_loop(0, SLOTS, body, 0)
-    order[n] = SLOTS
+    for k in range(UNROLL - 1):
+        order[n + k] = SLOTS
     return n
 
 
 def clear(left_hi, left_lo, acc):
     acc[...] = jnp.zeros_like(acc)
     zeros = jnp.zeros((48, LANES), BF16)
-    for u in range(2):
+    for u in range(UNROLL):
         left_hi[u, 0:48, LANES : 2 * LANES] = zeros
         left_lo[u, 0:48, LANES : 2 * LANES] = zeros
 
@@ -164,12 +166,12 @@
             acc[tile_y, f, 0, window, :] += total[16 * f : 16 * f + 16, 0:LANES]
             acc[tile_y, f, 1, window, 0:64] += total[16 * f : 16 * f + 16, LANES:192]
 
-    def step(pair, carry):
-        one(pair * 2, 0)
-        one(pair * 2 + 1, 1)
+    def step(group, carry):
+        for u in range(UNROLL):
+            one(group * UNROLL + u, u)
         return carry
 
-    lax.fori_loop(0, lax.shift_right_logical(count + 1, 1), step, 0)
+    lax.fori_loop(0, lax.div(count + UNROLL - 1, UNROLL), step, 0)
 
     for ty in range(2):
         for f in range(2):
@@ -365,12 +367,47 @@
     return jnp.where(((x == 0) & (index == 0)) | ((x == SIDE - 1) & (index == last[0])), 0.0, 1.0)
 
 
-def middle_kernel(last, order, halves, edge, nodes, work):
+def tile_of(tile_ref, s):
+    tile = tile_ref[0, s]
+    tile_z = tile & 31
+    j = lax.div(tile_z, 7)
+    return (
+        lax.shift_right_logical(tile, 6),
+        lax.shift_right_logical(tile, 5) & 1,
+        j,
+        (tile_z - 7 * j) * 8,
+    )
+
+
+def z_window(value, shift):
+    lane = iota(value.shape, 1) & 63
+    window = pltpu.roll(value, lax.rem(128 - shift, 128), 1)
+    window = jnp.where(lane < 16, window, pltpu.roll(value, lax.rem(144 - shift, 128), 1))
+    window = jnp.where(lane < 32, window, pltpu.roll(value, lax.rem(160 - shift, 128), 1))
+    high = window.astype(BF16).astype(F32)
+    return jnp.where(lane < 32, high, window - high).astype(BF16)
+
+
+def collect(partial, k):
+    total = partial[k, pl.ds(0, CHUNK, stride=8), :]
+    for y in range(1, 8):
+        total = total + partial[k, pl.ds(y, CHUNK, stride=8), :]
+    return total
+
+
+def chunk_of(chunk):
+    return pl.ds(pl.multiple_of(chunk * CHUNK, CHUNK), CHUNK)
+
+
+def middle_kernel(
+    last, order, tile_ref, halves, edge, table, right, gathered, work, nodes, partial,
+):
     for c in range(CHANNELS):
         for x in range(SIDE):
             work[c, x] = plane(halves, edge, c, x, slice(0, 8))
-
-    def step(x, carry):
+    inner = iota((8, LANES), 0) >= 2
+
+    def node_step(x, carry):
         inside = inside_x(x, last)
         found = [
             node_speeds([work[c, x, :, half(h)] for c in range(8)], work[8, x, :, half(h)], inside)
@@ -380,17 +417,55 @@
         for c in range(3):
             ready = tiles(*([found[h][f][c] for h in range(2)] for f in range(2)))
             for j in range(5):
-                for ty in range(2):
-                    nodes[ty, j, c, pl.ds(at, 8), :] = ready[j]
+                nodes[j, c, pl.ds(at, 8), :] = jnp.where(inner, ready[j], 0.0)
         return carry
 
-    lax.fori_loop(0, SIDE, step, 0, unroll=2)
+    lax.fori_loop(0, SIDE, node_step, 0, unroll=2)
+
+    def one(chunk, slot):
+        s = chunk * CHUNK + slot
+        tile_x, tile_y, j, shift = tile_of(tile_ref, s)
+
+        def row(k):
+            return table[k, pl.ds(s, 1), :]
+
+        first = pl.multiple_of(tile_x * 32, 32)
+        left = [z_window(nodes[j, c, pl.ds(first, 48), :], shift) for c in range(3)]
+        summed = matmul(jnp.concatenate(left, 0), right[s])
+        dy = y_coords(tile_y) - row(POS_Y)
+        wy = spline(dy)
+        pos_x = row(POS_X)
+        wxy = [wy * row(WX + x) for x in range(6)]
+        place = slice(slot * 8, slot * 8 + 8)
+        for c in range(3):
+            speed = along_x = along_z = None
+            for x in range(5, -1, -1):
+                at = (c * 6 + x) * 8
+                part = wxy[x] * summed[at : at + 8, 0:LANES]
+                moment = wxy[x] * summed[at : at + 8, LANES : 2 * LANES]
+                speed = part if speed is None else speed + part
+                along_z = moment if along_z is None else along_z + moment
+                if x:
+                    along_x = speed if along_x is None else along_x + speed
+            partial[4 * c, place, :] = speed
+            partial[4 * c + 1, place, :] = along_x - pos_x * speed
+            partial[4 * c + 2, place, :] = speed * dy
+            partial[4 * c + 3, place, :] = along_z
+
+    def step(chunk, carry):
+        for slot in range(CHUNK):
+            one(chunk, slot)
+        for k in range(12):
+            gathered[k, chunk_of(chunk), :] = collect(partial, k)
+        return carry
+
+    lax.fori_loop(0, SLOTS // CHUNK, step, 0)
 
 
 def gather_kernel(
-    last, tile_ref, middle, own_a, own_d, y_a, y_d, table, right, deform,
-    velocity_out, affine_out, deform_out, stress_out, nodes,
-    partial, new_velocity, new_affine, new_deform, new_stress, sems,
+    last, tile_ref, gathered, own_a, own_d, y_a, y_d, table, right, deform,
+    velocity_out, affine_out, deform_out, stress_out,
+    nodes, partial, new_velocity, new_affine, new_deform, new_stress, sems,
 ):
     side_y = low_side("gy")
     index_y = lax.axis_index("gy")
@@ -411,83 +486,66 @@
             for c in range(3):
                 ready = tiles(*([found[h][f][c] for h in range(2)] for f in range(2)))
                 for j in range(5):
-                    for x in range(count):
-                        at = (first + x) * 8
-                        nodes[high, j, c, at : at + 2, :] = ready[j][2 * x : 2 * x + 2]
+                    nodes[high, j, c, 2 * first : 2 * (first + count), :] = ready[j]
+        for c in range(3):
+            for j in range(5):
+                nodes[high, j, c, 2 * SIDE : 24, :] = jnp.zeros((24 - 2 * SIDE, LANES), F32)
 
     def one(chunk, slot):
         s = chunk * CHUNK + slot
-        tile = tile_ref[0, s]
-        tile_x = lax.shift_right_logical(tile, 6)
-        tile_y = lax.shift_right_logical(tile, 5) & 1
-        tile_z = tile & 31
-        j = lax.div(tile_z, 7)
-        shift = (tile_z - 7 * j) * 8
+        tile_x, tile_y, j, shift = tile_of(tile_ref, s)
 
         def row(k):
             return table[k, pl.ds(s, 1), :]
 
-        first = pl.multiple_of(tile_x * 32, 32)
-        lane = iota((48, LANES), 1) & 63
-        left = []
-        for c in range(3):
-            value = nodes[tile_y, j, c, pl.ds(first, 48), :]
-            window = pltpu.roll(value, lax.rem(128 - shift, 128), 1)
-            window = jnp.where(lane < 16, window, pltpu.roll(value, lax.rem(144 - shift, 128), 1))
-            window = jnp.where(lane < 32, window, pltpu.roll(value, 160 - shift - 128 * (shift <= 32).astype(jnp.int32), 1))
-            high = window.astype(BF16).astype(F32)
-            left.append(jnp.where(lane < 32, high, window - high).astype(BF16))
-        summed = matmul(jnp.concatenate(left, 0), right[s])
-
-        dy = y_coords(tile_y) - row(POS_Y)
+        first = pl.multiple_of(tile_x * 8, 8)
+        left = [nodes[tile_y, j, c, pl.ds(first, 16), :] for c in range(3)]
+        summed = matmul(z_window(jnp.concatenate(left, 0), shift), right[s])
+        sublane = iota((8, LANES), 0)
+        dy = ((sublane & 1) + 4 * tile_y).astype(F32) - row(POS_Y)
         wy = spline(dy)
-        pos_x = row(POS_X)
-        wxy = [wy * row(WX + x) for x in range(6)]
+        speed, along_x, along_z = [None] * 3, [None] * 3, [None] * 3
+        for q in range(2):
+            dx = (lax.shift_right_logical(sublane, 1) + 4 * q).astype(F32) - row(POS_X)
+            weight = wy * spline(dx)
+            for c in range(3):
+                at = c * 16 + q * 8
+                part = weight * summed[at : at + 8, 0:LANES]
+                moment = weight * summed[at : at + 8, LANES : 2 * LANES]
+                speed[c] = part if q == 0 else speed[c] + part
+                along_x[c] = part * dx if q == 0 else along_x[c] + part * dx
+                along_z[c] = moment if q == 0 else along_z[c] + moment
         place = slice(slot * 8, slot * 8 + 8)
         for c in range(3):
-            speed = along_x = along_z = None
-            for x in range(5, -1, -1):
-                at = (c * 6 + x) * 8
-                part = wxy[x] * summed[at : at + 8, 0:LANES]
-                moment = wxy[x] * summed[at : at + 8, LANES : 2 * LANES]
-                speed = part if speed is None else speed + part
-                along_z = moment if along_z is None else along_z + moment
-                if x:
-                    along_x = speed if along_x is None else along_x + speed
-            partial[4 * c, place, :] = speed
-            partial[4 * c + 1, place, :] = along_x - pos_x * speed
-            partial[4 * c + 2, place, :] = speed * dy
-            partial[4 * c + 3, place, :] = along_z
-
-    def collect(k):
-        total = partial[k, pl.ds(0, CHUNK, stride=8), :]
-        for y in range(1, 8):
-            total = total + partial[k, pl.ds(y, CHUNK, stride=8), :]
-        return total
+            partial[4 * c, place, :] = speed[c]
+            partial[4 * c + 1, place, :] = along_x[c]
+            partial[4 * c + 2, place, :] = speed[c] * dy
+            partial[4 * c + 3, place, :] = along_z[c]
 
     ready = (new_velocity, new_affine, new_deform, new_stress)
     finals = (velocity_out, affine_out, deform_out, stress_out)
 
     def sends(chunk):
-        own_slots = pl.ds(pl.multiple_of(chunk * CHUNK, CHUNK), CHUNK)
+        slots = chunk_of(chunk)
         return [
-            pltpu.make_async_copy(src.at[:, own_slots], dst.at[:, own_slots], sems.at[chunk, i])
+            pltpu.make_async_copy(src.at[:, slots], dst.at[:, slots], sems.at[chunk, i])
             for i, (src, dst) in enumerate(zip(ready, finals))
         ]
 
     def step(chunk, carry):
         for slot in range(CHUNK):
             one(chunk, slot)
-        own_slots = pl.ds(pl.multiple_of(chunk * CHUNK, CHUNK), CHUNK)
-        live = table[LIVE, own_slots, :]
+        slots = chunk_of(chunk)
+        live = table[LIVE, slots, :]
+        total = [(gathered[k, slots, :] + collect(partial, k)) * live for k in range(12)]
         moved = []
         for c in range(3):
-            new_velocity[c, own_slots, :] = collect(4 * c) * live
+            new_velocity[c, slots, :] = total[4 * c]
             for k in range(3):
-                value = 4.0 * collect(4 * c + 1 + k) * live
-                new_affine[3 * c + k, own_slots, :] = value
+                value = 4.0 * total[4 * c + 1 + k]
+                new_affine[3 * c + k, slots, :] = value
                 moved.append(value)
-        old = [deform[k, own_slots, :] for k in range(9)]
+        old = [deform[k, slots, :] for k in range(9)]
         fresh = []
         for i in range(3):
             for j in range(3):
@@ -496,10 +554,10 @@
                     value = value + DT * moved[3 * i + k] * old[3 * k + j]
                 fresh.append(value * live)
         for k in range(9):
-            new_deform[k, own_slots, :] = fresh[k]
+            new_deform[k, slots, :] = fresh[k]
         stress = kirchhoff(fresh)
         for k, entry in enumerate((0, 4, 8, 1, 2, 5)):
-            new_stress[k, own_slots, :] = stress[entry] * live
+            new_stress[k, slots, :] = stress[entry] * live
         for send in sends(chunk):
             send.start()
         return carry
@@ -533,7 +591,6 @@
     hbm = pl.BlockSpec(memory_space=pltpu.HBM)
     whole = pl.BlockSpec(memory_space=pltpu.VMEM)
     face = jax.ShapeDtypeStruct((FACE_ROWS, DEPTH), F32)
-    nodes = jax.ShapeDtypeStruct((2, 5, 3, 8 * SIDE, LANES), F32)
     right_shape = jax.ShapeDtypeStruct((SLOTS, LANES, 256), BF16)
     last = (lax.axis_size("gx") - 1, lax.axis_size("gy") - 1)
     inputs = (
@@ -544,8 +601,8 @@
     halves_shape = jax.ShapeDtypeStruct((2, CHANNELS, 6, 16, DEPTH), F32)
     scatter_scratch = [
         pltpu.SMEM((32,), jnp.int32),
-        vmem((2, 192, 256), BF16),
-        vmem((2, 192, 256), BF16),
+        vmem((UNROLL, 192, 256), BF16),
+        vmem((UNROLL, 192, 256), BF16),
         vmem((2, 2, 2, 280, LANES)),
         vmem((2, 2, 192, DEPTH)),
     ]
@@ -604,34 +661,32 @@
     )(right, halves, got_x_a, got_x_d)
     got_y_d = swap_pairs(y_d, "gy", 1)
     got_y_a = swap_pairs(y_a, "gy", 0)
-    middle = pl.pallas_call(
+    slots, particles = particle_mass.shape
+    gathered = pl.pallas_call(
         functools.partial(middle_kernel, last),
-        out_shape=nodes,
-        in_specs=[anywhere] + [whole] * 2,
+        out_shape=jax.ShapeDtypeStruct((12, slots, particles), F32),
+        in_specs=[anywhere, smem] + [whole] * 4,
         out_specs=whole,
-        scratch_shapes=[vmem((CHANNELS, SIDE, 8, DEPTH))],
+        scratch_shapes=[
+            vmem((CHANNELS, SIDE, 8, DEPTH)),
+            vmem((5, 3, 8 * SIDE, LANES)),
+            vmem((12, 8 * CHUNK, LANES)),
+        ],
         compiler_params=params,
         cost_estimate=cost(3000000),
         name="middle",
-    )(y_a, halves, edge)
-
-    slots, particles = particle_mass.shape
-    out = pl.pallas_call(
+    )(y_a, tile_numbers, halves, edge, table, right)
+    return pl.pallas_call(
         functools.partial(gather_kernel, last),
-        out_shape=tuple(jax.ShapeDtypeStruct((k, slots, particles), F32) for k in (3, 9, 9, 6))
-        + (nodes,),
+        out_shape=tuple(jax.ShapeDtypeStruct((k, slots, particles), F32) for k in (3, 9, 9, 6)),
         in_specs=[smem] + [whole] * 8,
-        out_specs=(hbm,) * 4 + (whole,),
-        scratch_shapes=[vmem((12, 8 * CHUNK, LANES))]
+        out_specs=(hbm,) * 4,
+        scratch_shapes=[vmem((2, 5, 3, 24, LANES)), vmem((12, 8 * CHUNK, LANES))]
         + [vmem((k, slots, particles)) for k in (3, 9, 9, 6)]
         + [pltpu.SemaphoreType.DMA((SLOTS // CHUNK, 4))],
-        input_output_aliases={1: 4},
         compiler_params=params,
         name="gather",
-    )(
-        tile_numbers, middle, y_a, y_d, got_y_a, got_y_d, table, right, deform,
-    )
-    return out[:4]
+    )(tile_numbers, gathered, y_a, y_d, got_y_a, got_y_d, table, right, deform)
 
 
 def solution(mesh):

time: 32.9 us -> 31.2 us (0.948)
  waiting for transfers between devices: 7.3 us -> 4.8 us
  Pallas kernels: 12.1 us -> 13.4 us
  starting transfers between devices: 11.9 us -> 11.5 us
    pallas_call x1, Pallas kernels: 0.88 us -> 3.5 us  [per_device(): pl.pallas_call(functools.partial(middle_kernel, last), out_shape=jax.Shap...]
    ppermute x4, waiting for transfers between devices: 7.3 us -> 4.8 us  [swap_pairs(): lax.ppermute(block, axis, [(i, k) for i, k in route if 0 <= k < size])]
    pallas_call x1, Pallas kernels: 3.74 us -> 2.87 us  [per_device(): pl.pallas_call(functools.partial(gather_kernel, last), out_shape=tuple((j...]
    ppermute x4, starting transfers between devices: 11.9 us -> 11.5 us  [swap_pairs(): lax.ppermute(block, axis, [(i, k) for i, k in route if 0 <= k < size])]
  transfers between devices with their start and end apart: 4 -> 4, of which waited for: 2 -> 2; matrix products, arithmetic and copies ran while one was open for 0% -> 0% of each run, Pallas kernels for 5% -> 14%
where the time goes in v5:
time: 31.2 us; the launch traced here: 31.1 us
  Pallas kernels  13.4 us (43%)
  starting transfers between devices  11.5 us (37%)
  waiting for transfers between devices  4.8 us (15%)
  between operations  1.36 us (4%)
    ppermute x4, starting transfers between devices, swap_pairs(): lax.ppermute(block, axis, [(i, k) for i, k in route if 0 <= k < size])  11.5 us
    ppermute x4, waiting for transfers between devices, swap_pairs(): lax.ppermute(block, axis, [(i, k) for i, k in route if 0 <= k < size])  4.8 us
    pallas_call x1, Pallas kernels, per_device(): pl.pallas_call(first_kernel, out_shape=(halves_shape, face, jax.ShapeDtyp...  3.51 us
    pallas_call x1, Pallas kernels, per_device(): pl.pallas_call(functools.partial(middle_kernel, last), out_shape=jax.Shap...  3.5 us
    pallas_call x1, Pallas kernels, per_device(): pl.pallas_call(functools.partial(gather_kernel, last), out_shape=tuple((j...  2.87 us
    pallas_call x1, Pallas kernels, per_device(): pl.pallas_call(second_kernel, out_shape=(halves_shape, face), in_specs=[s...  2.32 us
    pallas_call x1, Pallas kernels, per_device(): pl.pallas_call(prepare_kernel, out_shape=right_shape, in_specs=[anywhere,...  0.83 us
  transfers between devices with their start and end apart: 4, of which 2 were waited for; matrix products, arithmetic and copies ran while one was open for 0% of the time, Pallas kernels for 14%

profile of v5, /device:TPU:6, one launch (start us, length us, event | category | flops | bytes accessed | tf_op | source)
XLA Modules:
  0.0 31.1 jit_solution(9462055839935355730)
XLA Ops:
  1.3 3.5 %scatter_first.1 = (f32[2,9,6,16,256]{4,3,2,1,0:T(8,128)S(1)}, f32[184,256]{1,0:T(8,128)S(1)}, f32[12,32,128]{2,1,0:T(8,128)S(1)}, f32[13,32,128]{2,1,0:T(8,128)S(1)}, s32[1,24]{1,0:T(1,128)S(1)}) custom-call(s32[1,1]{1,0:T(1,128)S(6)} %copy.16.count_ref, s32[24]{0:T(128)} %tile_in.1, f32[3,24,128]{2,1,0:T(8,128)} %offset_in.1, f32[24,128]{1,0:T(8,128)} %mass_in.1, ...), custom_call_target="tpu_custom_call" | custom-call | flops 3000000 | bytes 4000000 | tf_op jit(solution)/shard_map/scatter_first/pallas_call | solution.py:611
  4.8 2.3 %scatter_second.1 = (f32[2,9,6,16,256]{4,3,2,1,0:T(8,128)S(1)}, f32[184,256]{1,0:T(8,128)S(1)}) custom-call(s32[1,24]{1,0:T(1,128)S(1)} %get-tuple-element.14.tile_ref, f32[2,9,6,16,256]{4,3,2,1,0:T(8,128)S(1)} %get-tuple-element.15.half_in, f32[12,32,128]{2,1,0:T(8,128)S(1)} %get-tuple-element.16.table, ...), custom_call_target="tpu_custom_call", output_to_operand_aliasing={{0}: (1, {})} | custom-call | flops 3000000 | bytes 4000000 | tf_op jit(solution)/shard_map/scatter_second/pallas_call | solution.py:633
  7.1 0.1 collective-permute-start
  7.2 6.3 %collective-permute-start.1 = (f32[184,256]{1,0:T(8,128)S(1)}, f32[184,256]{1,0:T(8,128)S(1)}, u32[]{:S(2)}, u32[]{:S(2)}) collective-permute-start(f32[184,256]{1,0:T(8,128)S(1)} %get-tuple-element.20), channel_id=1, source_target_pairs={{8,16},{16,8},{24,32},{32,24},{40,48},{48,40},{56,64},{64,56},{72,... | collective-permute-start | bytes 565256 | tf_op jit(solution)/shard_map/ppermute | solution.py:582
  13.5 0.8 %prepare.1.order.right = bf16[24,128,256]{2,1,0:T(8,128)(2,1)S(1)} custom-call(f32[184,256]{1,0:T(8,128)S(1)} %get-tuple-element.18.order, s32[1,24]{1,0:T(1,128)S(1)} %get-tuple-element.14.tile_ref, f32[12,32,128]{2,1,0:T(8,128)S(1)} %get-tuple-element.16.table), custom_call_target="tpu_custom_call" | custom-call | flops 3000000 | bytes 4000000 | tf_op jit(solution)/shard_map/prepare/pallas_call | solution.py:645
  14.4 0.0 collective-permute-done.recv_a
  14.4 2.4 %collective-permute-done.1.recv_d = f32[184,256]{1,0:T(8,128)S(1)} collective-permute-done((f32[184,256]{1,0:T(8,128)S(1)}, f32[184,256]{1,0:T(8,128)S(1)}, u32[]{:S(2)}, u32[]{:S(2)}) %collective-permute-start.1) | collective-permute-done | bytes 188448 | tf_op jit(solution)/shard_map/ppermute | solution.py:582
  16.8 0.3 %corners.1 = (f32[184,256]{1,0:T(8,128)S(1)}, f32[184,256]{1,0:T(8,128)S(1)}, f32[9,4,16,256]{3,2,1,0:T(8,128)S(1)}) custom-call(bf16[24,128,256]{2,1,0:T(8,128)(2,1)S(1)} %prepare.1.order.right, f32[2,9,6,16,256]{4,3,2,1,0:T(8,128)S(1)} %get-tuple-element.19.halves, f32[184,256]{1,0:T(8,128)S(1)} %collective-permute-done.recv_a, ...), custom_call_target="tpu_custom_call" | custom-call | tf_op jit(solution)/shard_map/corners/pallas_call | solution.py:654
  17.1 5.1 %collective-permute-start.3 = (f32[184,256]{1,0:T(8,128)S(1)}, f32[184,256]{1,0:T(8,128)S(1)}, u32[]{:S(2)}, u32[]{:S(2)}) collective-permute-start(f32[184,256]{1,0:T(8,128)S(1)} %get-tuple-element.23.own_d), channel_id=1, source_target_pairs={{1,2},{2,1},{3,4},{4,3},{5,6},{6,5},{9,10},{10,9},{11,12},{12,11},... | collective-permute-start | bytes 565256 | tf_op jit(solution)/shard_map/ppermute | solution.py:582
  22.2 0.1 collective-permute-start.2
  22.3 0.0 copy-start
  22.3 3.5 %middle.1.gathered = f32[12,24,128]{2,1,0:T(8,128)S(1)} custom-call(f32[184,256]{1,0:T(8,128)S(1)} %get-tuple-element.21.order.own_a, s32[1,24]{1,0:T(1,128)S(1)} %get-tuple-element.14.tile_ref, f32[2,9,6,16,256]{4,3,2,1,0:T(8,128)S(1)} %get-tuple-element.19.halves, f32[9,4,16,256]{3,2,1,0:T(8,128)S(1)} %get-tuple-element.22.edge, ...), custom_call_target="tpu_custom_call" | custom-call | flops 3000000 | bytes 4000000 | tf_op jit(solution)/shard_map/middle/pallas_call | solution.py:665
  25.8 2.4 %collective-permute-done.3.y_d = f32[184,256]{1,0:T(8,128)S(1)} collective-permute-done((f32[184,256]{1,0:T(8,128)S(1)}, f32[184,256]{1,0:T(8,128)S(1)}, u32[]{:S(2)}, u32[]{:S(2)}) %collective-permute-start.3) | collective-permute-done | bytes 188448 | tf_op jit(solution)/shard_map/ppermute | solution.py:582
  28.2 0.0 collective-permute-done.2.y_a
  28.2 0.0 copy-done
  28.2 2.9 %gather.1 = (f32[3,24,128]{2,1,0:T(8,128)}, f32[9,24,128]{2,1,0:T(8,128)}, f32[9,24,128]{2,1,0:T(8,128)}, f32[6,24,128]{2,1,0:T(8,128)}) custom-call(s32[1,24]{1,0:T(1,128)S(1)} %get-tuple-element.14.tile_ref, f32[12,24,128]{2,1,0:T(8,128)S(1)} %middle.1.gathered, f32[184,256]{1,0:T(8,128)S(1)} %get-tuple-element.21.order.own_a, ...), custom_call_target="tpu_custom_call" | custom-call | tf_op jit(solution)/shard_map/gather/pallas_call | solution.py:679
Async XLA Ops:
  7.1 7.2 %collective-permute-start = (f32[184,256]{1,0:T(8,128)S(1)}, f32[184,256]{1,0:T(8,128)S(1)}, u32[]{:S(2)}, u32[]{:S(2)}) collective-permute-start(f32[184,256]{1,0:T(8,128)S(1)} %get-tuple-element.18.order), channel_id=1, source_target_pairs={{0,8},{8,0},{16,24},{24,16},{32,40},{40,32},{48,56},{56,48},{64,72... | collective-permute-start | bytes 565256 | tf_op jit(solution)/shard_map/ppermute | solution.py:582
  7.2 9.6 %collective-permute-start.1 = (f32[184,256]{1,0:T(8,128)S(1)}, f32[184,256]{1,0:T(8,128)S(1)}, u32[]{:S(2)}, u32[]{:S(2)}) collective-permute-start(f32[184,256]{1,0:T(8,128)S(1)} %get-tuple-element.20), channel_id=1, source_target_pairs={{8,16},{16,8},{24,32},{32,24},{40,48},{48,40},{56,64},{64,56},{72,... | collective-permute-start | bytes 565256 | tf_op jit(solution)/shard_map/ppermute | solution.py:582
  17.1 11.1 %collective-permute-start.3 = (f32[184,256]{1,0:T(8,128)S(1)}, f32[184,256]{1,0:T(8,128)S(1)}, u32[]{:S(2)}, u32[]{:S(2)}) collective-permute-start(f32[184,256]{1,0:T(8,128)S(1)} %get-tuple-element.23.own_d), channel_id=1, source_target_pairs={{1,2},{2,1},{3,4},{4,3},{5,6},{6,5},{9,10},{10,9},{11,12},{12,11},... | collective-permute-start | bytes 565256 | tf_op jit(solution)/shard_map/ppermute | solution.py:582
  22.2 6.0 %collective-permute-start.2 = (f32[184,256]{1,0:T(8,128)S(1)}, f32[184,256]{1,0:T(8,128)S(1)}, u32[]{:S(2)}, u32[]{:S(2)}) collective-permute-start(f32[184,256]{1,0:T(8,128)S(1)} %get-tuple-element.21.order.own_a), channel_id=1, source_target_pairs={{0,1},{1,0},{2,3},{3,2},{4,5},{5,4},{6,7},{7,6},{8,9},{9,8},{10,11... | collective-permute-start | bytes 565256 | tf_op jit(solution)/shard_map/ppermute | solution.py:582
  22.3 5.9 %copy-start = (f32[9,24,128]{2,1,0:T(8,128)S(1)}, f32[9,24,128]{2,1,0:T(8,128)}, u32[]{:S(2)}) copy-start(f32[9,24,128]{2,1,0:T(8,128)} %deform.1) | copy-start | bytes 331780

commit v6 on v5

--- a/solution.py
+++ b/solution.py
@@ -22,7 +22,8 @@
 DEPTH = 256
 SLOTS = 24
 LANES = 128
-FACE_ROWS = 184
+X_FACE_ROWS = 184
+Y_FACE_ROWS = 176
 CHANNELS = 9
 CHUNK = 8
 UNROLL = 4
@@ -93,11 +94,10 @@
 
 
 def matching_slots(order, tile_ref, tile_x):
-    def body(s, n):
+    n = jnp.int32(0)
+    for s in range(SLOTS):
         order[n] = s
-        return n + (lax.shift_right_logical(tile_ref[0, s], 6) == tile_x).astype(jnp.int32)
-
-    n = lax.fori_loop(0, SLOTS, body, 0)
+        n = n + (lax.shift_right_logical(tile_ref[0, s], 6) == tile_x).astype(jnp.int32)
     for k in range(UNROLL - 1):
         order[n + k] = SLOTS
     return n
@@ -291,7 +291,7 @@
 
 
 def y_face_row(c, x):
-    return c * 16 + x * 2 if x < 8 else 144 + c * 4 + (x - 8) * 2
+    return c * 16 + x * 2 if x < 8 else 128 + c * 4 + (x - 8) * 2
 
 
 def corner_kernel(order, halves, recv_a, recv_d, face_a, face_d, edge):
@@ -308,11 +308,14 @@
                 edge[(*to, slice(8, 10))] += recv[144 + at * 2 : 146 + at * 2]
     for face, high in ((face_a, 1 - side_y), (face_d, side_y)):
         rows = pl.ds(pl.multiple_of(high * 8, 8), 2)
-        for c in range(CHANNELS):
+        for c in range(8):
             for x in range(SIDE):
                 at = y_face_row(c, x)
                 face[at : at + 2, :] = plane(halves, edge, c, x, rows)
-        face[180:184, :] = jnp.zeros((4, DEPTH), F32)
+        own_row = pl.ds(1 + 7 * high, 1)
+        for x in range(SIDE):
+            face[160 + x : 161 + x, :] = plane(halves, edge, 8, x, own_row)
+        face[170:176, :] = jnp.zeros((6, DEPTH), F32)
 
 
 def node_speeds(sums, code, inside):
@@ -396,6 +399,8 @@
 
 
 def chunk_of(chunk):
+    if isinstance(chunk, int):
+        return slice(chunk * CHUNK, (chunk + 1) * CHUNK)
     return pl.ds(pl.multiple_of(chunk * CHUNK, CHUNK), CHUNK)
 
 
@@ -465,12 +470,15 @@
 def gather_kernel(
     last, tile_ref, gathered, own_a, own_d, y_a, y_d, table, right, deform,
     velocity_out, affine_out, deform_out, stress_out,
-    nodes, partial, new_velocity, new_affine, new_deform, new_stress, sems,
+    nodes, codes, partial, new_velocity, new_affine, new_deform, new_stress, sems,
 ):
     side_y = low_side("gy")
     index_y = lax.axis_index("gy")
     for own, recv, high in ((own_a, y_a, 1 - side_y), (own_d, y_d, side_y)):
         edge_y = jnp.where(high == 0, (index_y == 0), (index_y == last[1]))
+        for x in range(SIDE):
+            codes[pl.ds(2 * x + 1 - high, 1), :] = own[160 + x : 161 + x, :]
+            codes[pl.ds(2 * x + high, 1), :] = recv[160 + x : 161 + x, :]
         for first, count in ((0, 8), (8, 2)):
             row = iota((2 * count, LANES), 0)
             inside = inside_x(lax.shift_right_logical(row, 1) + first, last)
@@ -478,11 +486,12 @@
             found = []
             for h in range(2):
                 sums = []
-                for c in range(CHANNELS):
+                for c in range(8):
                     at = y_face_row(c, first)
                     rows = slice(at, at + 2 * count)
                     sums.append(own[rows, half(h)] + recv[rows, half(h)])
-                found.append(node_speeds(sums[:8], sums[8], inside))
+                code = codes[2 * first : 2 * (first + count), half(h)]
+                found.append(node_speeds(sums, code, inside))
             for c in range(3):
                 ready = tiles(*([found[h][f][c] for h in range(2)] for f in range(2)))
                 for j in range(5):
@@ -517,10 +526,10 @@
                 along_z[c] = moment if q == 0 else along_z[c] + moment
         place = slice(slot * 8, slot * 8 + 8)
         for c in range(3):
-            partial[4 * c, place, :] = speed[c]
-            partial[4 * c + 1, place, :] = along_x[c]
-            partial[4 * c + 2, place, :] = speed[c] * dy
-            partial[4 * c + 3, place, :] = along_z[c]
+            partial[chunk, 4 * c, place, :] = speed[c]
+            partial[chunk, 4 * c + 1, place, :] = along_x[c]
+            partial[chunk, 4 * c + 2, place, :] = speed[c] * dy
+            partial[chunk, 4 * c + 3, place, :] = along_z[c]
 
     ready = (new_velocity, new_affine, new_deform, new_stress)
     finals = (velocity_out, affine_out, deform_out, stress_out)
@@ -532,12 +541,12 @@
             for i, (src, dst) in enumerate(zip(ready, finals))
         ]
 
-    def step(chunk, carry):
+    def step(chunk):
         for slot in range(CHUNK):
             one(chunk, slot)
         slots = chunk_of(chunk)
         live = table[LIVE, slots, :]
-        total = [(gathered[k, slots, :] + collect(partial, k)) * live for k in range(12)]
+        total = [(gathered[k, slots, :] + collect(partial.at[chunk], k)) * live for k in range(12)]
         moved = []
         for c in range(3):
             new_velocity[c, slots, :] = total[4 * c]
@@ -560,9 +569,9 @@
             new_stress[k, slots, :] = stress[entry] * live
         for send in sends(chunk):
             send.start()
-        return carry
-
-    lax.fori_loop(0, SLOTS // CHUNK, step, 0)
+
+    for chunk in range(SLOTS // CHUNK):
+        step(chunk)
     for chunk in range(SLOTS // CHUNK):
         for send in sends(chunk):
             send.wait()
@@ -590,7 +599,8 @@
     smem = pl.BlockSpec(memory_space=pltpu.SMEM)
     hbm = pl.BlockSpec(memory_space=pltpu.HBM)
     whole = pl.BlockSpec(memory_space=pltpu.VMEM)
-    face = jax.ShapeDtypeStruct((FACE_ROWS, DEPTH), F32)
+    x_face = jax.ShapeDtypeStruct((X_FACE_ROWS, DEPTH), F32)
+    y_face = jax.ShapeDtypeStruct((Y_FACE_ROWS, DEPTH), F32)
     right_shape = jax.ShapeDtypeStruct((SLOTS, LANES, 256), BF16)
     last = (lax.axis_size("gx") - 1, lax.axis_size("gy") - 1)
     inputs = (
@@ -612,7 +622,7 @@
         first_kernel,
         out_shape=(
             halves_shape,
-            face,
+            x_face,
             jax.ShapeDtypeStruct((GATHER_ROWS, 32, LANES), F32),
             jax.ShapeDtypeStruct((SCATTER_ROWS - GATHER_ROWS, 32, LANES), F32),
             jax.ShapeDtypeStruct((1, SLOTS), jnp.int32),
@@ -632,7 +642,7 @@
     got_x_d = swap_pairs(x_d, "gx", 1)
     halves, x_a = pl.pallas_call(
         second_kernel,
-        out_shape=(halves_shape, face),
+        out_shape=(halves_shape, x_face),
         in_specs=[smem] + [whole] * 3,
         out_specs=(whole,) * 2,
         scratch_shapes=scatter_scratch,
@@ -653,7 +663,7 @@
     )(x_a, tile_numbers, table)
     y_a, y_d, edge = pl.pallas_call(
         corner_kernel,
-        out_shape=(face, face, jax.ShapeDtypeStruct((CHANNELS, 4, 16, DEPTH), F32)),
+        out_shape=(y_face, y_face, jax.ShapeDtypeStruct((CHANNELS, 4, 16, DEPTH), F32)),
         in_specs=[anywhere] + [whole] * 3,
         out_specs=(whole,) * 3,
         compiler_params=params,
@@ -681,7 +691,7 @@
         out_shape=tuple(jax.ShapeDtypeStruct((k, slots, particles), F32) for k in (3, 9, 9, 6)),
         in_specs=[smem] + [whole] * 8,
         out_specs=(hbm,) * 4,
-        scratch_shapes=[vmem((2, 5, 3, 24, LANES)), vmem((12, 8 * CHUNK, LANES))]
+        scratch_shapes=[vmem((2, 5, 3, 24, LANES)), vmem((24, DEPTH)), vmem((SLOTS // CHUNK, 12, 8 * CHUNK, LANES))]
         + [vmem((k, slots, particles)) for k in (3, 9, 9, 6)]
         + [pltpu.SemaphoreType.DMA((SLOTS // CHUNK, 4))],
         compiler_params=params,

time: 31.2 us -> 30.4 us (0.974)
  Pallas kernels: 13.4 us -> 12.6 us
    pallas_call x1, Pallas kernels: 2.87 us -> 2.45 us  [per_device(): pl.pallas_call(functools.partial(gather_kernel, last), out_shape=tuple((j...]
    pallas_call x3, Pallas kernels: 6.16 us -> 5.82 us  [the longest x1 3.35 us: per_device(): pl.pallas_call(first_kernel, out_shape=(halves_shape, x_face, jax.ShapeDt...]
where the time goes in v6:
time: 30.4 us; the launch traced here: 30.2 us
  Pallas kernels  12.6 us (41%)
  starting transfers between devices  11.5 us (38%)
  waiting for transfers between devices  4.72 us (16%)
  between operations  1.36 us (4%)
    ppermute x4, starting transfers between devices, swap_pairs(): lax.ppermute(block, axis, [(i, k) for i, k in route if 0 <= k < size])  11.5 us
    ppermute x4, waiting for transfers between devices, swap_pairs(): lax.ppermute(block, axis, [(i, k) for i, k in route if 0 <= k < size])  4.72 us
    pallas_call x1, Pallas kernels, per_device(): pl.pallas_call(functools.partial(middle_kernel, last), out_shape=jax.Shap...  3.5 us
    pallas_call x1, Pallas kernels, per_device(): pl.pallas_call(first_kernel, out_shape=(halves_shape, x_face, jax.ShapeDt...  3.35 us
    pallas_call x1, Pallas kernels, per_device(): pl.pallas_call(functools.partial(gather_kernel, last), out_shape=tuple((j...  2.45 us
    pallas_call x1, Pallas kernels, per_device(): pl.pallas_call(second_kernel, out_shape=(halves_shape, x_face), in_specs=...  2.15 us
    pallas_call x1, Pallas kernels, per_device(): pl.pallas_call(prepare_kernel, out_shape=right_shape, in_specs=[anywhere,...  0.83 us
  transfers between devices with their start and end apart: 4, of which 2 were waited for; matrix products, arithmetic and copies ran while one was open for 0% of the time, Pallas kernels for 14%

profile of v6, /device:TPU:6, one launch (start us, length us, event | category | flops | bytes accessed | tf_op | source)
XLA Modules:
  0.0 30.2 jit_solution(6939999685573926037)
XLA Ops:
  1.3 3.4 %scatter_first.1 = (f32[2,9,6,16,256]{4,3,2,1,0:T(8,128)S(1)}, f32[184,256]{1,0:T(8,128)S(1)}, f32[12,32,128]{2,1,0:T(8,128)S(1)}, f32[13,32,128]{2,1,0:T(8,128)S(1)}, s32[1,24]{1,0:T(1,128)S(1)}) custom-call(s32[1,1]{1,0:T(1,128)S(6)} %copy.16.count_ref, s32[24]{0:T(128)} %tile_in.1, f32[3,24,128]{2,1,0:T(8,128)} %offset_in.1, f32[24,128]{1,0:T(8,128)} %mass_in.1, ...), custom_call_target="tpu_custom_call" | custom-call | flops 3000000 | bytes 4000000 | tf_op jit(solution)/shard_map/scatter_first/pallas_call | solution.py:621
  4.6 2.2 %scatter_second.1 = (f32[2,9,6,16,256]{4,3,2,1,0:T(8,128)S(1)}, f32[184,256]{1,0:T(8,128)S(1)}) custom-call(s32[1,24]{1,0:T(1,128)S(1)} %get-tuple-element.14.tile_ref, f32[2,9,6,16,256]{4,3,2,1,0:T(8,128)S(1)} %get-tuple-element.15.half_in, f32[12,32,128]{2,1,0:T(8,128)S(1)} %get-tuple-element.16.table, ...), custom_call_target="tpu_custom_call", output_to_operand_aliasing={{0}: (1, {})} | custom-call | flops 3000000 | bytes 4000000 | tf_op jit(solution)/shard_map/scatter_second/pallas_call | solution.py:643
  6.8 0.1 collective-permute-start
  6.9 6.3 %collective-permute-start.1 = (f32[184,256]{1,0:T(8,128)S(1)}, f32[184,256]{1,0:T(8,128)S(1)}, u32[]{:S(2)}, u32[]{:S(2)}) collective-permute-start(f32[184,256]{1,0:T(8,128)S(1)} %get-tuple-element.20), channel_id=1, source_target_pairs={{8,16},{16,8},{24,32},{32,24},{40,48},{48,40},{56,64},{64,56},{72,... | collective-permute-start | bytes 565256 | tf_op jit(solution)/shard_map/ppermute | solution.py:591
  13.2 0.8 %prepare.1.order.right = bf16[24,128,256]{2,1,0:T(8,128)(2,1)S(1)} custom-call(f32[184,256]{1,0:T(8,128)S(1)} %get-tuple-element.18.order, s32[1,24]{1,0:T(1,128)S(1)} %get-tuple-element.14.tile_ref, f32[12,32,128]{2,1,0:T(8,128)S(1)} %get-tuple-element.16.table), custom_call_target="tpu_custom_call" | custom-call | flops 3000000 | bytes 4000000 | tf_op jit(solution)/shard_map/prepare/pallas_call | solution.py:655
  14.0 0.0 collective-permute-done.recv_a
  14.0 2.4 %collective-permute-done.1.recv_d = f32[184,256]{1,0:T(8,128)S(1)} collective-permute-done((f32[184,256]{1,0:T(8,128)S(1)}, f32[184,256]{1,0:T(8,128)S(1)}, u32[]{:S(2)}, u32[]{:S(2)}) %collective-permute-start.1) | collective-permute-done | bytes 188448 | tf_op jit(solution)/shard_map/ppermute | solution.py:591
  16.4 0.3 %corners.1 = (f32[176,256]{1,0:T(8,128)S(1)}, f32[176,256]{1,0:T(8,128)S(1)}, f32[9,4,16,256]{3,2,1,0:T(8,128)S(1)}) custom-call(bf16[24,128,256]{2,1,0:T(8,128)(2,1)S(1)} %prepare.1.order.right, f32[2,9,6,16,256]{4,3,2,1,0:T(8,128)S(1)} %get-tuple-element.19.halves, f32[184,256]{1,0:T(8,128)S(1)} %collective-permute-done.recv_a, ...), custom_call_target="tpu_custom_call" | custom-call | tf_op jit(solution)/shard_map/corners/pallas_call | solution.py:664
  16.8 5.1 %collective-permute-start.3 = (f32[176,256]{1,0:T(8,128)S(1)}, f32[176,256]{1,0:T(8,128)S(1)}, u32[]{:S(2)}, u32[]{:S(2)}) collective-permute-start(f32[176,256]{1,0:T(8,128)S(1)} %get-tuple-element.23.own_d), channel_id=1, source_target_pairs={{1,2},{2,1},{3,4},{4,3},{5,6},{6,5},{9,10},{10,9},{11,12},{12,11},... | collective-permute-start | bytes 540680 | tf_op jit(solution)/shard_map/ppermute | solution.py:591
  21.9 0.1 collective-permute-start.2
  21.9 0.0 copy-start
  22.0 3.5 %middle.1.gathered = f32[12,24,128]{2,1,0:T(8,128)S(1)} custom-call(f32[176,256]{1,0:T(8,128)S(1)} %get-tuple-element.21.order.own_a, s32[1,24]{1,0:T(1,128)S(1)} %get-tuple-element.14.tile_ref, f32[2,9,6,16,256]{4,3,2,1,0:T(8,128)S(1)} %get-tuple-element.19.halves, f32[9,4,16,256]{3,2,1,0:T(8,128)S(1)} %get-tuple-element.22.edge, ...), custom_call_target="tpu_custom_call" | custom-call | flops 3000000 | bytes 4000000 | tf_op jit(solution)/shard_map/middle/pallas_call | solution.py:675
  25.5 2.3 %collective-permute-done.3.y_d = f32[176,256]{1,0:T(8,128)S(1)} collective-permute-done((f32[176,256]{1,0:T(8,128)S(1)}, f32[176,256]{1,0:T(8,128)S(1)}, u32[]{:S(2)}, u32[]{:S(2)}) %collective-permute-start.3) | collective-permute-done | bytes 180256 | tf_op jit(solution)/shard_map/ppermute | solution.py:591
  27.8 0.0 collective-permute-done.2.y_a
  27.8 0.0 copy-done
  27.8 2.4 %gather.1 = (f32[3,24,128]{2,1,0:T(8,128)}, f32[9,24,128]{2,1,0:T(8,128)}, f32[9,24,128]{2,1,0:T(8,128)}, f32[6,24,128]{2,1,0:T(8,128)}) custom-call(s32[1,24]{1,0:T(1,128)S(1)} %get-tuple-element.14.tile_ref, f32[12,24,128]{2,1,0:T(8,128)S(1)} %middle.1.gathered, f32[176,256]{1,0:T(8,128)S(1)} %get-tuple-element.21.order.own_a, ...), custom_call_target="tpu_custom_call" | custom-call | tf_op jit(solution)/shard_map/gather/pallas_call | solution.py:689
Async XLA Ops:
  6.8 7.2 %collective-permute-start = (f32[184,256]{1,0:T(8,128)S(1)}, f32[184,256]{1,0:T(8,128)S(1)}, u32[]{:S(2)}, u32[]{:S(2)}) collective-permute-start(f32[184,256]{1,0:T(8,128)S(1)} %get-tuple-element.18.order), channel_id=1, source_target_pairs={{0,8},{8,0},{16,24},{24,16},{32,40},{40,32},{48,56},{56,48},{64,72... | collective-permute-start | bytes 565256 | tf_op jit(solution)/shard_map/ppermute | solution.py:591
  6.9 9.6 %collective-permute-start.1 = (f32[184,256]{1,0:T(8,128)S(1)}, f32[184,256]{1,0:T(8,128)S(1)}, u32[]{:S(2)}, u32[]{:S(2)}) collective-permute-start(f32[184,256]{1,0:T(8,128)S(1)} %get-tuple-element.20), channel_id=1, source_target_pairs={{8,16},{16,8},{24,32},{32,24},{40,48},{48,40},{56,64},{64,56},{72,... | collective-permute-start | bytes 565256 | tf_op jit(solution)/shard_map/ppermute | solution.py:591
  16.8 11.0 %collective-permute-start.3 = (f32[176,256]{1,0:T(8,128)S(1)}, f32[176,256]{1,0:T(8,128)S(1)}, u32[]{:S(2)}, u32[]{:S(2)}) collective-permute-start(f32[176,256]{1,0:T(8,128)S(1)} %get-tuple-element.23.own_d), channel_id=1, source_target_pairs={{1,2},{2,1},{3,4},{4,3},{5,6},{6,5},{9,10},{10,9},{11,12},{12,11},... | collective-permute-start | bytes 540680 | tf_op jit(solution)/shard_map/ppermute | solution.py:591
  21.9 5.9 %collective-permute-start.2 = (f32[176,256]{1,0:T(8,128)S(1)}, f32[176,256]{1,0:T(8,128)S(1)}, u32[]{:S(2)}, u32[]{:S(2)}) collective-permute-start(f32[176,256]{1,0:T(8,128)S(1)} %get-tuple-element.21.order.own_a), channel_id=1, source_target_pairs={{0,1},{1,0},{2,3},{3,2},{4,5},{5,4},{6,7},{7,6},{8,9},{9,8},{10,11... | collective-permute-start | bytes 540680 | tf_op jit(solution)/shard_map/ppermute | solution.py:591
  21.9 5.8 %copy-start = (f32[9,24,128]{2,1,0:T(8,128)S(1)}, f32[9,24,128]{2,1,0:T(8,128)}, u32[]{:S(2)}) copy-start(f32[9,24,128]{2,1,0:T(8,128)} %deform.1) | copy-start | bytes 331780

commit v7 on v6

--- a/solution.py
+++ b/solution.py
@@ -261,7 +261,7 @@
     )
 
 
-def prepare_kernel(order, tile_ref, table, right):
+def prepare_kernel(order, tile_ref, table, right, edge_weights):
     none = jnp.zeros((16, 2 * LANES), BF16)
 
     def one(s, carry):
@@ -273,6 +273,12 @@
             hi, lo = split(jnp.concatenate([wz * mask, mz * mask], 1))
             for k, rows in enumerate((hi, lo, hi, none)):
                 right[s, 64 * f + 16 * k : 64 * f + 16 * k + 16, :] = rows
+        sublane = iota((8, LANES), 0)
+        tile_y = lax.shift_right_logical(tile_ref[0, s], 5) & 1
+        wy = spline(((sublane & 1) + 4 * tile_y).astype(F32) - table[POS_Y, pl.ds(s, 1), :])
+        for q in range(2):
+            dx = (lax.shift_right_logical(sublane, 1) + 4 * q).astype(F32)
+            edge_weights[s, q] = wy * spline(dx - table[POS_X, pl.ds(s, 1), :])
         return carry
 
     lax.fori_loop(0, SLOTS, one, 0, unroll=2)
@@ -303,9 +309,10 @@
                 at = c * 2 + p
                 own = (high, c, 4 * high + p)
                 to = (c, 2 * high + p)
-                edge[(*to, slice(0, 8))] = halves[(*own, slice(0, 8))] + recv[at * 8 : at * 8 + 8]
-                edge[(*to, slice(8, 16))] = halves[(*own, slice(8, 16))]
-                edge[(*to, slice(8, 10))] += recv[144 + at * 2 : 146 + at * 2]
+                edge[(*to, slice(0, 2))] = halves[(*own, slice(0, 2))] + recv[at * 8 : at * 8 + 2]
+                edge[(*to, slice(8, 10))] = (
+                    halves[(*own, slice(8, 10))] + recv[144 + at * 2 : 146 + at * 2]
+                )
     for face, high in ((face_a, 1 - side_y), (face_d, side_y)):
         rows = pl.ds(pl.multiple_of(high * 8, 8), 2)
         for c in range(8):
@@ -405,11 +412,16 @@
 
 
 def middle_kernel(
-    last, order, tile_ref, halves, edge, table, right, gathered, work, nodes, partial,
+    last, order, tile_ref, halves, x_a, x_d, table, right, gathered, work, nodes, partial,
 ):
+    side_x = low_side("gx")
     for c in range(CHANNELS):
-        for x in range(SIDE):
-            work[c, x] = plane(halves, edge, c, x, slice(0, 8))
+        for x in range(2, SIDE - 2):
+            work[c, x] = plane(halves, None, c, x, slice(0, 8))
+        for recv, high in ((x_a, 1 - side_x), (x_d, side_x)):
+            for p in range(2):
+                at = (c * 2 + p) * 8
+                work[c, 8 * high + p] = halves[high, c, 4 * high + p, 0:8, :] + recv[at : at + 8]
     inner = iota((8, LANES), 0) >= 2
 
     def node_step(x, carry):
@@ -468,7 +480,7 @@
 
 
 def gather_kernel(
-    last, tile_ref, gathered, own_a, own_d, y_a, y_d, table, right, deform,
+    last, tile_ref, gathered, own_a, own_d, y_a, y_d, table, right, edge_weights, deform,
     velocity_out, affine_out, deform_out, stress_out,
     nodes, codes, partial, new_velocity, new_affine, new_deform, new_stress, sems,
 ):
@@ -512,11 +524,10 @@
         summed = matmul(z_window(jnp.concatenate(left, 0), shift), right[s])
         sublane = iota((8, LANES), 0)
         dy = ((sublane & 1) + 4 * tile_y).astype(F32) - row(POS_Y)
-        wy = spline(dy)
         speed, along_x, along_z = [None] * 3, [None] * 3, [None] * 3
         for q in range(2):
             dx = (lax.shift_right_logical(sublane, 1) + 4 * q).astype(F32) - row(POS_X)
-            weight = wy * spline(dx)
+            weight = edge_weights[s, q]
             for c in range(3):
                 at = c * 16 + q * 8
                 part = weight * summed[at : at + 8, 0:LANES]
@@ -652,20 +663,21 @@
         name="scatter_second",
     )(tile_numbers, halves, table, rows)
     got_x_a = swap_pairs(x_a, "gx", 0)
-    right = pl.pallas_call(
+    right, edge_weights = pl.pallas_call(
         prepare_kernel,
-        out_shape=right_shape,
+        out_shape=(right_shape, jax.ShapeDtypeStruct((SLOTS, 2, 8, LANES), F32)),
         in_specs=[anywhere, smem, whole],
-        out_specs=whole,
+        out_specs=(whole,) * 2,
         compiler_params=params,
         cost_estimate=cost(3000000),
         name="prepare",
     )(x_a, tile_numbers, table)
-    y_a, y_d, edge = pl.pallas_call(
+    y_a, y_d = pl.pallas_call(
         corner_kernel,
-        out_shape=(y_face, y_face, jax.ShapeDtypeStruct((CHANNELS, 4, 16, DEPTH), F32)),
+        out_shape=(y_face, y_face),
         in_specs=[anywhere] + [whole] * 3,
-        out_specs=(whole,) * 3,
+        out_specs=(whole,) * 2,
+        scratch_shapes=[vmem((CHANNELS, 4, 16, DEPTH))],
         compiler_params=params,
         name="corners",
     )(right, halves, got_x_a, got_x_d)
@@ -675,7 +687,7 @@
     gathered = pl.pallas_call(
         functools.partial(middle_kernel, last),
         out_shape=jax.ShapeDtypeStruct((12, slots, particles), F32),
-        in_specs=[anywhere, smem] + [whole] * 4,
+        in_specs=[anywhere, smem] + [whole] * 5,
         out_specs=whole,
         scratch_shapes=[
             vmem((CHANNELS, SIDE, 8, DEPTH)),
@@ -685,18 +697,20 @@
         compiler_params=params,
         cost_estimate=cost(3000000),
         name="middle",
-    )(y_a, tile_numbers, halves, edge, table, right)
+    )(y_a, tile_numbers, halves, got_x_a, got_x_d, table, right)
     return pl.pallas_call(
         functools.partial(gather_kernel, last),
         out_shape=tuple(jax.ShapeDtypeStruct((k, slots, particles), F32) for k in (3, 9, 9, 6)),
-        in_specs=[smem] + [whole] * 8,
+        in_specs=[smem] + [whole] * 9,
         out_specs=(hbm,) * 4,
         scratch_shapes=[vmem((2, 5, 3, 24, LANES)), vmem((24, DEPTH)), vmem((SLOTS // CHUNK, 12, 8 * CHUNK, LANES))]
         + [vmem((k, slots, particles)) for k in (3, 9, 9, 6)]
         + [pltpu.SemaphoreType.DMA((SLOTS // CHUNK, 4))],
         compiler_params=params,
         name="gather",
-    )(tile_numbers, gathered, y_a, y_d, got_y_a, got_y_d, table, right, deform)
+    )(
+        tile_numbers, gathered, y_a, y_d, got_y_a, got_y_d, table, right, edge_weights, deform
+    )
 
 
 def solution(mesh):

time: 30.4 us -> 30.3 us (level)
  transfers between devices with their start and end apart: 4 -> 4, of which waited for: 2 -> 2; matrix products, arithmetic and copies ran while one was open for 0% -> 0% of each run, Pallas kernels for 14% -> 15%
where the time goes in v7:
time: 30.3 us; the launch traced here: 30.2 us
  Pallas kernels  12.7 us (42%)
  starting transfers between devices  11.5 us (38%)
  waiting for transfers between devices  4.58 us (15%)
  between operations  1.36 us (4%)
    ppermute x4, starting transfers between devices, swap_pairs(): lax.ppermute(block, axis, [(i, k) for i, k in route if 0 <= k < size])  11.5 us
    ppermute x4, waiting for transfers between devices, swap_pairs(): lax.ppermute(block, axis, [(i, k) for i, k in route if 0 <= k < size])  4.58 us
    pallas_call x1, Pallas kernels, per_device(): pl.pallas_call(functools.partial(middle_kernel, last), out_shape=jax.Shap...  3.52 us
    pallas_call x1, Pallas kernels, per_device(): pl.pallas_call(first_kernel, out_shape=(halves_shape, x_face, jax.ShapeDt...  3.35 us
    pallas_call x1, Pallas kernels, per_device(): pl.pallas_call(functools.partial(gather_kernel, last), out_shape=tuple((j...  2.44 us
    pallas_call x1, Pallas kernels, per_device(): pl.pallas_call(second_kernel, out_shape=(halves_shape, x_face), in_specs=...  2.15 us
    pallas_call x1, Pallas kernels, per_device(): pl.pallas_call(prepare_kernel, out_shape=(right_shape, jax.ShapeDtypeStru...  0.93 us
  transfers between devices with their start and end apart: 4, of which 2 were waited for; matrix products, arithmetic and copies ran while one was open for 0% of the time, Pallas kernels for 15%

profile of v7, /device:TPU:6, one launch (start us, length us, event | category | flops | bytes accessed | tf_op | source)
XLA Modules:
  0.0 30.2 jit_solution(176019611251264782)
XLA Ops:
  1.3 3.4 %scatter_first.1 = (f32[2,9,6,16,256]{4,3,2,1,0:T(8,128)S(1)}, f32[184,256]{1,0:T(8,128)S(1)}, f32[12,32,128]{2,1,0:T(8,128)S(1)}, f32[13,32,128]{2,1,0:T(8,128)S(1)}, s32[1,24]{1,0:T(1,128)S(1)}) custom-call(s32[1,1]{1,0:T(1,128)S(6)} %copy.16.count_ref, s32[24]{0:T(128)} %tile_in.1, f32[3,24,128]{2,1,0:T(8,128)} %offset_in.1, f32[24,128]{1,0:T(8,128)} %mass_in.1, ...), custom_call_target="tpu_custom_call" | custom-call | flops 3000000 | bytes 4000000 | tf_op jit(solution)/shard_map/scatter_first/pallas_call | solution.py:632
  4.6 2.2 %scatter_second.1 = (f32[2,9,6,16,256]{4,3,2,1,0:T(8,128)S(1)}, f32[184,256]{1,0:T(8,128)S(1)}) custom-call(s32[1,24]{1,0:T(1,128)S(1)} %get-tuple-element.15.tile_ref, f32[2,9,6,16,256]{4,3,2,1,0:T(8,128)S(1)} %get-tuple-element.16.half_in, f32[12,32,128]{2,1,0:T(8,128)S(1)} %get-tuple-element.17.table, ...), custom_call_target="tpu_custom_call", output_to_operand_aliasing={{0}: (1, {})} | custom-call | flops 3000000 | bytes 4000000 | tf_op jit(solution)/shard_map/scatter_second/pallas_call | solution.py:654
  6.8 0.1 collective-permute-start
  6.9 6.3 %collective-permute-start.1 = (f32[184,256]{1,0:T(8,128)S(1)}, f32[184,256]{1,0:T(8,128)S(1)}, u32[]{:S(2)}, u32[]{:S(2)}) collective-permute-start(f32[184,256]{1,0:T(8,128)S(1)} %get-tuple-element.22), channel_id=1, source_target_pairs={{8,16},{16,8},{24,32},{32,24},{40,48},{48,40},{56,64},{64,56},{72,... | collective-permute-start | bytes 565256 | tf_op jit(solution)/shard_map/ppermute | solution.py:602
  13.2 0.9 %prepare.1 = (bf16[24,128,256]{2,1,0:T(8,128)(2,1)S(1)}, f32[24,2,8,128]{3,2,1,0:T(8,128)S(1)}) custom-call(f32[184,256]{1,0:T(8,128)S(1)} %get-tuple-element.19.order, s32[1,24]{1,0:T(1,128)S(1)} %get-tuple-element.15.tile_ref, f32[12,32,128]{2,1,0:T(8,128)S(1)} %get-tuple-element.17.table), custom_call_target="tpu_custom_call" | custom-call | flops 3000000 | bytes 4000000 | tf_op jit(solution)/shard_map/prepare/pallas_call | solution.py:666
  14.1 0.0 collective-permute-done.recv_a.x_a
  14.1 2.3 %collective-permute-done.1.recv_d.x_d = f32[184,256]{1,0:T(8,128)S(1)} collective-permute-done((f32[184,256]{1,0:T(8,128)S(1)}, f32[184,256]{1,0:T(8,128)S(1)}, u32[]{:S(2)}, u32[]{:S(2)}) %collective-permute-start.1) | collective-permute-done | bytes 188448 | tf_op jit(solution)/shard_map/ppermute | solution.py:602
  16.4 0.3 corners.1
  16.7 5.1 %collective-permute-start.3 = (f32[176,256]{1,0:T(8,128)S(1)}, f32[176,256]{1,0:T(8,128)S(1)}, u32[]{:S(2)}, u32[]{:S(2)}) collective-permute-start(f32[176,256]{1,0:T(8,128)S(1)} %get-tuple-element.24.own_d), channel_id=1, source_target_pairs={{1,2},{2,1},{3,4},{4,3},{5,6},{6,5},{9,10},{10,9},{11,12},{12,11},... | collective-permute-start | bytes 540680 | tf_op jit(solution)/shard_map/ppermute | solution.py:602
  21.8 0.0 copy-start
  21.8 0.1 collective-permute-start.2
  21.9 3.5 %middle.1.gathered = f32[12,24,128]{2,1,0:T(8,128)S(1)} custom-call(f32[176,256]{1,0:T(8,128)S(1)} %get-tuple-element.23.order.own_a, s32[1,24]{1,0:T(1,128)S(1)} %get-tuple-element.15.tile_ref, f32[2,9,6,16,256]{4,3,2,1,0:T(8,128)S(1)} %get-tuple-element.21.halves, f32[184,256]{1,0:T(8,128)S(1)} %collective-permute-done.recv_a.x_a, ...), custom_call_target="tpu_custom_call" | custom-call | flops 3000000 | bytes 4000000 | tf_op jit(solution)/shard_map/middle/pallas_call | solution.py:687
  25.4 2.3 %collective-permute-done.3.y_d = f32[176,256]{1,0:T(8,128)S(1)} collective-permute-done((f32[176,256]{1,0:T(8,128)S(1)}, f32[176,256]{1,0:T(8,128)S(1)}, u32[]{:S(2)}, u32[]{:S(2)}) %collective-permute-start.3) | collective-permute-done | bytes 180256 | tf_op jit(solution)/shard_map/ppermute | solution.py:602
  27.7 0.0 collective-permute-done.2.y_a
  27.7 0.0 copy-done
  27.7 2.4 %gather.1 = (f32[3,24,128]{2,1,0:T(8,128)}, f32[9,24,128]{2,1,0:T(8,128)}, f32[9,24,128]{2,1,0:T(8,128)}, f32[6,24,128]{2,1,0:T(8,128)}) custom-call(s32[1,24]{1,0:T(1,128)S(1)} %get-tuple-element.15.tile_ref, f32[12,24,128]{2,1,0:T(8,128)S(1)} %middle.1.gathered, f32[176,256]{1,0:T(8,128)S(1)} %get-tuple-element.23.order.own_a, ...), custom_call_target="tpu_custom_call" | custom-call | tf_op jit(solution)/shard_map/gather/pallas_call | solution.py:701
Async XLA Ops:
  6.8 7.3 %collective-permute-start = (f32[184,256]{1,0:T(8,128)S(1)}, f32[184,256]{1,0:T(8,128)S(1)}, u32[]{:S(2)}, u32[]{:S(2)}) collective-permute-start(f32[184,256]{1,0:T(8,128)S(1)} %get-tuple-element.19.order), channel_id=1, source_target_pairs={{0,8},{8,0},{16,24},{24,16},{32,40},{40,32},{48,56},{56,48},{64,72... | collective-permute-start | bytes 565256 | tf_op jit(solution)/shard_map/ppermute | solution.py:602
  6.9 9.6 %collective-permute-start.1 = (f32[184,256]{1,0:T(8,128)S(1)}, f32[184,256]{1,0:T(8,128)S(1)}, u32[]{:S(2)}, u32[]{:S(2)}) collective-permute-start(f32[184,256]{1,0:T(8,128)S(1)} %get-tuple-element.22), channel_id=1, source_target_pairs={{8,16},{16,8},{24,32},{32,24},{40,48},{48,40},{56,64},{64,56},{72,... | collective-permute-start | bytes 565256 | tf_op jit(solution)/shard_map/ppermute | solution.py:602
  16.7 11.0 %collective-permute-start.3 = (f32[176,256]{1,0:T(8,128)S(1)}, f32[176,256]{1,0:T(8,128)S(1)}, u32[]{:S(2)}, u32[]{:S(2)}) collective-permute-start(f32[176,256]{1,0:T(8,128)S(1)} %get-tuple-element.24.own_d), channel_id=1, source_target_pairs={{1,2},{2,1},{3,4},{4,3},{5,6},{6,5},{9,10},{10,9},{11,12},{12,11},... | collective-permute-start | bytes 540680 | tf_op jit(solution)/shard_map/ppermute | solution.py:602
  21.8 5.9 %copy-start = (f32[9,24,128]{2,1,0:T(8,128)S(1)}, f32[9,24,128]{2,1,0:T(8,128)}, u32[]{:S(2)}) copy-start(f32[9,24,128]{2,1,0:T(8,128)} %deform.1) | copy-start | bytes 331780
  21.8 5.9 %collective-permute-start.2 = (f32[176,256]{1,0:T(8,128)S(1)}, f32[176,256]{1,0:T(8,128)S(1)}, u32[]{:S(2)}, u32[]{:S(2)}) collective-permute-start(f32[176,256]{1,0:T(8,128)S(1)} %get-tuple-element.23.order.own_a), channel_id=1, source_target_pairs={{0,1},{1,0},{2,3},{3,2},{4,5},{5,4},{6,7},{7,6},{8,9},{9,8},{10,11... | collective-permute-start | bytes 540680 | tf_op jit(solution)/shard_map/ppermute | solution.py:602

commit v8 on v7

--- a/solution.py
+++ b/solution.py
@@ -171,7 +171,15 @@
             one(group * UNROLL + u, u)
         return carry
 
-    lax.fori_loop(0, lax.div(count + UNROLL - 1, UNROLL), step, 0)
+    groups = lax.shift_right_logical(count + 1, 2)
+    lax.fori_loop(0, groups, step, 0)
+
+    def pair(k, carry):
+        for u in range(2):
+            one(groups * UNROLL + u, u)
+        return carry
+
+    lax.fori_loop(0, lax.shift_right_logical(count - groups * UNROLL + 1, 1), pair, 0)
 
     for ty in range(2):
         for f in range(2):

time: 30.3 us -> 30.2 us (level)
  no operation moved by 1% of the time
where the time goes in v8:
time: 30.2 us; the launch traced here: 30 us
  Pallas kernels  12.4 us (41%)
  starting transfers between devices  11.8 us (39%)
  waiting for transfers between devices  4.45 us (15%)
  between operations  1.36 us (5%)
    ppermute x4, starting transfers between devices, swap_pairs(): lax.ppermute(block, axis, [(i, k) for i, k in route if 0 <= k < size])  11.8 us
    ppermute x4, waiting for transfers between devices, swap_pairs(): lax.ppermute(block, axis, [(i, k) for i, k in route if 0 <= k < size])  4.45 us
    pallas_call x1, Pallas kernels, per_device(): pl.pallas_call(functools.partial(middle_kernel, last), out_shape=jax.Shap...  3.52 us
    pallas_call x1, Pallas kernels, per_device(): pl.pallas_call(first_kernel, out_shape=(halves_shape, x_face, jax.ShapeDt...  3.23 us
    pallas_call x1, Pallas kernels, per_device(): pl.pallas_call(functools.partial(gather_kernel, last), out_shape=tuple((j...  2.44 us
    pallas_call x1, Pallas kernels, per_device(): pl.pallas_call(second_kernel, out_shape=(halves_shape, x_face), in_specs=...  2.03 us
    pallas_call x1, Pallas kernels, per_device(): pl.pallas_call(prepare_kernel, out_shape=(right_shape, jax.ShapeDtypeStru...  0.93 us
  transfers between devices with their start and end apart: 4, of which 2 were waited for; matrix products, arithmetic and copies ran while one was open for 0% of the time, Pallas kernels for 15%

profile of v8, /device:TPU:6, one launch (start us, length us, event | category | flops | bytes accessed | tf_op | source)
XLA Modules:
  0.0 30.0 jit_solution(14332979747082254801)
XLA Ops:
  1.3 3.2 %scatter_first.1 = (f32[2,9,6,16,256]{4,3,2,1,0:T(8,128)S(1)}, f32[184,256]{1,0:T(8,128)S(1)}, f32[12,32,128]{2,1,0:T(8,128)S(1)}, f32[13,32,128]{2,1,0:T(8,128)S(1)}, s32[1,24]{1,0:T(1,128)S(1)}) custom-call(s32[1,1]{1,0:T(1,128)S(6)} %copy.16.count_ref, s32[24]{0:T(128)} %tile_in.1, f32[3,24,128]{2,1,0:T(8,128)} %offset_in.1, f32[24,128]{1,0:T(8,128)} %mass_in.1, ...), custom_call_target="tpu_custom_call" | custom-call | flops 3000000 | bytes 4000000 | tf_op jit(solution)/shard_map/scatter_first/pallas_call | solution.py:640
  4.5 2.0 %scatter_second.1 = (f32[2,9,6,16,256]{4,3,2,1,0:T(8,128)S(1)}, f32[184,256]{1,0:T(8,128)S(1)}) custom-call(s32[1,24]{1,0:T(1,128)S(1)} %get-tuple-element.15.tile_ref, f32[2,9,6,16,256]{4,3,2,1,0:T(8,128)S(1)} %get-tuple-element.16.half_in, f32[12,32,128]{2,1,0:T(8,128)S(1)} %get-tuple-element.17.table, ...), custom_call_target="tpu_custom_call", output_to_operand_aliasing={{0}: (1, {})} | custom-call | flops 3000000 | bytes 4000000 | tf_op jit(solution)/shard_map/scatter_second/pallas_call | solution.py:662
  6.6 0.1 collective-permute-start
  6.7 6.4 %collective-permute-start.1 = (f32[184,256]{1,0:T(8,128)S(1)}, f32[184,256]{1,0:T(8,128)S(1)}, u32[]{:S(2)}, u32[]{:S(2)}) collective-permute-start(f32[184,256]{1,0:T(8,128)S(1)} %get-tuple-element.22), channel_id=1, source_target_pairs={{8,16},{16,8},{24,32},{32,24},{40,48},{48,40},{56,64},{64,56},{72,... | collective-permute-start | bytes 565256 | tf_op jit(solution)/shard_map/ppermute | solution.py:610
  13.1 0.9 %prepare.1 = (bf16[24,128,256]{2,1,0:T(8,128)(2,1)S(1)}, f32[24,2,8,128]{3,2,1,0:T(8,128)S(1)}) custom-call(f32[184,256]{1,0:T(8,128)S(1)} %get-tuple-element.19.order, s32[1,24]{1,0:T(1,128)S(1)} %get-tuple-element.15.tile_ref, f32[12,32,128]{2,1,0:T(8,128)S(1)} %get-tuple-element.17.table), custom_call_target="tpu_custom_call" | custom-call | flops 3000000 | bytes 4000000 | tf_op jit(solution)/shard_map/prepare/pallas_call | solution.py:674
  14.0 0.0 collective-permute-done.recv_a.x_a
  14.0 2.3 %collective-permute-done.1.recv_d.x_d = f32[184,256]{1,0:T(8,128)S(1)} collective-permute-done((f32[184,256]{1,0:T(8,128)S(1)}, f32[184,256]{1,0:T(8,128)S(1)}, u32[]{:S(2)}, u32[]{:S(2)}) %collective-permute-start.1) | collective-permute-done | bytes 188448 | tf_op jit(solution)/shard_map/ppermute | solution.py:610
  16.3 0.3 corners.1
  16.6 5.2 %collective-permute-start.3 = (f32[176,256]{1,0:T(8,128)S(1)}, f32[176,256]{1,0:T(8,128)S(1)}, u32[]{:S(2)}, u32[]{:S(2)}) collective-permute-start(f32[176,256]{1,0:T(8,128)S(1)} %get-tuple-element.24.own_d), channel_id=1, source_target_pairs={{1,2},{2,1},{3,4},{4,3},{5,6},{6,5},{9,10},{10,9},{11,12},{12,11},... | collective-permute-start | bytes 540680 | tf_op jit(solution)/shard_map/ppermute | solution.py:610
  21.8 0.0 copy-start
  21.8 0.1 collective-permute-start.2
  21.9 3.5 %middle.1.gathered = f32[12,24,128]{2,1,0:T(8,128)S(1)} custom-call(f32[176,256]{1,0:T(8,128)S(1)} %get-tuple-element.23.order.own_a, s32[1,24]{1,0:T(1,128)S(1)} %get-tuple-element.15.tile_ref, f32[2,9,6,16,256]{4,3,2,1,0:T(8,128)S(1)} %get-tuple-element.21.halves, f32[184,256]{1,0:T(8,128)S(1)} %collective-permute-done.recv_a.x_a, ...), custom_call_target="tpu_custom_call" | custom-call | flops 3000000 | bytes 4000000 | tf_op jit(solution)/shard_map/middle/pallas_call | solution.py:695
  25.4 2.1 %collective-permute-done.3.y_d = f32[176,256]{1,0:T(8,128)S(1)} collective-permute-done((f32[176,256]{1,0:T(8,128)S(1)}, f32[176,256]{1,0:T(8,128)S(1)}, u32[]{:S(2)}, u32[]{:S(2)}) %collective-permute-start.3) | collective-permute-done | bytes 180256 | tf_op jit(solution)/shard_map/ppermute | solution.py:610
  27.6 0.0 collective-permute-done.2.y_a
  27.6 0.0 copy-done
  27.6 2.4 %gather.1 = (f32[3,24,128]{2,1,0:T(8,128)}, f32[9,24,128]{2,1,0:T(8,128)}, f32[9,24,128]{2,1,0:T(8,128)}, f32[6,24,128]{2,1,0:T(8,128)}) custom-call(s32[1,24]{1,0:T(1,128)S(1)} %get-tuple-element.15.tile_ref, f32[12,24,128]{2,1,0:T(8,128)S(1)} %middle.1.gathered, f32[176,256]{1,0:T(8,128)S(1)} %get-tuple-element.23.order.own_a, ...), custom_call_target="tpu_custom_call" | custom-call | tf_op jit(solution)/shard_map/gather/pallas_call | solution.py:709
Async XLA Ops:
  6.6 7.5 %collective-permute-start = (f32[184,256]{1,0:T(8,128)S(1)}, f32[184,256]{1,0:T(8,128)S(1)}, u32[]{:S(2)}, u32[]{:S(2)}) collective-permute-start(f32[184,256]{1,0:T(8,128)S(1)} %get-tuple-element.19.order), channel_id=1, source_target_pairs={{0,8},{8,0},{16,24},{24,16},{32,40},{40,32},{48,56},{56,48},{64,72... | collective-permute-start | bytes 565256 | tf_op jit(solution)/shard_map/ppermute | solution.py:610
  6.7 9.7 %collective-permute-start.1 = (f32[184,256]{1,0:T(8,128)S(1)}, f32[184,256]{1,0:T(8,128)S(1)}, u32[]{:S(2)}, u32[]{:S(2)}) collective-permute-start(f32[184,256]{1,0:T(8,128)S(1)} %get-tuple-element.22), channel_id=1, source_target_pairs={{8,16},{16,8},{24,32},{32,24},{40,48},{48,40},{56,64},{64,56},{72,... | collective-permute-start | bytes 565256 | tf_op jit(solution)/shard_map/ppermute | solution.py:610
  16.6 11.0 %collective-permute-start.3 = (f32[176,256]{1,0:T(8,128)S(1)}, f32[176,256]{1,0:T(8,128)S(1)}, u32[]{:S(2)}, u32[]{:S(2)}) collective-permute-start(f32[176,256]{1,0:T(8,128)S(1)} %get-tuple-element.24.own_d), channel_id=1, source_target_pairs={{1,2},{2,1},{3,4},{4,3},{5,6},{6,5},{9,10},{10,9},{11,12},{12,11},... | collective-permute-start | bytes 540680 | tf_op jit(solution)/shard_map/ppermute | solution.py:610
  21.8 5.8 %copy-start = (f32[9,24,128]{2,1,0:T(8,128)S(1)}, f32[9,24,128]{2,1,0:T(8,128)}, u32[]{:S(2)}) copy-start(f32[9,24,128]{2,1,0:T(8,128)} %deform.1) | copy-start | bytes 331780
  21.8 5.8 %collective-permute-start.2 = (f32[176,256]{1,0:T(8,128)S(1)}, f32[176,256]{1,0:T(8,128)S(1)}, u32[]{:S(2)}, u32[]{:S(2)}) collective-permute-start(f32[176,256]{1,0:T(8,128)S(1)} %get-tuple-element.23.order.own_a), channel_id=1, source_target_pairs={{0,1},{1,0},{2,3},{3,2},{4,5},{5,4},{6,7},{7,6},{8,9},{9,8},{10,11... | collective-permute-start | bytes 540680 | tf_op jit(solution)/shard_map/ppermute | solution.py:610
